TPU v7x, 32 devices: a whole 2x2x4 slice. The times are simulated.
32 devices in a mesh: gx: 4 (over x, core), gy: 8 (over z, y).
Axes of the slice: x: 2, y: 2, z: 4, core: 2. Of those that a mesh axis runs over, the one named last changes fastest.
Arguments:
- queries: bfloat16 [256, 2560], P('gx'), may hold values from -8 to 8
- token_key_value: bfloat16 [256, 1024], P('gx'), may hold values from -6 to 6
- group_cached_keys: bfloat16 [4, 32768, 512], P('gx', 'gy'), may hold values from -8 to 8
- group_cached_values: bfloat16 [4, 32768, 512], P('gx', 'gy'), may hold values from -6 to 6
- owners: int32 [4, 32768], P('gx', 'gy'), may hold values from 0 to 63, never falling along the last dimension, each value on 1 to 16384 neighbouring positions
- out_weight: bfloat16 [2560, 2560], P(None, 'gy'), may hold values from -0.125 to 0.125
- residual: bfloat16 [256, 2560], P('gx', 'gy'), may hold values from -6 to 6
- norm_gain: bfloat16 [2560], P('gy'), may hold values from 0.099609375 to 1.8984375
- expert_ids: int32 [256, 6], replicated, may hold values from 0 to 63, all different within a row; in each aligned block of 64 rows (0 to 63, 64 to 127, ...) at most 12 rows name the same one
- gate_logits: float32 [256, 6], replicated, may hold values from -0.5 to 0.5
- w_gate_up: bfloat16 [64, 2560, 3072], P('gx', 'gy'), may hold values from -0.125 to 0.125
- w_down: bfloat16 [64, 1536, 2560], P('gx', None, 'gy'), may hold values from -0.15625 to 0.15625
Outputs:
- layer_out: float32 [256, 2560], P('gx', 'gy')
Inputs may be any that keep to these rules, and one draw needn't show every extreme that they name: `owners`: each request's positions form one run; every request owns at least one position and at most 16384, and some request owns exactly 16384. `expert_ids`: within each group of 64 requests no expert is named by more than 12 requests, a bound that some block reaches.
All inputs are finite; a program needn't handle non-finite values.
Results may differ from a plain program's by a relative error of at most 0.0075.
Values may be sent and summed in bfloat16 or wider, within the bound.
No kernel may reach another device: no remote copies, remote signals or barrier semaphores. Data moves between devices by JAX's collectives and lax.ppermute only.
A program may use at most 192 MiB of HBM per device.

v0:
```python
import functools

import jax
import jax.numpy as jnp
from jax import lax
from jax.experimental import pallas as pl
from jax.experimental.pallas import tpu as pltpu
from jax.sharding import PartitionSpec as P

D = 2560
QUERY_HEADS = 20
KEY_VALUE_HEADS = 4
HEAD_SIZE = 128
GROUP = QUERY_HEADS // KEY_VALUE_HEADS
E = 64
TOPK = 6
CAPS = 12

LOWEST = -1e30
EPSILON = 1e-05
SCALING = HEAD_SIZE ** (-0.5)
BLOCK = 512
ROWS = 16
ALIGN = 8
CHUNKS = 4
UNROLL = 4

f32 = jnp.float32
bf16 = jnp.bfloat16
VMEM_LIMIT = 56 * 1024 * 1024


def params(**more):
    return pltpu.CompilerParams(vmem_limit_bytes=VMEM_LIMIT, **more)


def whole(shape):
    return pl.BlockSpec(shape, lambda *_: (0,) * len(shape))


def attend_kernel(
    owner_s, q_ref, own_ref, k_hbm, v_hbm, out_ref, k_scr, v_scr, q_scr, m_scr, l_scr, acc_scr, sem
):
    groups = q_scr.shape[0]
    blocks = sem.shape[1]
    block = k_scr.shape[0] // blocks

    def copies(b):
        rows = pl.ds(b * block, block)
        return (
            pltpu.make_async_copy(k_hbm.at[0, rows], k_scr.at[rows], sem.at[0, b]),
            pltpu.make_async_copy(v_hbm.at[0, rows], v_scr.at[rows], sem.at[1, b]),
        )

    for b in range(blocks):
        for copy in copies(b):
            copy.start()
    for rg in range(groups):
        for c in range(KEY_VALUE_HEADS):
            for g in range(GROUP):
                h = c * GROUP + g
                q_scr[rg, c, g * ROWS : (g + 1) * ROWS, :] = q_ref[
                    rg * ROWS : (rg + 1) * ROWS, h * HEAD_SIZE : (h + 1) * HEAD_SIZE
                ]
    m_scr[...] = jnp.full(m_scr.shape, LOWEST, f32)
    l_scr[...] = jnp.zeros(l_scr.shape, f32)
    acc_scr[...] = jnp.zeros(acc_scr.shape, f32)
    heads = range(KEY_VALUE_HEADS)
    lanes = [slice(c * HEAD_SIZE, (c + 1) * HEAD_SIZE) for c in heads]

    def walk(b, carry):
        for copy in copies(b):
            copy.wait()
        at = pl.multiple_of(b * block, block)
        rows = pl.ds(at, block)
        owner = own_ref[0:1, rows]

        def visit(rg, carry):
            ids = rg * ROWS + lax.broadcasted_iota(jnp.int32, (ROWS, block), 0)
            member = owner == ids
            states = [(m_scr[rg, c], l_scr[rg, c], acc_scr[rg, c]) for c in heads]
            scores = [
                lax.dot_general(
                    q_scr[rg, c],
                    k_scr[rows, lanes[c]],
                    (((1,), (1,)), ((), ())),
                    preferred_element_type=f32,
                )
                * SCALING
                for c in heads
            ]
            results = []
            for c in heads:
                s = jnp.where(member[None], scores[c].reshape(GROUP, ROWS, block), LOWEST)
                s = s.reshape(GROUP * ROWS, block)
                m_old, l_old, acc_old = states[c]
                m_new = jnp.maximum(m_old, jnp.max(s, axis=1, keepdims=True))
                alpha = jnp.exp(m_old - m_new)
                p = jnp.exp(s - m_new[:, :1]).astype(bf16)
                l_new = l_old * alpha + jnp.sum(p.astype(f32), axis=1, keepdims=True)
                acc_new = acc_old * alpha + jnp.dot(
                    p, v_scr[rows, lanes[c]], preferred_element_type=f32
                )
                results.append((m_new, l_new, acc_new))
            for c in heads:
                m_scr[rg, c], l_scr[rg, c], acc_scr[rg, c] = results[c]
            return carry

        first = owner_s[at] // ROWS
        last = owner_s[at + block - 1] // ROWS
        return lax.fori_loop(first, last + 1, visit, carry)

    lax.fori_loop(0, blocks, walk, 0)

    width = QUERY_HEADS * HEAD_SIZE
    lane = lax.broadcasted_iota(jnp.int32, (ROWS, 128), 1)
    piece = lane % 3
    per = out_ref.shape[1]
    for rg in range(groups):

        def put(value, lanes):
            if per >= ROWS:
                at = rg * ROWS
                out_ref[at // per, at % per : at % per + ROWS, lanes] = value.astype(bf16)
            else:
                for i in range(ROWS // per):
                    out_ref[(rg * ROWS) // per + i, :, lanes] = value[
                        i * per : (i + 1) * per
                    ].astype(bf16)

        tail = jnp.zeros((ROWS, 128), f32)
        for c in heads:
            for g in range(GROUP):
                h = c * GROUP + g
                rows = slice(g * ROWS, (g + 1) * ROWS)
                m = m_scr[rg, c, rows, :]
                l = l_scr[rg, c, rows, :]
                tail = jnp.where(lane // 6 == h, jnp.where(lane % 6 < 3, m, l), tail)
                put(
                    acc_scr[rg, c, rows, :] / jnp.maximum(l, 1e-30),
                    slice(h * HEAD_SIZE, (h + 1) * HEAD_SIZE),
                )
        high = tail.astype(bf16).astype(f32)
        rest = tail - high
        middle = rest.astype(bf16).astype(f32)
        low = (rest - middle).astype(bf16).astype(f32)
        put(
            jnp.where(piece == 0, high, jnp.where(piece == 1, middle, low)),
            slice(width, width + 128),
        )


def attend_local(queries, keys, values, owners, parts):
    rows, width = queries.shape
    positions, kv = keys.shape[1:]
    block = min(BLOCK, positions)
    groups = rows // ROWS
    state = (groups, KEY_VALUE_HEADS, GROUP * ROWS, 128)
    out = jax.ShapeDtypeStruct((parts, rows // parts, width + 128), bf16)
    return pl.pallas_call(
        attend_kernel,
        out_shape=out,
        grid_spec=pltpu.PrefetchScalarGridSpec(
            num_scalar_prefetch=1,
            grid=(1,),
            in_specs=[
                whole((rows, width)),
                whole((1, positions)),
                pl.BlockSpec(memory_space=pl.ANY),
                pl.BlockSpec(memory_space=pl.ANY),
            ],
            out_specs=whole(out.shape),
            scratch_shapes=[
                pltpu.VMEM((positions, kv), bf16),
                pltpu.VMEM((positions, kv), bf16),
                pltpu.VMEM((groups, KEY_VALUE_HEADS, GROUP * ROWS, HEAD_SIZE), bf16),
                pltpu.VMEM(state, f32),
                pltpu.VMEM(state, f32),
                pltpu.VMEM(state, f32),
                pltpu.SemaphoreType.DMA((2, positions // block)),
            ],
        ),
        compiler_params=params(),
        name="attend",
    )(owners.reshape(-1), queries, owners, keys, values)


def merge_kernel(part_ref, q_ref, kv_ref, out_ref):
    parts, rows, _ = part_ref.shape
    width = QUERY_HEADS * HEAD_SIZE
    kv = KEY_VALUE_HEADS * HEAD_SIZE
    source = lax.broadcasted_iota(jnp.int32, (128, 256), 0)
    target = lax.broadcasted_iota(jnp.int32, (128, 256), 1)
    wanted = (target % 128) * 6 + (target // 128) * 3
    pick = jnp.where(
        (source >= wanted) & (source < wanted + 3) & (target % 128 < QUERY_HEADS), 1.0, 0.0
    ).astype(bf16)
    lane = lax.broadcasted_iota(jnp.int32, (rows, 128), 1)
    own = jnp.zeros((rows, 128), f32)
    for h in range(QUERY_HEADS):
        c = h // GROUP
        product = q_ref[:, h * HEAD_SIZE : (h + 1) * HEAD_SIZE].astype(f32) * kv_ref[
            :, c * HEAD_SIZE : (c + 1) * HEAD_SIZE
        ].astype(f32)
        own = jnp.where(lane == h, jnp.sum(product, axis=1, keepdims=True) * SCALING, own)
    maxima, sums = [], []
    peak = own
    for j in range(parts):
        both = jnp.dot(part_ref[j, :, width:], pick, preferred_element_type=f32)
        maxima.append(both[:, :128])
        sums.append(both[:, 128:])
        peak = jnp.maximum(peak, both[:, :128])
    own_prob = jnp.exp(own - peak).astype(bf16).astype(f32)
    weights = [l * jnp.exp(m - peak) for m, l in zip(maxima, sums)]
    den = own_prob
    for w in weights:
        den = den + w
    own_prob = own_prob / den
    weights = [w / den for w in weights]
    for h in range(QUERY_HEADS):
        c = h // GROUP
        lanes = slice(h * HEAD_SIZE, (h + 1) * HEAD_SIZE)
        acc = own_prob[:, h : h + 1] * kv_ref[
            :, kv + c * HEAD_SIZE : kv + (c + 1) * HEAD_SIZE
        ].astype(f32)
        for j in range(parts):
            acc = acc + weights[j][:, h : h + 1] * part_ref[j, :, lanes].astype(f32)
        out_ref[:, lanes] = acc.astype(bf16)


def merge(part, queries, token_key_value):
    return pl.pallas_call(
        merge_kernel,
        out_shape=jax.ShapeDtypeStruct(queries.shape, bf16),
        compiler_params=params(),
        name="merge",
    )(part, queries, token_key_value)


def routing(expert_ids, mixing, num_gx, group_index):
    local = E // num_gx
    hit = expert_ids[:, :, None] == lax.iota(jnp.int32, E)
    named = jnp.any(hit, axis=1)
    counts = jnp.sum(named.astype(jnp.int32), axis=0).reshape(num_gx, local)
    needed = jnp.max(jnp.sum(counts, axis=1))
    earlier = lax.iota(jnp.int32, local)[:, None] < lax.iota(jnp.int32, local)[None, :]
    starts = jnp.sum(jnp.where(earlier[None], counts[:, :, None], 0), axis=1)
    mine = group_index * local + lax.iota(jnp.int32, local)
    hit_mine = expert_ids[:, :, None] == mine
    mine_named = jnp.any(hit_mine, axis=1)
    weight = jnp.sum(jnp.where(hit_mine, mixing[:, :, None], 0.0), axis=1)
    requests = expert_ids.shape[0]
    before = (lax.iota(jnp.int32, requests)[None, :] < lax.iota(jnp.int32, requests)[:, None])
    rank = jnp.dot(
        before.astype(bf16), mine_named.astype(bf16), preferred_element_type=f32
    ).astype(jnp.int32)
    start = lax.dynamic_index_in_dim(starts, group_index, 0, False)
    place = jnp.where(mine_named, rank + start[None, :], -1)
    base = start // ALIGN * ALIGN
    rank = jnp.where(mine_named, place - base[None, :], -1)
    return rank, place, weight, base, needed


def dispatch_kernel(h_ref, gain_ref, rank_ref, x_ref, square_ref):
    slots = x_ref.shape[1]
    h = h_ref[...].astype(f32)
    square_ref[...] = lax.dot_general(
        jnp.ones((8, h.shape[1]), f32),
        h * h,
        (((1,), (1,)), ((), ())),
        precision=lax.Precision.HIGHEST,
        preferred_element_type=f32,
    )
    scaled = (h * gain_ref[...].astype(f32)).astype(bf16)
    slot = lax.broadcasted_iota(jnp.int32, (slots, h.shape[0]), 0)
    for e in range(x_ref.shape[0]):
        pick = (rank_ref[e : e + 1, :] == slot).astype(f32).astype(bf16)
        x_ref[e] = jnp.dot(pick, scaled, preferred_element_type=f32).astype(bf16)


def dispatch(hidden_all, gain, rank_t, slots):
    requests, features = hidden_all.shape
    return pl.pallas_call(
        dispatch_kernel,
        out_shape=(
            jax.ShapeDtypeStruct((rank_t.shape[0], slots, features), bf16),
            jax.ShapeDtypeStruct((8, requests), f32),
        ),
        compiler_params=params(),
        name="dispatch",
    )(hidden_all, gain.reshape(1, -1), rank_t)


def gate_up_kernel(bit, chunk, me_s, base_s, x_ref, w_hbm, keep_ref, send_ref, scr, buf, sem):
    experts, slots, _ = x_ref.shape
    units = buf.shape[3]
    hidden_units = units * CHUNKS

    def copies(e):
        return [
            pltpu.make_async_copy(
                w_hbm.at[e, :, pl.ds(half * hidden_units + chunk * units, units)],
                buf.at[e, half],
                sem.at[e, half],
            )
            for half in range(2)
        ]

    for e in range(experts):
        for copy in copies(e):
            copy.start()
    scr[...] = jnp.zeros(scr.shape, f32)
    unroll = min(UNROLL, experts)

    def visit(step, carry):
        for i in range(unroll):
            e = step * unroll + i
            rows = pl.ds(pl.multiple_of(base_s[e], ALIGN), slots)
            x = x_ref[e]
            for half, copy in enumerate(copies(e)):
                copy.wait()
                lanes = slice(half * units, (half + 1) * units)
                scr[rows, lanes] += jnp.dot(x, buf[e, half], preferred_element_type=f32)
        return carry

    lax.fori_loop(0, experts // unroll, visit, 0)
    half, each, _ = keep_ref.shape
    me = me_s[0]
    for i in range(half):
        other = (i // bit) * 2 * bit + i % bit
        at = jnp.bitwise_xor(me, other) * each
        keep_ref[i] = scr[pl.ds(pl.multiple_of(at, ALIGN), each), :].astype(bf16)
        at = jnp.bitwise_xor(me, other + bit) * each
        send_ref[i] = scr[pl.ds(pl.multiple_of(at, ALIGN), each), :].astype(bf16)


def gate_up(x, w_gate_up, base, me, capacity, parts, chunk, bit):
    experts, slots, features = x.shape
    units = w_gate_up.shape[2] // (2 * CHUNKS)
    out = jax.ShapeDtypeStruct((parts // 2, capacity // parts, 2 * units), bf16)
    return pl.pallas_call(
        functools.partial(gate_up_kernel, bit, chunk),
        out_shape=(out, out),
        grid_spec=pltpu.PrefetchScalarGridSpec(
            num_scalar_prefetch=2,
            grid=(1,),
            in_specs=[whole(x.shape), pl.BlockSpec(memory_space=pl.ANY)],
            out_specs=(whole(out.shape), whole(out.shape)),
            scratch_shapes=[
                pltpu.VMEM((capacity + slots, 2 * units), f32),
                pltpu.VMEM((experts, 2, features, units), bf16),
                pltpu.SemaphoreType.DMA((experts, 2)),
            ],
        ),
        compiler_params=params(),
        cost_estimate=pl.CostEstimate(
            flops=4 * experts * slots * features * units,
            bytes_accessed=experts * features * units * 4 + out.size * 4,
            transcendentals=0,
        ),
        name="gate_up",
    )(me, base, x, w_gate_up)


def exchange(x, k, parts):
    return lax.ppermute(x, "gy", [(i, i ^ k) for i in range(parts)])


def scatter_sums(keep, send, order, parts):
    names = [k for k in range(parts) if not k & order[0]]
    total = keep.astype(f32) + exchange(send, order[0], parts).astype(f32)
    for k in order[1:]:
        kept = [i for i, n in enumerate(names) if not n & k]
        sent = [i for i, n in enumerate(names) if n & k]
        rest = jnp.stack([total[i] for i in sent]).astype(bf16)
        total = jnp.stack([total[i] for i in kept]) + exchange(rest, k, parts).astype(f32)
        names = [names[i] for i in kept]
    return total[0]


def gather_rows(x, order, parts):
    names = [0]
    x = x[None]
    for k in order[:-1]:
        x = jnp.concatenate([x, exchange(x, k, parts)], axis=0)
        names = names + [n ^ k for n in names]
    return x, exchange(x, order[-1], parts), names, [n ^ order[-1] for n in names]


def down_kernel(names, me_s, base_s, *refs):
    acts = refs[: len(names)]
    rank_ref, weight_ref, w_hbm, out_ref, scr, buf, sem = refs[len(names) :]
    experts = buf.shape[0]
    each = acts[0].shape[1]
    capacity = 2 * acts[0].shape[0] * each
    slots = scr.shape[0] - capacity
    total = rank_ref.shape[0]
    me = me_s[0]

    def fetch(e):
        return pltpu.make_async_copy(w_hbm.at[e], buf.at[e], sem.at[e])

    for e in range(experts):
        fetch(e).start()
    scr[capacity:, :] = jnp.zeros((slots, scr.shape[1]), f32)
    for a, (ref, ns) in enumerate(zip(acts, names)):
        units = ref.shape[2]
        lanes = slice((a // 2) * units, (a // 2 + 1) * units)
        for i, n in enumerate(ns):
            at = jnp.bitwise_xor(me, n) * each
            scr[pl.ds(pl.multiple_of(at, ALIGN), each), lanes] = ref[i].astype(f32)
    out_ref[...] = jnp.zeros(out_ref.shape, f32)
    column = lax.broadcasted_iota(jnp.int32, (total, 128), 1)
    slot = lax.broadcasted_iota(jnp.int32, (total, slots), 1)
    unroll = min(UNROLL, experts)

    def visit(step, carry):
        add = None
        for i in range(unroll):
            e = step * unroll + i
            rows = pl.ds(pl.multiple_of(base_s[e], ALIGN), slots)
            x = scr[rows, :].astype(bf16)
            fetch(e).wait()
            y = lax.dot_general(
                x, buf[e], (((1,), (1,)), ((), ())), preferred_element_type=f32
            ).astype(bf16)
            rank = jnp.sum(jnp.where(column == e, rank_ref[...], 0), axis=1, keepdims=True)
            weight = jnp.sum(
                jnp.where(column == e, weight_ref[...], 0.0), axis=1, keepdims=True
            )
            pick = (rank == slot).astype(f32).astype(bf16)
            term = weight * jnp.dot(pick, y, preferred_element_type=f32)
            add = term if add is None else add + term
        out_ref[...] += add
        return carry

    lax.fori_loop(0, experts // unroll, visit, 0)


def down(acts, names, w_down_t, base, me, rank, weight, slots):
    experts, features, hidden_units = w_down_t.shape
    capacity = acts[0].shape[0] * acts[0].shape[1] * 2
    total = rank.shape[0]
    pad = ((0, 0), (0, 128 - experts))
    rank = jnp.pad(rank, pad)
    weight = jnp.pad(weight, pad)
    return pl.pallas_call(
        functools.partial(down_kernel, names),
        out_shape=jax.ShapeDtypeStruct((total, features), f32),
        grid_spec=pltpu.PrefetchScalarGridSpec(
            num_scalar_prefetch=2,
            grid=(1,),
            in_specs=[whole(a.shape) for a in acts]
            + [whole(rank.shape), whole(weight.shape), pl.BlockSpec(memory_space=pl.ANY)],
            out_specs=whole((total, features)),
            scratch_shapes=[
                pltpu.VMEM((capacity + slots, hidden_units), f32),
                pltpu.VMEM(w_down_t.shape, bf16),
                pltpu.SemaphoreType.DMA((experts,)),
            ],
        ),
        compiler_params=params(),
        name="down",
    )(me, base, *acts, rank, weight, w_down_t)


def sum_over_gy(x, parts):
    k = 1
    while k < parts:
        x = x + exchange(x, k, parts)
        k *= 2
    return x


def experts_part(capacity, x, square, w_gate_up, w_down_t, base, rank, place, weight, me, parts, slots):
    units = w_down_t.shape[2] // CHUNKS
    rows = capacity // parts
    here = me[0] * rows + lax.iota(jnp.int32, rows)
    mine = jnp.any(place[None] == here[:, None, None], axis=2)
    bits = [1 << i for i in range(parts.bit_length() - 1)]
    acts, names = [], []
    scale = None
    for chunk in range(CHUNKS):
        order = bits if chunk % 2 == 0 else bits[1:] + bits[:1]
        keep, send = gate_up(x, w_gate_up, base, me, capacity, parts, chunk, order[0])
        both = scatter_sums(keep, send, order, parts)
        if scale is None:
            inv = lax.rsqrt(sum_over_gy(square, parts).reshape(-1) / D + EPSILON)
            scale = jnp.sum(jnp.where(mine, inv[None, :], 0.0), axis=1)[:, None]
        gate = both[:, :units] * scale
        up = both[:, units:] * scale
        act = (jax.nn.silu(gate) * up).astype(bf16)
        left, right, left_names, right_names = gather_rows(act, order[::-1], parts)
        acts += [left, right]
        names += [left_names, right_names]
    return down(acts, names, w_down_t, base, me, rank, weight, slots)


def out_kernel(a_ref, w_ref, r_ref, o_ref):
    projected = lax.dot_general(
        a_ref[...], w_ref[...], (((1,), (1,)), ((), ())), preferred_element_type=f32
    )
    o_ref[...] = (r_ref[...].astype(f32) + projected).astype(bf16)


def project(attention, out_weight, residual):
    return pl.pallas_call(
        out_kernel,
        out_shape=jax.ShapeDtypeStruct(residual.shape, bf16),
        compiler_params=params(),
        name="project",
    )(attention, out_weight, residual)


def shards(
    queries,
    token_key_value,
    group_cached_keys,
    group_cached_values,
    owners,
    out_weight,
    residual,
    norm_gain,
    expert_ids,
    gate_logits,
    w_gate_up,
    w_down,
):
    rows, width = queries.shape
    parts = lax.axis_size("gy")
    num_gx = lax.axis_size("gx")
    me_y = lax.axis_index("gy")
    me_x = lax.axis_index("gx")
    me = jnp.full((1,), me_y, jnp.int32)
    each = rows // parts
    slots = -(-(num_gx * CAPS + ALIGN - 1) // ALIGN) * ALIGN
    local = w_gate_up.shape[0]

    part = attend_local(queries, group_cached_keys, group_cached_values, owners, parts)
    part = lax.all_to_all(part, "gy", 0, 0)
    attention = merge(
        part,
        lax.dynamic_slice_in_dim(queries, me_y * each, each, 0),
        lax.dynamic_slice_in_dim(token_key_value, me_y * each, each, 0),
    )
    attention = lax.all_to_all(
        jnp.broadcast_to(attention[None], (parts,) + attention.shape), "gy", 0, 0
    ).reshape(rows, width)
    hidden = project(attention, out_weight.T, residual)
    hidden_all = lax.all_gather(hidden, "gx", axis=0, tiled=True)

    mixing = jax.nn.softmax(gate_logits, axis=-1)
    rank, place, weight, base, needed = routing(expert_ids, mixing, num_gx, me_x)
    x, square = dispatch(hidden_all, norm_gain, rank.T, slots)

    capacity = local * num_gx * CAPS
    sizes = [c for c in (448, 512) if c < capacity and c % (ALIGN * parts) == 0] + [capacity]
    branch = sum((needed > c).astype(jnp.int32) for c in sizes[:-1])
    operands = (
        x,
        square[0].reshape(-1, 128),
        w_gate_up,
        jnp.swapaxes(w_down, 1, 2),
        base,
        rank,
        place,
        weight,
        me,
    )
    routed = lax.switch(
        branch,
        [lambda *o, c=c: experts_part(c, *o, parts=parts, slots=slots) for c in sizes],
        *operands,
    )
    routed = lax.all_to_all(routed.reshape(num_gx, rows, -1), "gx", 0, 0)
    return hidden.astype(f32) + jnp.sum(routed, axis=0)


def solution(mesh):
    placed = (
        P("gx", None),
        P("gx", None),
        P("gx", "gy", None),
        P("gx", "gy", None),
        P("gx", "gy"),
        P(None, "gy"),
        P("gx", "gy"),
        P("gy"),
        P(),
        P(),
        P("gx", "gy", None),
        P("gx", None, "gy"),
    )
    return jax.shard_map(
        shards, mesh=mesh, in_specs=placed, out_specs=P("gx", "gy"), check_vma=False
    )
```

profile of v0, /device:TPU:0, one launch (start us, length us, event | category | flops | bytes accessed | tf_op | source)
XLA Modules:
  0.0 190.8 jit_solution(5395640326092606311)
XLA Ops:
  0.0 10.9 %attend.1 = bf16[8,8,2688]{2,1,0:T(8,128)(2,1)} custom-call(s32[4096]{0:T(1024)} %bitcast.81, bf16[64,2560]{1,0:T(8,128)(2,1)} %q_ref.1, s32[1,4096]{1,0:T(1,128)} %own_ref.1, bf16[1,4096,512]{2,1,0:T(8,128)(2,1)} %k_hbm.1, bf16[1,4096,512]{2,1,0:T(8,128)(2,1)} %v_hbm.1), custom_call_target="tpu_custom_call" | custom-call | tf_op jit(solution)/shard_map/attend/pallas_call | solution.py:160
  10.9 8.1 %all-to-all-start = ((bf16[8,8,2688]{2,1,0:T(8,128)(2,1)}), bf16[8,8,2688]{2,1,0:T(8,128)(2,1)S(1)}, u32[]{:S(2)}, u32[]{:S(2)}) async-start(bf16[8,8,2688]{2,1,0:T(8,128)(2,1)} %attend.1), calls=%async_computation | async-start | bytes 688128 | tf_op jit(solution)/shard_map/all_to_all | solution.py:540
  21.6 7.2 %all-to-all-done.part_ref = bf16[8,8,2688]{2,1,0:T(8,128)(2,1)S(1)} async-done(((bf16[8,8,2688]{2,1,0:T(8,128)(2,1)}), bf16[8,8,2688]{2,1,0:T(8,128)(2,1)S(1)}, u32[]{:S(2)}, u32[]{:S(2)}) %all-to-all-start) | async-done | bytes 344096 | tf_op jit(solution)/shard_map/all_to_all | solution.py:540
  29.6 2.1 %merge.1 = bf16[8,2560]{1,0:T(8,128)(2,1)} custom-call(bf16[8,8,2688]{2,1,0:T(8,128)(2,1)} %copy-done.2, bf16[8,2560]{1,0:T(8,128)(2,1)} %constant_dynamic-slice_fusion.2.q_ref, bf16[8,1024]{1,0:T(8,128)(2,1)} %constant_dynamic-slice_fusion.1.kv_ref), custom_call_target="tpu_custom_call" | custom-call | tf_op jit(solution)/shard_map/merge/pallas_call | solution.py:232
  33.2 3.6 %all-to-all-start.1 = ((bf16[8,8,2560]{2,1,0:T(8,128)(2,1)}), bf16[8,8,2560]{2,1,0:T(8,128)(2,1)S(1)}, u32[]{:S(2)}, u32[]{:S(2)}) async-start(bf16[8,8,2560]{2,1,0:T(8,128)(2,1)} %broadcast_in_dim.146), calls=%async_computation.1 | async-start | bytes 655360 | tf_op jit(solution)/shard_map/all_to_all | solution.py:546
  40.4 6.1 %all-to-all-done.1 = bf16[8,8,2560]{2,1,0:T(8,128)(2,1)S(1)} async-done(((bf16[8,8,2560]{2,1,0:T(8,128)(2,1)}), bf16[8,8,2560]{2,1,0:T(8,128)(2,1)S(1)}, u32[]{:S(2)}, u32[]{:S(2)}) %all-to-all-start.1) | async-done | bytes 327712 | tf_op jit(solution)/shard_map/all_to_all | solution.py:546
  47.3 2.7 %project.1 = bf16[64,320]{1,0:T(8,128)(2,1)} custom-call(bf16[64,2560]{1,0:T(8,128)(2,1)} %bitcast.80, bf16[320,2560]{1,0:T(8,128)(2,1)} %bitcast.78, bf16[64,320]{1,0:T(8,128)(2,1)} %r_ref.1), custom_call_target="tpu_custom_call" | custom-call | tf_op jit(solution)/shard_map/project/pallas_call | solution.py:507
  50.0 8.1 %all_gather.3.h_ref = bf16[256,320]{1,0:T(8,128)(2,1)} all-gather(bf16[64,320]{1,0:T(8,128)(2,1)} %project.1), channel_id=1, replica_groups=mesh['gx'=4,'gy'=8] {'gx'}, dimensions={0}, use_global_device_ids=true | all-gather | bytes 204800 | tf_op jit(solution)/shard_map/all_gather | solution.py:550
  58.1 2.3 %dispatch.1 = (bf16[16,56,320]{2,1,0:T(8,128)(2,1)S(1)}, f32[8,256]{1,0:T(8,128)}) custom-call(bf16[256,320]{1,0:T(8,128)(2,1)} %all_gather.3.h_ref, bf16[1,320]{1,0:T(2,128)(2,1)} %reshape.97.gain_ref, s32[16,256]{1,0:T(8,128)} %get-tuple-element.239.rank_ref), custom_call_target="tpu_custom_call" | custom-call | tf_op jit(solution)/shard_map/dispatch/pallas_call | solution.py:283
  61.0 119.1 %conditional.1 = (f32[256,320]{1,0:T(8,128)S(1)}) conditional(s32[]{:T(128)} %clamp.3, (s32[1]{0:T(128)}, s32[16]{0:T(128)S(1)}, bf16[16,56,320]{2,1,0:T(8,128)(2,1)S(1)}, bf16[16,320,3072]{2,1,0:T(8,128)(2,1)}, s32[256,16]{0,1:T(8,128)S(1)}, /*index=5*/s32[]{:T(128)}, f32[2,128]{1,0:T(2,128)S(1)}, s32[256,16]{0,1:T(8,128)S(1)}, ...), branch_computations={%region_9.12_spmd, %region_12.15_spmd, %region_15.18_spmd} | conditional | flops 1771562240 | bytes 111829928 | solution.py:570
  61.0 8.7 %gate_up.14 = (bf16[4,56,768]{2,1,0:T(8,128)(2,1)}, bf16[4,56,768]{2,1,0:T(8,128)(2,1)}) custom-call(s32[1]{0:T(128)} %get-tuple-element.68.me_s, s32[16]{0:T(128)S(1)} %get-tuple-element.70.base_s, bf16[16,56,320]{2,1,0:T(8,128)(2,1)S(1)} %get-tuple-element.71.x_ref, bf16[16,320,3072]{2,1,0:T(8,128)(2,1)} %get-tuple-element.72.w_hbm), custom_call_target="tpu_custom_call" | custom-call | flops 440401920 | bytes 8552448 | tf_op jit(solution)/shard_map/cond/branch_0_fun/gate_up/pallas_call | solution.py:341
  71.4 8.7 %gate_up.12 = (bf16[4,56,768]{2,1,0:T(8,128)(2,1)}, bf16[4,56,768]{2,1,0:T(8,128)(2,1)}) custom-call(s32[1]{0:T(128)} %get-tuple-element.68.me_s, s32[16]{0:T(128)S(1)} %get-tuple-element.70.base_s, bf16[16,56,320]{2,1,0:T(8,128)(2,1)S(1)} %get-tuple-element.71.x_ref, bf16[16,320,3072]{2,1,0:T(8,128)(2,1)} %get-tuple-element.72.w_hbm), custom_call_target="tpu_custom_call" | custom-call | flops 440401920 | bytes 8552448 | tf_op jit(solution)/shard_map/cond/branch_0_fun/gate_up/pallas_call | solution.py:341
  80.7 8.7 %gate_up.13 = (bf16[4,56,768]{2,1,0:T(8,128)(2,1)}, bf16[4,56,768]{2,1,0:T(8,128)(2,1)}) custom-call(s32[1]{0:T(128)} %get-tuple-element.68.me_s, s32[16]{0:T(128)S(1)} %get-tuple-element.70.base_s, bf16[16,56,320]{2,1,0:T(8,128)(2,1)S(1)} %get-tuple-element.71.x_ref, bf16[16,320,3072]{2,1,0:T(8,128)(2,1)} %get-tuple-element.72.w_hbm), custom_call_target="tpu_custom_call" | custom-call | flops 440401920 | bytes 8552448 | tf_op jit(solution)/shard_map/cond/branch_0_fun/gate_up/pallas_call | solution.py:341
  91.1 8.7 %gate_up.15 = (bf16[4,56,768]{2,1,0:T(8,128)(2,1)}, bf16[4,56,768]{2,1,0:T(8,128)(2,1)}) custom-call(s32[1]{0:T(128)} %get-tuple-element.68.me_s, s32[16]{0:T(128)S(1)} %get-tuple-element.70.base_s, bf16[16,56,320]{2,1,0:T(8,128)(2,1)S(1)} %get-tuple-element.71.x_ref, bf16[16,320,3072]{2,1,0:T(8,128)(2,1)} %get-tuple-element.72.w_hbm), custom_call_target="tpu_custom_call" | custom-call | flops 440401920 | bytes 8552448 | tf_op jit(solution)/shard_map/cond/branch_0_fun/gate_up/pallas_call | solution.py:341
  102.0 7.7 %collective-permute-done.4 = f32[2,128]{1,0:T(2,128)S(1)} collective-permute-done((f32[2,128]{1,0:T(2,128)S(1)}, f32[2,128]{1,0:T(2,128)S(1)}, u32[]{:S(2)}, u32[]{:S(2)}) %collective-permute-start.4) | collective-permute-done | bytes 1056 | tf_op jit(solution)/shard_map/cond/branch_0_fun/ppermute | solution.py:366
  111.5 2.6 %collective-permute-done.5 = f32[2,128]{1,0:T(2,128)S(1)} collective-permute-done((f32[2,128]{1,0:T(2,128)S(1)}, f32[2,128]{1,0:T(2,128)S(1)}, u32[]{:S(2)}, u32[]{:S(2)}) %collective-permute-start.5) | collective-permute-done | bytes 1056 | tf_op jit(solution)/shard_map/cond/branch_0_fun/ppermute | solution.py:366
  120.5 2.8 %collective-permute-done.16 = bf16[2,56,768]{2,1,0:T(8,128)(2,1)S(1)} collective-permute-done((bf16[2,56,768]{2,1,0:T(8,128)(2,1)S(1)}, bf16[2,56,768]{2,1,0:T(8,128)(2,1)S(1)}, u32[]{:S(2)}, u32[]{:S(2)}) %collective-permute-start.16) | collective-permute-done | bytes 172064 | tf_op jit(solution)/shard_map/cond/branch_0_fun/ppermute | solution.py:366
  123.7 3.0 %collective-permute-done.1 = bf16[2,56,768]{2,1,0:T(8,128)(2,1)S(1)} collective-permute-done((bf16[2,56,768]{2,1,0:T(8,128)(2,1)S(1)}, bf16[2,56,768]{2,1,0:T(8,128)(2,1)S(1)}, u32[]{:S(2)}, u32[]{:S(2)}) %collective-permute-start.1) | collective-permute-done | bytes 172064 | tf_op jit(solution)/shard_map/cond/branch_0_fun/ppermute | solution.py:366
  127.4 7.6 %collective-permute-done.10 = bf16[2,56,768]{2,1,0:T(8,128)(2,1)S(1)} collective-permute-done((bf16[2,56,768]{2,1,0:T(8,128)(2,1)S(1)}, bf16[2,56,768]{2,1,0:T(8,128)(2,1)S(1)}, u32[]{:S(2)}, u32[]{:S(2)}) %collective-permute-start.10) | collective-permute-done | bytes 172064 | tf_op jit(solution)/shard_map/cond/branch_0_fun/ppermute | solution.py:366
  135.7 2.2 %collective-permute-done.22 = bf16[2,56,768]{2,1,0:T(8,128)(2,1)S(1)} collective-permute-done((bf16[2,56,768]{2,1,0:T(8,128)(2,1)S(1)}, bf16[2,56,768]{2,1,0:T(8,128)(2,1)S(1)}, u32[]{:S(2)}, u32[]{:S(2)}) %collective-permute-start.22) | collective-permute-done | bytes 172064 | tf_op jit(solution)/shard_map/cond/branch_0_fun/ppermute | solution.py:366
  139.8 2.7 %collective-permute-done.23 = bf16[1,56,768]{2,1,0:T(8,128)(2,1)S(1)} collective-permute-done((bf16[1,56,768]{2,1,0:T(8,128)(2,1)S(1)}, bf16[1,56,768]{2,1,0:T(8,128)(2,1)S(1)}, u32[]{:S(2)}, u32[]{:S(2)}) %collective-permute-start.23) | collective-permute-done | bytes 86048 | tf_op jit(solution)/shard_map/cond/branch_0_fun/ppermute | solution.py:366
  144.9 2.9 %collective-permute-start.6 = (bf16[1,56,384]{2,1,0:T(8,128)(2,1)S(1)}, bf16[1,56,384]{2,1,0:T(8,128)(2,1)S(1)}, u32[]{:S(2)}, u32[]{:S(2)}) collective-permute-start(bf16[1,56,384]{2,1,0:T(8,128)(2,1)S(1)} %get-tuple-element.202), channel_id=1, source_target_pairs={{0,4},{1,5},{2,6},{3,7},{4,0},{5,1},{6,2},{7,3},{8,12},{9,13},{10,... | collective-permute-start | bytes 129032 | tf_op jit(solution)/shard_map/cond/branch_0_fun/ppermute | solution.py:366
  164.0 15.9 %down.3 = f32[256,320]{1,0:T(8,128)S(1)} custom-call(s32[1]{0:T(128)} %get-tuple-element.68.me_s, s32[16]{0:T(128)S(1)} %get-tuple-element.70.base_s, bf16[4,56,384]{2,1,0:T(8,128)(2,1)} %copy-done.15, bf16[4,56,384]{2,1,0:T(8,128)(2,1)} %copy-done.40, bf16[4,56,384]{2,1,0:T(8,128)(2,1)} %copy-done.14, bf16[4,56,384]{2,1,0:T(8,128)(2,1)} %copy-done.39, ...), custom_call_target="tpu_custom_call" | custom-call | tf_op jit(solution)/shard_map/cond/branch_0_fun/down/pallas_call | solution.py:447
  180.1 10.0 %all_to_all.15 = f32[4,64,320]{2,1,0:T(8,128)S(1)} all-to-all(f32[4,64,320]{2,1,0:T(8,128)S(1)} %bitcast.79), channel_id=1, replica_groups=mesh['gx'=4,'gy'=8] {'gx'}, dimensions={0} | all-to-all | bytes 655360 | tf_op jit(solution)/shard_map/all_to_all | solution.py:575
  (153 shorter events, 45.3 us)
Async XLA Ops:
  10.9 17.9 %all-to-all-start = ((bf16[8,8,2688]{2,1,0:T(8,128)(2,1)}), bf16[8,8,2688]{2,1,0:T(8,128)(2,1)S(1)}, u32[]{:S(2)}, u32[]{:S(2)}) async-start(bf16[8,8,2688]{2,1,0:T(8,128)(2,1)} %attend.1), calls=%async_computation | async-start | bytes 688128 | tf_op jit(solution)/shard_map/all_to_all | solution.py:540
  33.2 13.3 %all-to-all-start.1 = ((bf16[8,8,2560]{2,1,0:T(8,128)(2,1)}), bf16[8,8,2560]{2,1,0:T(8,128)(2,1)S(1)}, u32[]{:S(2)}, u32[]{:S(2)}) async-start(bf16[8,8,2560]{2,1,0:T(8,128)(2,1)} %broadcast_in_dim.146), calls=%async_computation.1 | async-start | bytes 655360 | tf_op jit(solution)/shard_map/all_to_all | solution.py:546
  69.8 44.4 %collective-permute-start.15 = (bf16[4,56,768]{2,1,0:T(8,128)(2,1)}, bf16[4,56,768]{2,1,0:T(8,128)(2,1)S(1)}, u32[]{:S(2)}, u32[]{:S(2)}) collective-permute-start(bf16[4,56,768]{2,1,0:T(8,128)(2,1)} %get-tuple-element.81), channel_id=1, source_target_pairs={{0,1},{1,0},{2,3},{3,2},{4,5},{5,4},{6,7},{7,6},{8,9},{9,8},{10,11... | collective-permute-start | bytes 1032200 | tf_op jit(solution)/shard_map/cond/branch_0_fun/ppermute | solution.py:366
  80.1 36.0 %collective-permute-start = (bf16[4,56,768]{2,1,0:T(8,128)(2,1)}, bf16[4,56,768]{2,1,0:T(8,128)(2,1)S(1)}, u32[]{:S(2)}, u32[]{:S(2)}) collective-permute-start(bf16[4,56,768]{2,1,0:T(8,128)(2,1)} %get-tuple-element.74), channel_id=1, source_target_pairs={{0,1},{1,0},{2,3},{3,2},{4,5},{5,4},{6,7},{7,6},{8,9},{9,8},{10,11... | collective-permute-start | bytes 1032200 | tf_op jit(solution)/shard_map/cond/branch_0_fun/ppermute | solution.py:366
  89.4 27.7 %collective-permute-start.9 = (bf16[4,56,768]{2,1,0:T(8,128)(2,1)}, bf16[4,56,768]{2,1,0:T(8,128)(2,1)S(1)}, u32[]{:S(2)}, u32[]{:S(2)}) collective-permute-start(bf16[4,56,768]{2,1,0:T(8,128)(2,1)} %get-tuple-element.79), channel_id=1, source_target_pairs={{0,2},{1,3},{2,0},{3,1},{4,6},{5,7},{6,4},{7,5},{8,10},{9,11},{10,... | collective-permute-start | bytes 1032200 | tf_op jit(solution)/shard_map/cond/branch_0_fun/ppermute | solution.py:366
  90.6 11.3 %collective-permute-start.3 = (f32[2,128]{1,0:T(2,128)S(1)}, f32[2,128]{1,0:T(2,128)S(1)}, u32[]{:S(2)}, u32[]{:S(2)}) collective-permute-start(f32[2,128]{1,0:T(2,128)S(1)} %get-tuple-element.77), channel_id=1, source_target_pairs={{0,1},{1,0},{2,3},{3,2},{4,5},{5,4},{6,7},{7,6},{8,9},{9,8},{10,11... | collective-permute-start | bytes 3080 | tf_op jit(solution)/shard_map/cond/branch_0_fun/ppermute | solution.py:366
  99.8 18.7 %collective-permute-start.21 = (bf16[4,56,768]{2,1,0:T(8,128)(2,1)}, bf16[4,56,768]{2,1,0:T(8,128)(2,1)S(1)}, u32[]{:S(2)}, u32[]{:S(2)}) collective-permute-start(bf16[4,56,768]{2,1,0:T(8,128)(2,1)} %get-tuple-element.83), channel_id=1, source_target_pairs={{0,2},{1,3},{2,0},{3,1},{4,6},{5,7},{6,4},{7,5},{8,10},{9,11},{10,... | collective-permute-start | bytes 1032200 | tf_op jit(solution)/shard_map/cond/branch_0_fun/ppermute | solution.py:366
  101.8 7.8 %collective-permute-start.4 = (f32[2,128]{1,0:T(2,128)S(1)}, f32[2,128]{1,0:T(2,128)S(1)}, u32[]{:S(2)}, u32[]{:S(2)}) collective-permute-start(f32[2,128]{1,0:T(2,128)S(1)} %add.201), channel_id=1, source_target_pairs={{0,2},{1,3},{2,0},{3,1},{4,6},{5,7},{6,4},{7,5},{8,10},{9,11},{10,... | collective-permute-start | bytes 3080 | tf_op jit(solution)/shard_map/cond/branch_0_fun/ppermute | solution.py:366
  114.4 8.9 %collective-permute-start.16 = (bf16[2,56,768]{2,1,0:T(8,128)(2,1)S(1)}, bf16[2,56,768]{2,1,0:T(8,128)(2,1)S(1)}, u32[]{:S(2)}, u32[]{:S(2)}) collective-permute-start(bf16[2,56,768]{2,1,0:T(8,128)(2,1)S(1)} %pad_maximum_fusion.3), channel_id=1, source_target_pairs={{0,2},{1,3},{2,0},{3,1},{4,6},{5,7},{6,4},{7,5},{8,10},{9,11},{10,... | collective-permute-start | bytes 516104 | tf_op jit(solution)/shard_map/cond/branch_0_fun/ppermute | solution.py:366
  116.3 10.4 %collective-permute-start.1 = (bf16[2,56,768]{2,1,0:T(8,128)(2,1)S(1)}, bf16[2,56,768]{2,1,0:T(8,128)(2,1)S(1)}, u32[]{:S(2)}, u32[]{:S(2)}) collective-permute-start(bf16[2,56,768]{2,1,0:T(8,128)(2,1)S(1)} %pad_maximum_fusion), channel_id=1, source_target_pairs={{0,2},{1,3},{2,0},{3,1},{4,6},{5,7},{6,4},{7,5},{8,10},{9,11},{10,... | collective-permute-start | bytes 516104 | tf_op jit(solution)/shard_map/cond/branch_0_fun/ppermute | solution.py:366
  117.2 17.8 %collective-permute-start.10 = (bf16[2,56,768]{2,1,0:T(8,128)(2,1)S(1)}, bf16[2,56,768]{2,1,0:T(8,128)(2,1)S(1)}, u32[]{:S(2)}, u32[]{:S(2)}) collective-permute-start(bf16[2,56,768]{2,1,0:T(8,128)(2,1)S(1)} %stack.103), channel_id=1, source_target_pairs={{0,4},{1,5},{2,6},{3,7},{4,0},{5,1},{6,2},{7,3},{8,12},{9,13},{10,... | collective-permute-start | bytes 516104 | tf_op jit(solution)/shard_map/cond/branch_0_fun/ppermute | solution.py:366
  118.7 19.3 %collective-permute-start.22 = (bf16[2,56,768]{2,1,0:T(8,128)(2,1)S(1)}, bf16[2,56,768]{2,1,0:T(8,128)(2,1)S(1)}, u32[]{:S(2)}, u32[]{:S(2)}) collective-permute-start(bf16[2,56,768]{2,1,0:T(8,128)(2,1)S(1)} %stack.102), channel_id=1, source_target_pairs={{0,4},{1,5},{2,6},{3,7},{4,0},{5,1},{6,2},{7,3},{8,12},{9,13},{10,... | collective-permute-start | bytes 516104 | tf_op jit(solution)/shard_map/cond/branch_0_fun/ppermute | solution.py:366
  123.3 15.5 %collective-permute-start.17 = (bf16[1,56,768]{2,1,0:T(8,128)(2,1)S(1)}, bf16[1,56,768]{2,1,0:T(8,128)(2,1)S(1)}, u32[]{:S(2)}, u32[]{:S(2)}) collective-permute-start(bf16[1,56,768]{2,1,0:T(8,128)(2,1)S(1)} %slice.551), channel_id=1, source_target_pairs={{0,4},{1,5},{2,6},{3,7},{4,0},{5,1},{6,2},{7,3},{8,12},{9,13},{10,... | collective-permute-start | bytes 258056 | tf_op jit(solution)/shard_map/cond/branch_0_fun/ppermute | solution.py:366
  126.8 13.0 %collective-permute-start.2 = (bf16[1,56,768]{2,1,0:T(8,128)(2,1)S(1)}, bf16[1,56,768]{2,1,0:T(8,128)(2,1)S(1)}, u32[]{:S(2)}, u32[]{:S(2)}) collective-permute-start(bf16[1,56,768]{2,1,0:T(8,128)(2,1)S(1)} %slice.553), channel_id=1, source_target_pairs={{0,4},{1,5},{2,6},{3,7},{4,0},{5,1},{6,2},{7,3},{8,12},{9,13},{10,... | collective-permute-start | bytes 258056 | tf_op jit(solution)/shard_map/cond/branch_0_fun/ppermute | solution.py:366
  143.6 5.5 %collective-permute-start.18 = (bf16[1,56,384]{2,1,0:T(8,128)(2,1)S(1)}, bf16[1,56,384]{2,1,0:T(8,128)(2,1)S(1)}, u32[]{:S(2)}, u32[]{:S(2)}) collective-permute-start(bf16[1,56,384]{2,1,0:T(8,128)(2,1)S(1)} %get-tuple-element.203), channel_id=1, source_target_pairs={{0,4},{1,5},{2,6},{3,7},{4,0},{5,1},{6,2},{7,3},{8,12},{9,13},{10,... | collective-permute-start | bytes 129032 | tf_op jit(solution)/shard_map/cond/branch_0_fun/ppermute | solution.py:366
  143.7 6.3 %collective-permute-start.12 = (bf16[1,56,384]{2,1,0:T(8,128)(2,1)S(1)}, bf16[1,56,384]{2,1,0:T(8,128)(2,1)S(1)}, u32[]{:S(2)}, u32[]{:S(2)}) collective-permute-start(bf16[1,56,384]{2,1,0:T(8,128)(2,1)S(1)} %get-tuple-element.204), channel_id=1, source_target_pairs={{0,1},{1,0},{2,3},{3,2},{4,5},{5,4},{6,7},{7,6},{8,9},{9,8},{10,11... | collective-permute-start | bytes 129032 | tf_op jit(solution)/shard_map/cond/branch_0_fun/ppermute | solution.py:366
  144.9 7.0 %collective-permute-start.6 = (bf16[1,56,384]{2,1,0:T(8,128)(2,1)S(1)}, bf16[1,56,384]{2,1,0:T(8,128)(2,1)S(1)}, u32[]{:S(2)}, u32[]{:S(2)}) collective-permute-start(bf16[1,56,384]{2,1,0:T(8,128)(2,1)S(1)} %get-tuple-element.202), channel_id=1, source_target_pairs={{0,4},{1,5},{2,6},{3,7},{4,0},{5,1},{6,2},{7,3},{8,12},{9,13},{10,... | collective-permute-start | bytes 129032 | tf_op jit(solution)/shard_map/cond/branch_0_fun/ppermute | solution.py:366
  147.8 6.0 %collective-permute-start.25 = (bf16[2,56,384]{2,1,0:T(8,128)(2,1)S(1)}, bf16[2,56,384]{2,1,0:T(8,128)(2,1)S(1)}, u32[]{:S(2)}, u32[]{:S(2)}) collective-permute-start(bf16[2,56,384]{2,1,0:T(8,128)(2,1)S(1)} %pad_maximum_fusion.9), channel_id=1, source_target_pairs={{0,4},{1,5},{2,6},{3,7},{4,0},{5,1},{6,2},{7,3},{8,12},{9,13},{10,... | collective-permute-start | bytes 258056 | tf_op jit(solution)/shard_map/cond/branch_0_fun/ppermute | solution.py:366
  149.2 6.7 %collective-permute-start.19 = (bf16[2,56,384]{2,1,0:T(8,128)(2,1)S(1)}, bf16[2,56,384]{2,1,0:T(8,128)(2,1)S(1)}, u32[]{:S(2)}, u32[]{:S(2)}) collective-permute-start(bf16[2,56,384]{2,1,0:T(8,128)(2,1)S(1)} %pad_maximum_fusion.8), channel_id=1, source_target_pairs={{0,2},{1,3},{2,0},{3,1},{4,6},{5,7},{6,4},{7,5},{8,10},{9,11},{10,... | collective-permute-start | bytes 258056 | tf_op jit(solution)/shard_map/cond/branch_0_fun/ppermute | solution.py:366
  150.0 6.8 %collective-permute-start.13 = (bf16[2,56,384]{2,1,0:T(8,128)(2,1)S(1)}, bf16[2,56,384]{2,1,0:T(8,128)(2,1)S(1)}, u32[]{:S(2)}, u32[]{:S(2)}) collective-permute-start(bf16[2,56,384]{2,1,0:T(8,128)(2,1)S(1)} %pad_maximum_fusion.7), channel_id=1, source_target_pairs={{0,4},{1,5},{2,6},{3,7},{4,0},{5,1},{6,2},{7,3},{8,12},{9,13},{10,... | collective-permute-start | bytes 258056 | tf_op jit(solution)/shard_map/cond/branch_0_fun/ppermute | solution.py:366
  151.9 5.5 %collective-permute-start.7 = (bf16[2,56,384]{2,1,0:T(8,128)(2,1)S(1)}, bf16[2,56,384]{2,1,0:T(8,128)(2,1)S(1)}, u32[]{:S(2)}, u32[]{:S(2)}) collective-permute-start(bf16[2,56,384]{2,1,0:T(8,128)(2,1)S(1)} %pad_maximum_fusion.6), channel_id=1, source_target_pairs={{0,2},{1,3},{2,0},{3,1},{4,6},{5,7},{6,4},{7,5},{8,10},{9,11},{10,... | collective-permute-start | bytes 258056 | tf_op jit(solution)/shard_map/cond/branch_0_fun/ppermute | solution.py:366
  153.8 6.0 %collective-permute-start.26 = (bf16[4,56,384]{2,1,0:T(8,128)(2,1)S(1)}, bf16[4,56,384]{2,1,0:T(8,128)(2,1)S(1)}, u32[]{:S(2)}, u32[]{:S(2)}) collective-permute-start(bf16[4,56,384]{2,1,0:T(8,128)(2,1)S(1)} %pad_maximum_fusion.5.refs_6_), channel_id=1, source_target_pairs={{0,2},{1,3},{2,0},{3,1},{4,6},{5,7},{6,4},{7,5},{8,10},{9,11},{10,... | collective-permute-start | bytes 516104 | tf_op jit(solution)/shard_map/cond/branch_0_fun/ppermute | solution.py:366
  156.8 5.5 %collective-permute-start.14 = (bf16[4,56,384]{2,1,0:T(8,128)(2,1)S(1)}, bf16[4,56,384]{2,1,0:T(8,128)(2,1)S(1)}, u32[]{:S(2)}, u32[]{:S(2)}) collective-permute-start(bf16[4,56,384]{2,1,0:T(8,128)(2,1)S(1)} %pad_maximum_fusion.2.refs_2_), channel_id=1, source_target_pairs={{0,2},{1,3},{2,0},{3,1},{4,6},{5,7},{6,4},{7,5},{8,10},{9,11},{10,... | collective-permute-start | bytes 516104 | tf_op jit(solution)/shard_map/cond/branch_0_fun/ppermute | solution.py:366
  157.5 5.8 %collective-permute-start.8 = (bf16[4,56,384]{2,1,0:T(8,128)(2,1)S(1)}, bf16[4,56,384]{2,1,0:T(8,128)(2,1)S(1)}, u32[]{:S(2)}, u32[]{:S(2)}) collective-permute-start(bf16[4,56,384]{2,1,0:T(8,128)(2,1)S(1)} %pad_maximum_fusion.1.refs_0_), channel_id=1, source_target_pairs={{0,1},{1,0},{2,3},{3,2},{4,5},{5,4},{6,7},{7,6},{8,9},{9,8},{10,11... | collective-permute-start | bytes 516104 | tf_op jit(solution)/shard_map/cond/branch_0_fun/ppermute | solution.py:366
  (25 other events, 194.6 us)
where the time goes:
time: 192 us; the launch traced here: 191 us
  Pallas kernels  68.8 us (36%)
  waiting for transfers between devices  50.4 us (26%)
  starting transfers between devices  38.7 us (20%)
  blocking collectives  18.1 us (9%)
  local copies, waits for them, and re-layouts  8.77 us (5%)
  other arithmetic  3.31 us (2%)
    ppermute x27, waiting for transfers between devices, exchange(): return lax.ppermute(x, 'gy', [(i, i ^ k) for i in range(parts)])  37 us
    pallas_call x4, Pallas kernels, gate_up(): pl.pallas_call(functools.partial(gate_up_kernel, bit, chunk), out_shape=(...  34.9 us
    ppermute x27, starting transfers between devices, exchange(): return lax.ppermute(x, 'gy', [(i, i ^ k) for i in range(parts)])  26.9 us
    pallas_call x1, Pallas kernels, down(): pl.pallas_call(functools.partial(down_kernel, names), out_shape=jax.Shape...  15.9 us
    pallas_call x1, Pallas kernels, attend_local(): pl.pallas_call(attend_kernel, out_shape=out, grid_spec=pltpu.PrefetchScal...  10.9 us
    all_to_all x1, blocking collectives, shards(): routed = lax.all_to_all(routed.reshape(num_gx, rows, -1), 'gx', 0, 0)  9.97 us
    all_to_all x1, starting transfers between devices, shards(): part = lax.all_to_all(part, 'gy', 0, 0)  8.11 us
    all_gather x1, blocking collectives, shards(): hidden_all = lax.all_gather(hidden, 'gx', axis=0, tiled=True)  8.1 us
  transfers between devices with their start and end apart: 29, of which 17 were waited for; matrix products, arithmetic and copies ran while one was open for 4% of the time, Pallas kernels for 14%

commit v1 on v0

--- a/solution.py
+++ b/solution.py
@@ -19,19 +19,19 @@
 LOWEST = -1e30
 EPSILON = 1e-05
 SCALING = HEAD_SIZE ** (-0.5)
-BLOCK = 512
+BLOCK = 1024
 ROWS = 16
 ALIGN = 8
 CHUNKS = 4
-UNROLL = 4
+UNROLL = 2
 
 f32 = jnp.float32
 bf16 = jnp.bfloat16
-VMEM_LIMIT = 56 * 1024 * 1024
-
-
-def params(**more):
-    return pltpu.CompilerParams(vmem_limit_bytes=VMEM_LIMIT, **more)
+MIB = 1024 * 1024
+
+
+def params(mib):
+    return pltpu.CompilerParams(vmem_limit_bytes=mib * MIB)
 
 
 def whole(shape):
@@ -166,8 +166,8 @@
             in_specs=[
                 whole((rows, width)),
                 whole((1, positions)),
-                pl.BlockSpec(memory_space=pl.ANY),
-                pl.BlockSpec(memory_space=pl.ANY),
+                pl.BlockSpec(memory_space=pltpu.HBM),
+                pl.BlockSpec(memory_space=pltpu.HBM),
             ],
             out_specs=whole(out.shape),
             scratch_shapes=[
@@ -180,7 +180,7 @@
                 pltpu.SemaphoreType.DMA((2, positions // block)),
             ],
         ),
-        compiler_params=params(),
+        compiler_params=params(56),
         name="attend",
     )(owners.reshape(-1), queries, owners, keys, values)
 
@@ -232,7 +232,7 @@
     return pl.pallas_call(
         merge_kernel,
         out_shape=jax.ShapeDtypeStruct(queries.shape, bf16),
-        compiler_params=params(),
+        compiler_params=params(6),
         name="merge",
     )(part, queries, token_key_value)
 
@@ -286,7 +286,7 @@
             jax.ShapeDtypeStruct((rank_t.shape[0], slots, features), bf16),
             jax.ShapeDtypeStruct((8, requests), f32),
         ),
-        compiler_params=params(),
+        compiler_params=params(6),
         name="dispatch",
     )(hidden_all, gain.reshape(1, -1), rank_t)
 
@@ -313,14 +313,18 @@
     unroll = min(UNROLL, experts)
 
     def visit(step, carry):
-        for i in range(unroll):
-            e = step * unroll + i
+        these = [step * unroll + i for i in range(unroll)]
+        for e in these:
+            for copy in copies(e):
+                copy.wait()
+        products = [
+            [jnp.dot(x_ref[e], buf[e, half], preferred_element_type=f32) for half in range(2)]
+            for e in these
+        ]
+        for e, pair in zip(these, products):
             rows = pl.ds(pl.multiple_of(base_s[e], ALIGN), slots)
-            x = x_ref[e]
-            for half, copy in enumerate(copies(e)):
-                copy.wait()
-                lanes = slice(half * units, (half + 1) * units)
-                scr[rows, lanes] += jnp.dot(x, buf[e, half], preferred_element_type=f32)
+            for half in range(2):
+                scr[rows, half * units : (half + 1) * units] += pair[half]
         return carry
 
     lax.fori_loop(0, experts // unroll, visit, 0)
@@ -344,7 +348,7 @@
         grid_spec=pltpu.PrefetchScalarGridSpec(
             num_scalar_prefetch=2,
             grid=(1,),
-            in_specs=[whole(x.shape), pl.BlockSpec(memory_space=pl.ANY)],
+            in_specs=[whole(x.shape), pl.BlockSpec(memory_space=pltpu.HBM)],
             out_specs=(whole(out.shape), whole(out.shape)),
             scratch_shapes=[
                 pltpu.VMEM((capacity + slots, 2 * units), f32),
@@ -352,7 +356,7 @@
                 pltpu.SemaphoreType.DMA((experts, 2)),
             ],
         ),
-        compiler_params=params(),
+        compiler_params=params(40),
         cost_estimate=pl.CostEstimate(
             flops=4 * experts * slots * features * units,
             bytes_accessed=experts * features * units * 4 + out.size * 4,
@@ -389,12 +393,11 @@
 
 def down_kernel(names, me_s, base_s, *refs):
     acts = refs[: len(names)]
-    rank_ref, weight_ref, w_hbm, out_ref, scr, buf, sem = refs[len(names) :]
+    high_ref, low_ref, w_hbm, out_ref, scr, rows_scr, buf, sem = refs[len(names) :]
     experts = buf.shape[0]
     each = acts[0].shape[1]
     capacity = 2 * acts[0].shape[0] * each
     slots = scr.shape[0] - capacity
-    total = rank_ref.shape[0]
     me = me_s[0]
 
     def fetch(e):
@@ -409,41 +412,37 @@
         for i, n in enumerate(ns):
             at = jnp.bitwise_xor(me, n) * each
             scr[pl.ds(pl.multiple_of(at, ALIGN), each), lanes] = ref[i].astype(f32)
-    out_ref[...] = jnp.zeros(out_ref.shape, f32)
-    column = lax.broadcasted_iota(jnp.int32, (total, 128), 1)
-    slot = lax.broadcasted_iota(jnp.int32, (total, slots), 1)
     unroll = min(UNROLL, experts)
 
     def visit(step, carry):
-        add = None
-        for i in range(unroll):
-            e = step * unroll + i
-            rows = pl.ds(pl.multiple_of(base_s[e], ALIGN), slots)
-            x = scr[rows, :].astype(bf16)
+        these = [step * unroll + i for i in range(unroll)]
+        for e in these:
             fetch(e).wait()
-            y = lax.dot_general(
-                x, buf[e], (((1,), (1,)), ((), ())), preferred_element_type=f32
+        products = [
+            lax.dot_general(
+                scr[pl.ds(pl.multiple_of(base_s[e], ALIGN), slots), :].astype(bf16),
+                buf[e],
+                (((1,), (1,)), ((), ())),
+                preferred_element_type=f32,
             ).astype(bf16)
-            rank = jnp.sum(jnp.where(column == e, rank_ref[...], 0), axis=1, keepdims=True)
-            weight = jnp.sum(
-                jnp.where(column == e, weight_ref[...], 0.0), axis=1, keepdims=True
-            )
-            pick = (rank == slot).astype(f32).astype(bf16)
-            term = weight * jnp.dot(pick, y, preferred_element_type=f32)
-            add = term if add is None else add + term
-        out_ref[...] += add
+            for e in these
+        ]
+        for e, product in zip(these, products):
+            rows_scr[pl.ds(pl.multiple_of(e * slots, 16), slots), :] = product
         return carry
 
     lax.fori_loop(0, experts // unroll, visit, 0)
-
-
-def down(acts, names, w_down_t, base, me, rank, weight, slots):
+    rows = rows_scr[...]
+    out_ref[...] = jnp.dot(high_ref[...], rows, preferred_element_type=f32) + jnp.dot(
+        low_ref[...], rows, preferred_element_type=f32
+    )
+
+
+def down(acts, names, w_down_t, base, me, high, low):
     experts, features, hidden_units = w_down_t.shape
     capacity = acts[0].shape[0] * acts[0].shape[1] * 2
-    total = rank.shape[0]
-    pad = ((0, 0), (0, 128 - experts))
-    rank = jnp.pad(rank, pad)
-    weight = jnp.pad(weight, pad)
+    slots = high.shape[1] // experts
+    total = high.shape[0]
     return pl.pallas_call(
         functools.partial(down_kernel, names),
         out_shape=jax.ShapeDtypeStruct((total, features), f32),
@@ -451,17 +450,46 @@
             num_scalar_prefetch=2,
             grid=(1,),
             in_specs=[whole(a.shape) for a in acts]
-            + [whole(rank.shape), whole(weight.shape), pl.BlockSpec(memory_space=pl.ANY)],
+            + [whole(high.shape), whole(low.shape), pl.BlockSpec(memory_space=pltpu.HBM)],
             out_specs=whole((total, features)),
             scratch_shapes=[
                 pltpu.VMEM((capacity + slots, hidden_units), f32),
+                pltpu.VMEM((experts * slots, features), bf16),
                 pltpu.VMEM(w_down_t.shape, bf16),
                 pltpu.SemaphoreType.DMA((experts,)),
             ],
         ),
-        compiler_params=params(),
+        compiler_params=params(26),
         name="down",
-    )(me, base, *acts, rank, weight, w_down_t)
+    )(me, base, *acts, high, low, w_down_t)
+
+
+def plan_kernel(rank_ref, weight_ref, high_ref, low_ref):
+    requests, experts = rank_ref.shape
+    slots = high_ref.shape[1] // experts
+    rank = rank_ref[...].astype(f32).astype(bf16)
+    weight = weight_ref[...]
+    weight_high = weight.astype(bf16)
+    weight_low = (weight - weight_high.astype(f32)).astype(bf16)
+    expert = lax.broadcasted_iota(jnp.int32, (experts, experts * slots), 0)
+    column = lax.broadcasted_iota(jnp.int32, (experts, experts * slots), 1)
+    spread = ((column >= expert * slots) & (column < (expert + 1) * slots)).astype(f32).astype(bf16)
+    offset = jnp.sum(jnp.where(column >= expert * slots, 1, 0), axis=0, keepdims=True) - 1
+    slot = column[0:1] - offset * slots
+
+    def over(x):
+        return jnp.dot(x, spread, preferred_element_type=f32)
+
+    here = over(rank).astype(jnp.int32) == slot
+    high_ref[...] = jnp.where(here, over(weight_high), 0.0).astype(bf16)
+    low_ref[...] = jnp.where(here, over(weight_low), 0.0).astype(bf16)
+
+
+def plan(rank, weight, slots):
+    out = jax.ShapeDtypeStruct((rank.shape[0], rank.shape[1] * slots), bf16)
+    return pl.pallas_call(
+        plan_kernel, out_shape=(out, out), compiler_params=params(6), name="plan"
+    )(rank, weight)
 
 
 def sum_over_gy(x, parts):
@@ -472,7 +500,7 @@
     return x
 
 
-def experts_part(capacity, x, square, w_gate_up, w_down_t, base, rank, place, weight, me, parts, slots):
+def experts_part(capacity, x, square, w_gate_up, w_down_t, base, place, high, low, me, parts):
     units = w_down_t.shape[2] // CHUNKS
     rows = capacity // parts
     here = me[0] * rows + lax.iota(jnp.int32, rows)
@@ -493,7 +521,7 @@
         left, right, left_names, right_names = gather_rows(act, order[::-1], parts)
         acts += [left, right]
         names += [left_names, right_names]
-    return down(acts, names, w_down_t, base, me, rank, weight, slots)
+    return down(acts, names, w_down_t, base, me, high, low)
 
 
 def out_kernel(a_ref, w_ref, r_ref, o_ref):
@@ -507,7 +535,7 @@
     return pl.pallas_call(
         out_kernel,
         out_shape=jax.ShapeDtypeStruct(residual.shape, bf16),
-        compiler_params=params(),
+        compiler_params=params(8),
         name="project",
     )(attention, out_weight, residual)
 
@@ -533,7 +561,7 @@
     me_x = lax.axis_index("gx")
     me = jnp.full((1,), me_y, jnp.int32)
     each = rows // parts
-    slots = -(-(num_gx * CAPS + ALIGN - 1) // ALIGN) * ALIGN
+    slots = -(-(num_gx * CAPS + ALIGN - 1) // 16) * 16
     local = w_gate_up.shape[0]
 
     part = attend_local(queries, group_cached_keys, group_cached_values, owners, parts)
@@ -551,6 +579,7 @@
 
     mixing = jax.nn.softmax(gate_logits, axis=-1)
     rank, place, weight, base, needed = routing(expert_ids, mixing, num_gx, me_x)
+    high, low = plan(rank, weight, slots)
     x, square = dispatch(hidden_all, norm_gain, rank.T, slots)
 
     capacity = local * num_gx * CAPS
@@ -562,14 +591,14 @@
         w_gate_up,
         jnp.swapaxes(w_down, 1, 2),
         base,
-        rank,
         place,
-        weight,
+        high,
+        low,
         me,
     )
     routed = lax.switch(
         branch,
-        [lambda *o, c=c: experts_part(c, *o, parts=parts, slots=slots) for c in sizes],
+        [lambda *o, c=c: experts_part(c, *o, parts=parts) for c in sizes],
         *operands,
     )
     routed = lax.all_to_all(routed.reshape(num_gx, rows, -1), "gx", 0, 0)

time: 192 us -> 163 us (0.85)
  Pallas kernels: 68.8 us -> 40.3 us
  local copies, waits for them, and re-layouts: 8.77 us -> 2.17 us
  other arithmetic: 3.31 us -> 7.85 us
    pallas_call x4, Pallas kernels: 34.9 us -> 19.1 us  [gate_up(): pl.pallas_call(functools.partial(gate_up_kernel, bit, chunk), out_shape=(...]
    pallas_call x1, Pallas kernels: 15.9 us -> 9 us  [down(): pl.pallas_call(functools.partial(down_kernel, names), out_shape=jax.Shape...]
    pallas_call x1, Pallas kernels: 2.7 us -> 0.61 us  [project(): pl.pallas_call(out_kernel, out_shape=jax.ShapeDtypeStruct(residual.shape,...]
    pallas_call x1, Pallas kernels: 10.9 us -> 8.83 us  [attend_local(): pl.pallas_call(attend_kernel, out_shape=out, grid_spec=pltpu.PrefetchScal...]
    another operation x2, other arithmetic: 0.18 us -> 2.14 us
    add x2, other arithmetic: 0.14 us -> 2.1 us  [scatter_sums(): total = keep.astype(f32) + exchange(send, order[0], parts).astype(f32)]
  transfers between devices with their start and end apart: 29 -> 29, of which waited for: 17 -> 16; matrix products, arithmetic and copies ran while one was open for 4% -> 5% of each run, Pallas kernels for 14% -> 10%
where the time goes in v1:
time: 163 us; the launch traced here: 162 us
  waiting for transfers between devices  51.3 us (31%)
  Pallas kernels  40.3 us (25%)
  starting transfers between devices  40.3 us (25%)
  blocking collectives  17.6 us (11%)
  other arithmetic  7.85 us (5%)
  local copies, waits for them, and re-layouts  2.17 us (1%)
    ppermute x27, waiting for transfers between devices, exchange(): return lax.ppermute(x, 'gy', [(i, i ^ k) for i in range(parts)])  38.1 us
    ppermute x27, starting transfers between devices, exchange(): return lax.ppermute(x, 'gy', [(i, i ^ k) for i in range(parts)])  28.3 us
    pallas_call x4, Pallas kernels, gate_up(): pl.pallas_call(functools.partial(gate_up_kernel, bit, chunk), out_shape=(...  19.1 us
    all_to_all x1, blocking collectives, shards(): routed = lax.all_to_all(routed.reshape(num_gx, rows, -1), 'gx', 0, 0)  11 us
    pallas_call x1, Pallas kernels, down(): pl.pallas_call(functools.partial(down_kernel, names), out_shape=jax.Shape...  9 us
    pallas_call x1, Pallas kernels, attend_local(): pl.pallas_call(attend_kernel, out_shape=out, grid_spec=pltpu.PrefetchScal...  8.83 us
    all_to_all x1, starting transfers between devices, shards(): part = lax.all_to_all(part, 'gy', 0, 0)  8.37 us
    all_to_all x1, waiting for transfers between devices, shards(): part = lax.all_to_all(part, 'gy', 0, 0)  7.78 us
  transfers between devices with their start and end apart: 29, of which 16 were waited for; matrix products, arithmetic and copies ran while one was open for 5% of the time, Pallas kernels for 10%

profile of v1, /device:TPU:0, one launch (start us, length us, event | category | flops | bytes accessed | tf_op | source)
XLA Modules:
  0.0 161.7 jit_solution(7727756094867667296)
XLA Ops:
  0.0 8.8 %attend.1 = bf16[8,8,2688]{2,1,0:T(8,128)(2,1)} custom-call(s32[4096]{0:T(1024)} %bitcast.82, bf16[64,2560]{1,0:T(8,128)(2,1)} %q_ref.1, s32[1,4096]{1,0:T(1,128)} %own_ref.1, bf16[1,4096,512]{2,1,0:T(8,128)(2,1)} %k_hbm.1, bf16[1,4096,512]{2,1,0:T(8,128)(2,1)} %v_hbm.1), custom_call_target="tpu_custom_call" | custom-call | tf_op jit(solution)/shard_map/attend/pallas_call | solution.py:160
  8.9 8.4 %all-to-all-start = ((bf16[8,8,2688]{2,1,0:T(8,128)(2,1)}), bf16[8,8,2688]{2,1,0:T(8,128)(2,1)S(1)}, u32[]{:S(2)}, u32[]{:S(2)}) async-start(bf16[8,8,2688]{2,1,0:T(8,128)(2,1)} %attend.1), calls=%async_computation | async-start | bytes 688128 | tf_op jit(solution)/shard_map/all_to_all | solution.py:568
  19.1 7.8 %all-to-all-done.part_ref = bf16[8,8,2688]{2,1,0:T(8,128)(2,1)S(1)} async-done(((bf16[8,8,2688]{2,1,0:T(8,128)(2,1)}), bf16[8,8,2688]{2,1,0:T(8,128)(2,1)S(1)}, u32[]{:S(2)}, u32[]{:S(2)}) %all-to-all-start) | async-done | bytes 344096 | tf_op jit(solution)/shard_map/all_to_all | solution.py:568
  28.2 3.6 %all-to-all-start.1 = ((bf16[8,8,2560]{2,1,0:T(8,128)(2,1)}), bf16[8,8,2560]{2,1,0:T(8,128)(2,1)S(1)}, u32[]{:S(2)}, u32[]{:S(2)}) async-start(bf16[8,8,2560]{2,1,0:T(8,128)(2,1)} %broadcast_in_dim.146), calls=%async_computation.1 | async-start | bytes 655360 | tf_op jit(solution)/shard_map/all_to_all | solution.py:574
  36.0 5.4 %all-to-all-done.1 = bf16[8,8,2560]{2,1,0:T(8,128)(2,1)S(1)} async-done(((bf16[8,8,2560]{2,1,0:T(8,128)(2,1)}), bf16[8,8,2560]{2,1,0:T(8,128)(2,1)S(1)}, u32[]{:S(2)}, u32[]{:S(2)}) %all-to-all-start.1) | async-done | bytes 327712 | tf_op jit(solution)/shard_map/all_to_all | solution.py:574
  42.0 6.6 %all_gather.3.h_ref = bf16[256,320]{1,0:T(8,128)(2,1)S(1)} all-gather(bf16[64,320]{1,0:T(8,128)(2,1)S(1)} %project.1), channel_id=1, replica_groups=mesh['gx'=4,'gy'=8] {'gx'}, dimensions={0}, use_global_device_ids=true | all-gather | bytes 204800 | tf_op jit(solution)/shard_map/all_gather | solution.py:578
  49.5 100.5 %conditional.1 = (f32[256,320]{1,0:T(8,128)}) conditional(s32[]{:T(128)} %clamp.3, (s32[1]{0:T(128)}, s32[16]{0:T(128)S(1)}, bf16[16,64,320]{2,1,0:T(8,128)(2,1)S(1)}, bf16[16,320,3072]{2,1,0:T(8,128)(2,1)}, s32[256,16]{1,0:T(8,128)}, /*index=5*/s32[]{:T(128)}, f32[2,128]{1,0:T(2,128)S(1)}, bf16[256,1024]{1,0:T(8,128)(2,1)S(1)}, ...), branch_computations={%region_9.12_spmd, %region_12.15_spmd, %region_15.18_spmd} | conditional | flops 2023220480 | bytes 151413600 | solution.py:599
  49.5 4.8 %gate_up.14 = (bf16[4,56,768]{2,1,0:T(8,128)(2,1)S(1)}, bf16[4,56,768]{2,1,0:T(8,128)(2,1)S(1)}) custom-call(s32[1]{0:T(128)} %get-tuple-element.68.me_s, s32[16]{0:T(128)S(1)} %get-tuple-element.70.base_s, bf16[16,64,320]{2,1,0:T(8,128)(2,1)S(1)} %get-tuple-element.71.x_ref, bf16[16,320,3072]{2,1,0:T(8,128)(2,1)} %get-tuple-element.72.w_hbm), custom_call_target="tpu_custom_call" | custom-call | flops 503316480 | bytes 8552448 | tf_op jit(solution)/shard_map/cond/branch_0_fun/gate_up/pallas_call | solution.py:345
  55.9 4.8 %gate_up.12 = (bf16[4,56,768]{2,1,0:T(8,128)(2,1)S(1)}, bf16[4,56,768]{2,1,0:T(8,128)(2,1)S(1)}) custom-call(s32[1]{0:T(128)} %get-tuple-element.68.me_s, s32[16]{0:T(128)S(1)} %get-tuple-element.70.base_s, bf16[16,64,320]{2,1,0:T(8,128)(2,1)S(1)} %get-tuple-element.71.x_ref, bf16[16,320,3072]{2,1,0:T(8,128)(2,1)} %get-tuple-element.72.w_hbm), custom_call_target="tpu_custom_call" | custom-call | flops 503316480 | bytes 8552448 | tf_op jit(solution)/shard_map/cond/branch_0_fun/gate_up/pallas_call | solution.py:345
  61.2 4.8 %gate_up.13 = (bf16[4,56,768]{2,1,0:T(8,128)(2,1)S(1)}, bf16[4,56,768]{2,1,0:T(8,128)(2,1)S(1)}) custom-call(s32[1]{0:T(128)} %get-tuple-element.68.me_s, s32[16]{0:T(128)S(1)} %get-tuple-element.70.base_s, bf16[16,64,320]{2,1,0:T(8,128)(2,1)S(1)} %get-tuple-element.71.x_ref, bf16[16,320,3072]{2,1,0:T(8,128)(2,1)} %get-tuple-element.72.w_hbm), custom_call_target="tpu_custom_call" | custom-call | flops 503316480 | bytes 8552448 | tf_op jit(solution)/shard_map/cond/branch_0_fun/gate_up/pallas_call | solution.py:345
  67.7 4.8 %gate_up.15 = (bf16[4,56,768]{2,1,0:T(8,128)(2,1)S(1)}, bf16[4,56,768]{2,1,0:T(8,128)(2,1)S(1)}) custom-call(s32[1]{0:T(128)} %get-tuple-element.68.me_s, s32[16]{0:T(128)S(1)} %get-tuple-element.70.base_s, bf16[16,64,320]{2,1,0:T(8,128)(2,1)S(1)} %get-tuple-element.71.x_ref, bf16[16,320,3072]{2,1,0:T(8,128)(2,1)} %get-tuple-element.72.w_hbm), custom_call_target="tpu_custom_call" | custom-call | flops 503316480 | bytes 8552448 | tf_op jit(solution)/shard_map/cond/branch_0_fun/gate_up/pallas_call | solution.py:345
  72.4 2.0 %collective-permute-start.21 = (bf16[4,56,768]{2,1,0:T(8,128)(2,1)S(1)}, bf16[4,56,768]{2,1,0:T(8,128)(2,1)}, u32[]{:S(2)}, u32[]{:S(2)}) collective-permute-start(bf16[4,56,768]{2,1,0:T(8,128)(2,1)S(1)} %get-tuple-element.83), channel_id=1, source_target_pairs={{0,2},{1,3},{2,0},{3,1},{4,6},{5,7},{6,4},{7,5},{8,10},{9,11},{10,... | collective-permute-start | bytes 1032200 | tf_op jit(solution)/shard_map/cond/branch_0_fun/ppermute | solution.py:370
  74.6 8.7 %collective-permute-done.4 = f32[2,128]{1,0:T(2,128)S(1)} collective-permute-done((f32[2,128]{1,0:T(2,128)S(1)}, f32[2,128]{1,0:T(2,128)S(1)}, u32[]{:S(2)}, u32[]{:S(2)}) %collective-permute-start.4) | collective-permute-done | bytes 1056 | tf_op jit(solution)/shard_map/cond/branch_0_fun/ppermute | solution.py:370
  84.6 3.2 %collective-permute-done.5 = f32[2,128]{1,0:T(2,128)S(1)} collective-permute-done((f32[2,128]{1,0:T(2,128)S(1)}, f32[2,128]{1,0:T(2,128)S(1)}, u32[]{:S(2)}, u32[]{:S(2)}) %collective-permute-start.5) | collective-permute-done | bytes 1056 | tf_op jit(solution)/shard_map/cond/branch_0_fun/ppermute | solution.py:370
  95.6 2.0 %collective-permute-start.22 = (bf16[2,56,768]{2,1,0:T(8,128)(2,1)S(1)}, bf16[2,56,768]{2,1,0:T(8,128)(2,1)S(1)}, u32[]{:S(2)}, u32[]{:S(2)}) collective-permute-start(bf16[2,56,768]{2,1,0:T(8,128)(2,1)S(1)} %stack.102), channel_id=1, source_target_pairs={{0,4},{1,5},{2,6},{3,7},{4,0},{5,1},{6,2},{7,3},{8,12},{9,13},{10,... | collective-permute-start | bytes 516104 | tf_op jit(solution)/shard_map/cond/branch_0_fun/ppermute | solution.py:370
  100.8 10.4 %collective-permute-done.10 = bf16[2,56,768]{2,1,0:T(8,128)(2,1)S(1)} collective-permute-done((bf16[2,56,768]{2,1,0:T(8,128)(2,1)S(1)}, bf16[2,56,768]{2,1,0:T(8,128)(2,1)S(1)}, u32[]{:S(2)}, u32[]{:S(2)}) %collective-permute-start.10) | collective-permute-done | bytes 172064 | tf_op jit(solution)/shard_map/cond/branch_0_fun/ppermute | solution.py:370
  111.2 1.7 %collective-permute-start.11 = (bf16[1,56,768]{2,1,0:T(8,128)(2,1)S(1)}, bf16[1,56,768]{2,1,0:T(8,128)(2,1)S(1)}, u32[]{:S(2)}, u32[]{:S(2)}) collective-permute-start(bf16[1,56,768]{2,1,0:T(8,128)(2,1)S(1)} %slice.552), channel_id=1, source_target_pairs={{0,1},{1,0},{2,3},{3,2},{4,5},{5,4},{6,7},{7,6},{8,9},{9,8},{10,11... | collective-permute-start | bytes 258056 | tf_op jit(solution)/shard_map/cond/branch_0_fun/ppermute | solution.py:370
  116.3 3.2 %collective-permute-done.23 = bf16[1,56,768]{2,1,0:T(8,128)(2,1)S(1)} collective-permute-done((bf16[1,56,768]{2,1,0:T(8,128)(2,1)S(1)}, bf16[1,56,768]{2,1,0:T(8,128)(2,1)S(1)}, u32[]{:S(2)}, u32[]{:S(2)}) %collective-permute-start.23) | collective-permute-done | bytes 86048 | tf_op jit(solution)/shard_map/cond/branch_0_fun/ppermute | solution.py:370
  121.8 2.9 %collective-permute-start.6 = (bf16[1,56,384]{2,1,0:T(8,128)(2,1)S(1)}, bf16[1,56,384]{2,1,0:T(8,128)(2,1)S(1)}, u32[]{:S(2)}, u32[]{:S(2)}) collective-permute-start(bf16[1,56,384]{2,1,0:T(8,128)(2,1)S(1)} %get-tuple-element.206), channel_id=1, source_target_pairs={{0,4},{1,5},{2,6},{3,7},{4,0},{5,1},{6,2},{7,3},{8,12},{9,13},{10,... | collective-permute-start | bytes 129032 | tf_op jit(solution)/shard_map/cond/branch_0_fun/ppermute | solution.py:370
  127.0 2.1 %collective-permute-start.13 = (bf16[2,56,384]{2,1,0:T(8,128)(2,1)S(1)}, bf16[2,56,384]{2,1,0:T(8,128)(2,1)S(1)}, u32[]{:S(2)}, u32[]{:S(2)}) collective-permute-start(bf16[2,56,384]{2,1,0:T(8,128)(2,1)S(1)} %pad_maximum_fusion.7), channel_id=1, source_target_pairs={{0,4},{1,5},{2,6},{3,7},{4,0},{5,1},{6,2},{7,3},{8,12},{9,13},{10,... | collective-permute-start | bytes 258056 | tf_op jit(solution)/shard_map/cond/branch_0_fun/ppermute | solution.py:370
  131.3 2.2 %collective-permute-done.19 = bf16[2,56,384]{2,1,0:T(8,128)(2,1)S(1)} collective-permute-done((bf16[2,56,384]{2,1,0:T(8,128)(2,1)S(1)}, bf16[2,56,384]{2,1,0:T(8,128)(2,1)S(1)}, u32[]{:S(2)}, u32[]{:S(2)}) %collective-permute-start.19) | collective-permute-done | bytes 86048 | tf_op jit(solution)/shard_map/cond/branch_0_fun/ppermute | solution.py:370
  136.6 2.4 %collective-permute-done.20.refs_5_ = bf16[4,56,384]{2,1,0:T(8,128)(2,1)S(1)} collective-permute-done((bf16[4,56,384]{2,1,0:T(8,128)(2,1)S(1)}, bf16[4,56,384]{2,1,0:T(8,128)(2,1)S(1)}, u32[]{:S(2)}, u32[]{:S(2)}) %collective-permute-start.20) | collective-permute-done | bytes 172064 | tf_op jit(solution)/shard_map/cond/branch_0_fun/ppermute | solution.py:370
  140.8 9.0 %down.3 = f32[256,320]{1,0:T(8,128)} custom-call(s32[1]{0:T(128)} %get-tuple-element.68.me_s, s32[16]{0:T(128)S(1)} %get-tuple-element.70.base_s, bf16[4,56,384]{2,1,0:T(8,128)(2,1)S(1)} %pad_maximum_fusion.1.refs_0_, bf16[4,56,384]{2,1,0:T(8,128)(2,1)S(1)} %collective-permute-done.8.refs_1_, bf16[4,56,384]{2,1,0:T(8,128)(2,1)S(1)} %pad_maximum_fusion.2.refs_2_, ...), custom_call_target="tpu_custom_call" | custom-call | tf_op jit(solution)/shard_map/cond/branch_0_fun/down/pallas_call | solution.py:446
  150.0 11.0 %all_to_all.15 = f32[4,64,320]{2,1,0:T(8,128)S(1)} all-to-all(f32[4,64,320]{2,1,0:T(8,128)} %bitcast.37), channel_id=1, replica_groups=mesh['gx'=4,'gy'=8] {'gx'}, dimensions={0} | all-to-all | bytes 655360 | tf_op jit(solution)/shard_map/all_to_all | solution.py:604
  (132 shorter events, 39.4 us)
Async XLA Ops:
  8.9 18.0 %all-to-all-start = ((bf16[8,8,2688]{2,1,0:T(8,128)(2,1)}), bf16[8,8,2688]{2,1,0:T(8,128)(2,1)S(1)}, u32[]{:S(2)}, u32[]{:S(2)}) async-start(bf16[8,8,2688]{2,1,0:T(8,128)(2,1)} %attend.1), calls=%async_computation | async-start | bytes 688128 | tf_op jit(solution)/shard_map/all_to_all | solution.py:568
  28.2 13.2 %all-to-all-start.1 = ((bf16[8,8,2560]{2,1,0:T(8,128)(2,1)}), bf16[8,8,2560]{2,1,0:T(8,128)(2,1)S(1)}, u32[]{:S(2)}, u32[]{:S(2)}) async-start(bf16[8,8,2560]{2,1,0:T(8,128)(2,1)} %broadcast_in_dim.146), calls=%async_computation.1 | async-start | bytes 655360 | tf_op jit(solution)/shard_map/all_to_all | solution.py:574
  54.3 33.6 %collective-permute-start.15 = (bf16[4,56,768]{2,1,0:T(8,128)(2,1)S(1)}, bf16[4,56,768]{2,1,0:T(8,128)(2,1)}, u32[]{:S(2)}, u32[]{:S(2)}) collective-permute-start(bf16[4,56,768]{2,1,0:T(8,128)(2,1)S(1)} %get-tuple-element.81), channel_id=1, source_target_pairs={{0,1},{1,0},{2,3},{3,2},{4,5},{5,4},{6,7},{7,6},{8,9},{9,8},{10,11... | collective-permute-start | bytes 1032200 | tf_op jit(solution)/shard_map/cond/branch_0_fun/ppermute | solution.py:370
  60.6 29.5 %collective-permute-start = (bf16[4,56,768]{2,1,0:T(8,128)(2,1)S(1)}, bf16[4,56,768]{2,1,0:T(8,128)(2,1)}, u32[]{:S(2)}, u32[]{:S(2)}) collective-permute-start(bf16[4,56,768]{2,1,0:T(8,128)(2,1)S(1)} %get-tuple-element.74), channel_id=1, source_target_pairs={{0,1},{1,0},{2,3},{3,2},{4,5},{5,4},{6,7},{7,6},{8,9},{9,8},{10,11... | collective-permute-start | bytes 1032200 | tf_op jit(solution)/shard_map/cond/branch_0_fun/ppermute | solution.py:370
  66.0 26.3 %collective-permute-start.9 = (bf16[4,56,768]{2,1,0:T(8,128)(2,1)S(1)}, bf16[4,56,768]{2,1,0:T(8,128)(2,1)}, u32[]{:S(2)}, u32[]{:S(2)}) collective-permute-start(bf16[4,56,768]{2,1,0:T(8,128)(2,1)S(1)} %get-tuple-element.79), channel_id=1, source_target_pairs={{0,2},{1,3},{2,0},{3,1},{4,6},{5,7},{6,4},{7,5},{8,10},{9,11},{10,... | collective-permute-start | bytes 1032200 | tf_op jit(solution)/shard_map/cond/branch_0_fun/ppermute | solution.py:370
  67.1 7.3 %collective-permute-start.3 = (f32[2,128]{1,0:T(2,128)S(1)}, f32[2,128]{1,0:T(2,128)S(1)}, u32[]{:S(2)}, u32[]{:S(2)}) collective-permute-start(f32[2,128]{1,0:T(2,128)S(1)} %get-tuple-element.77), channel_id=1, source_target_pairs={{0,1},{1,0},{2,3},{3,2},{4,5},{5,4},{6,7},{7,6},{8,9},{9,8},{10,11... | collective-permute-start | bytes 3080 | tf_op jit(solution)/shard_map/cond/branch_0_fun/ppermute | solution.py:370
  72.4 22.1 %collective-permute-start.21 = (bf16[4,56,768]{2,1,0:T(8,128)(2,1)S(1)}, bf16[4,56,768]{2,1,0:T(8,128)(2,1)}, u32[]{:S(2)}, u32[]{:S(2)}) collective-permute-start(bf16[4,56,768]{2,1,0:T(8,128)(2,1)S(1)} %get-tuple-element.83), channel_id=1, source_target_pairs={{0,2},{1,3},{2,0},{3,1},{4,6},{5,7},{6,4},{7,5},{8,10},{9,11},{10,... | collective-permute-start | bytes 1032200 | tf_op jit(solution)/shard_map/cond/branch_0_fun/ppermute | solution.py:370
  74.5 8.9 %collective-permute-start.4 = (f32[2,128]{1,0:T(2,128)S(1)}, f32[2,128]{1,0:T(2,128)S(1)}, u32[]{:S(2)}, u32[]{:S(2)}) collective-permute-start(f32[2,128]{1,0:T(2,128)S(1)} %add.197), channel_id=1, source_target_pairs={{0,2},{1,3},{2,0},{3,1},{4,6},{5,7},{6,4},{7,5},{8,10},{9,11},{10,... | collective-permute-start | bytes 3080 | tf_op jit(solution)/shard_map/cond/branch_0_fun/ppermute | solution.py:370
  89.0 8.6 %collective-permute-start.16 = (bf16[2,56,768]{2,1,0:T(8,128)(2,1)S(1)}, bf16[2,56,768]{2,1,0:T(8,128)(2,1)S(1)}, u32[]{:S(2)}, u32[]{:S(2)}) collective-permute-start(bf16[2,56,768]{2,1,0:T(8,128)(2,1)S(1)} %pad_maximum_fusion.3), channel_id=1, source_target_pairs={{0,2},{1,3},{2,0},{3,1},{4,6},{5,7},{6,4},{7,5},{8,10},{9,11},{10,... | collective-permute-start | bytes 516104 | tf_op jit(solution)/shard_map/cond/branch_0_fun/ppermute | solution.py:370
  91.3 9.0 %collective-permute-start.1 = (bf16[2,56,768]{2,1,0:T(8,128)(2,1)S(1)}, bf16[2,56,768]{2,1,0:T(8,128)(2,1)S(1)}, u32[]{:S(2)}, u32[]{:S(2)}) collective-permute-start(bf16[2,56,768]{2,1,0:T(8,128)(2,1)S(1)} %pad_maximum_fusion), channel_id=1, source_target_pairs={{0,2},{1,3},{2,0},{3,1},{4,6},{5,7},{6,4},{7,5},{8,10},{9,11},{10,... | collective-permute-start | bytes 516104 | tf_op jit(solution)/shard_map/cond/branch_0_fun/ppermute | solution.py:370
  93.4 17.7 %collective-permute-start.10 = (bf16[2,56,768]{2,1,0:T(8,128)(2,1)S(1)}, bf16[2,56,768]{2,1,0:T(8,128)(2,1)S(1)}, u32[]{:S(2)}, u32[]{:S(2)}) collective-permute-start(bf16[2,56,768]{2,1,0:T(8,128)(2,1)S(1)} %stack.103), channel_id=1, source_target_pairs={{0,4},{1,5},{2,6},{3,7},{4,0},{5,1},{6,2},{7,3},{8,12},{9,13},{10,... | collective-permute-start | bytes 516104 | tf_op jit(solution)/shard_map/cond/branch_0_fun/ppermute | solution.py:370
  95.6 18.8 %collective-permute-start.22 = (bf16[2,56,768]{2,1,0:T(8,128)(2,1)S(1)}, bf16[2,56,768]{2,1,0:T(8,128)(2,1)S(1)}, u32[]{:S(2)}, u32[]{:S(2)}) collective-permute-start(bf16[2,56,768]{2,1,0:T(8,128)(2,1)S(1)} %stack.102), channel_id=1, source_target_pairs={{0,4},{1,5},{2,6},{3,7},{4,0},{5,1},{6,2},{7,3},{8,12},{9,13},{10,... | collective-permute-start | bytes 516104 | tf_op jit(solution)/shard_map/cond/branch_0_fun/ppermute | solution.py:370
  97.7 18.4 %collective-permute-start.17 = (bf16[1,56,768]{2,1,0:T(8,128)(2,1)S(1)}, bf16[1,56,768]{2,1,0:T(8,128)(2,1)S(1)}, u32[]{:S(2)}, u32[]{:S(2)}) collective-permute-start(bf16[1,56,768]{2,1,0:T(8,128)(2,1)S(1)} %slice.551), channel_id=1, source_target_pairs={{0,4},{1,5},{2,6},{3,7},{4,0},{5,1},{6,2},{7,3},{8,12},{9,13},{10,... | collective-permute-start | bytes 258056 | tf_op jit(solution)/shard_map/cond/branch_0_fun/ppermute | solution.py:370
  100.4 15.9 %collective-permute-start.2 = (bf16[1,56,768]{2,1,0:T(8,128)(2,1)S(1)}, bf16[1,56,768]{2,1,0:T(8,128)(2,1)S(1)}, u32[]{:S(2)}, u32[]{:S(2)}) collective-permute-start(bf16[1,56,768]{2,1,0:T(8,128)(2,1)S(1)} %slice.553), channel_id=1, source_target_pairs={{0,4},{1,5},{2,6},{3,7},{4,0},{5,1},{6,2},{7,3},{8,12},{9,13},{10,... | collective-permute-start | bytes 258056 | tf_op jit(solution)/shard_map/cond/branch_0_fun/ppermute | solution.py:370
  120.9 5.7 %collective-permute-start.18 = (bf16[1,56,384]{2,1,0:T(8,128)(2,1)S(1)}, bf16[1,56,384]{2,1,0:T(8,128)(2,1)S(1)}, u32[]{:S(2)}, u32[]{:S(2)}) collective-permute-start(bf16[1,56,384]{2,1,0:T(8,128)(2,1)S(1)} %get-tuple-element.207), channel_id=1, source_target_pairs={{0,4},{1,5},{2,6},{3,7},{4,0},{5,1},{6,2},{7,3},{8,12},{9,13},{10,... | collective-permute-start | bytes 129032 | tf_op jit(solution)/shard_map/cond/branch_0_fun/ppermute | solution.py:370
  120.9 6.1 %collective-permute-start.12 = (bf16[1,56,384]{2,1,0:T(8,128)(2,1)S(1)}, bf16[1,56,384]{2,1,0:T(8,128)(2,1)S(1)}, u32[]{:S(2)}, u32[]{:S(2)}) collective-permute-start(bf16[1,56,384]{2,1,0:T(8,128)(2,1)S(1)} %get-tuple-element.208), channel_id=1, source_target_pairs={{0,1},{1,0},{2,3},{3,2},{4,5},{5,4},{6,7},{7,6},{8,9},{9,8},{10,11... | collective-permute-start | bytes 129032 | tf_op jit(solution)/shard_map/cond/branch_0_fun/ppermute | solution.py:370
  121.8 7.2 %collective-permute-start.6 = (bf16[1,56,384]{2,1,0:T(8,128)(2,1)S(1)}, bf16[1,56,384]{2,1,0:T(8,128)(2,1)S(1)}, u32[]{:S(2)}, u32[]{:S(2)}) collective-permute-start(bf16[1,56,384]{2,1,0:T(8,128)(2,1)S(1)} %get-tuple-element.206), channel_id=1, source_target_pairs={{0,4},{1,5},{2,6},{3,7},{4,0},{5,1},{6,2},{7,3},{8,12},{9,13},{10,... | collective-permute-start | bytes 129032 | tf_op jit(solution)/shard_map/cond/branch_0_fun/ppermute | solution.py:370
  124.8 5.9 %collective-permute-start.25 = (bf16[2,56,384]{2,1,0:T(8,128)(2,1)S(1)}, bf16[2,56,384]{2,1,0:T(8,128)(2,1)S(1)}, u32[]{:S(2)}, u32[]{:S(2)}) collective-permute-start(bf16[2,56,384]{2,1,0:T(8,128)(2,1)S(1)} %pad_maximum_fusion.9), channel_id=1, source_target_pairs={{0,4},{1,5},{2,6},{3,7},{4,0},{5,1},{6,2},{7,3},{8,12},{9,13},{10,... | collective-permute-start | bytes 258056 | tf_op jit(solution)/shard_map/cond/branch_0_fun/ppermute | solution.py:370
  126.6 6.9 %collective-permute-start.19 = (bf16[2,56,384]{2,1,0:T(8,128)(2,1)S(1)}, bf16[2,56,384]{2,1,0:T(8,128)(2,1)S(1)}, u32[]{:S(2)}, u32[]{:S(2)}) collective-permute-start(bf16[2,56,384]{2,1,0:T(8,128)(2,1)S(1)} %pad_maximum_fusion.8), channel_id=1, source_target_pairs={{0,2},{1,3},{2,0},{3,1},{4,6},{5,7},{6,4},{7,5},{8,10},{9,11},{10,... | collective-permute-start | bytes 258056 | tf_op jit(solution)/shard_map/cond/branch_0_fun/ppermute | solution.py:370
  127.0 7.8 %collective-permute-start.13 = (bf16[2,56,384]{2,1,0:T(8,128)(2,1)S(1)}, bf16[2,56,384]{2,1,0:T(8,128)(2,1)S(1)}, u32[]{:S(2)}, u32[]{:S(2)}) collective-permute-start(bf16[2,56,384]{2,1,0:T(8,128)(2,1)S(1)} %pad_maximum_fusion.7), channel_id=1, source_target_pairs={{0,4},{1,5},{2,6},{3,7},{4,0},{5,1},{6,2},{7,3},{8,12},{9,13},{10,... | collective-permute-start | bytes 258056 | tf_op jit(solution)/shard_map/cond/branch_0_fun/ppermute | solution.py:370
  129.1 5.9 %collective-permute-start.7 = (bf16[2,56,384]{2,1,0:T(8,128)(2,1)S(1)}, bf16[2,56,384]{2,1,0:T(8,128)(2,1)S(1)}, u32[]{:S(2)}, u32[]{:S(2)}) collective-permute-start(bf16[2,56,384]{2,1,0:T(8,128)(2,1)S(1)} %pad_maximum_fusion.6), channel_id=1, source_target_pairs={{0,2},{1,3},{2,0},{3,1},{4,6},{5,7},{6,4},{7,5},{8,10},{9,11},{10,... | collective-permute-start | bytes 258056 | tf_op jit(solution)/shard_map/cond/branch_0_fun/ppermute | solution.py:370
  130.7 5.9 %collective-permute-start.26 = (bf16[4,56,384]{2,1,0:T(8,128)(2,1)S(1)}, bf16[4,56,384]{2,1,0:T(8,128)(2,1)S(1)}, u32[]{:S(2)}, u32[]{:S(2)}) collective-permute-start(bf16[4,56,384]{2,1,0:T(8,128)(2,1)S(1)} %pad_maximum_fusion.5.refs_6_), channel_id=1, source_target_pairs={{0,2},{1,3},{2,0},{3,1},{4,6},{5,7},{6,4},{7,5},{8,10},{9,11},{10,... | collective-permute-start | bytes 516104 | tf_op jit(solution)/shard_map/cond/branch_0_fun/ppermute | solution.py:370
  133.5 5.5 %collective-permute-start.20 = (bf16[4,56,384]{2,1,0:T(8,128)(2,1)S(1)}, bf16[4,56,384]{2,1,0:T(8,128)(2,1)S(1)}, u32[]{:S(2)}, u32[]{:S(2)}) collective-permute-start(bf16[4,56,384]{2,1,0:T(8,128)(2,1)S(1)} %pad_maximum_fusion.4.refs_4_), channel_id=1, source_target_pairs={{0,1},{1,0},{2,3},{3,2},{4,5},{5,4},{6,7},{7,6},{8,9},{9,8},{10,11... | collective-permute-start | bytes 516104 | tf_op jit(solution)/shard_map/cond/branch_0_fun/ppermute | solution.py:370
  135.0 5.8 %collective-permute-start.8 = (bf16[4,56,384]{2,1,0:T(8,128)(2,1)S(1)}, bf16[4,56,384]{2,1,0:T(8,128)(2,1)S(1)}, u32[]{:S(2)}, u32[]{:S(2)}) collective-permute-start(bf16[4,56,384]{2,1,0:T(8,128)(2,1)S(1)} %pad_maximum_fusion.1.refs_0_), channel_id=1, source_target_pairs={{0,1},{1,0},{2,3},{3,2},{4,5},{5,4},{6,7},{7,6},{8,9},{9,8},{10,11... | collective-permute-start | bytes 516104 | tf_op jit(solution)/shard_map/cond/branch_0_fun/ppermute | solution.py:370
  (14 other events, 164.1 us)

commit v2 on v1

--- a/solution.py
+++ b/solution.py
@@ -291,7 +291,7 @@
     )(hidden_all, gain.reshape(1, -1), rank_t)
 
 
-def gate_up_kernel(bit, chunk, me_s, base_s, x_ref, w_hbm, keep_ref, send_ref, scr, buf, sem):
+def gate_up_kernel(names, bit, chunk, me_s, base_s, x_ref, w_hbm, keep_ref, send_ref, scr, buf, sem):
     experts, slots, _ = x_ref.shape
     units = buf.shape[3]
     hidden_units = units * CHUNKS
@@ -328,22 +328,21 @@
         return carry
 
     lax.fori_loop(0, experts // unroll, visit, 0)
-    half, each, _ = keep_ref.shape
+    each = keep_ref.shape[1]
     me = me_s[0]
-    for i in range(half):
-        other = (i // bit) * 2 * bit + i % bit
-        at = jnp.bitwise_xor(me, other) * each
+    for i, name in enumerate(names):
+        at = jnp.bitwise_xor(me, name) * each
         keep_ref[i] = scr[pl.ds(pl.multiple_of(at, ALIGN), each), :].astype(bf16)
-        at = jnp.bitwise_xor(me, other + bit) * each
+        at = jnp.bitwise_xor(me, name ^ bit) * each
         send_ref[i] = scr[pl.ds(pl.multiple_of(at, ALIGN), each), :].astype(bf16)
 
 
-def gate_up(x, w_gate_up, base, me, capacity, parts, chunk, bit):
+def gate_up(x, w_gate_up, base, me, capacity, parts, chunk, names, bit):
     experts, slots, features = x.shape
     units = w_gate_up.shape[2] // (2 * CHUNKS)
     out = jax.ShapeDtypeStruct((parts // 2, capacity // parts, 2 * units), bf16)
     return pl.pallas_call(
-        functools.partial(gate_up_kernel, bit, chunk),
+        functools.partial(gate_up_kernel, names, bit, chunk),
         out_shape=(out, out),
         grid_spec=pltpu.PrefetchScalarGridSpec(
             num_scalar_prefetch=2,
@@ -370,41 +369,15 @@
     return lax.ppermute(x, "gy", [(i, i ^ k) for i in range(parts)])
 
 
-def scatter_sums(keep, send, order, parts):
-    names = [k for k in range(parts) if not k & order[0]]
-    total = keep.astype(f32) + exchange(send, order[0], parts).astype(f32)
-    for k in order[1:]:
-        kept = [i for i, n in enumerate(names) if not n & k]
-        sent = [i for i, n in enumerate(names) if n & k]
-        rest = jnp.stack([total[i] for i in sent]).astype(bf16)
-        total = jnp.stack([total[i] for i in kept]) + exchange(rest, k, parts).astype(f32)
-        names = [names[i] for i in kept]
-    return total[0]
-
-
-def gather_rows(x, order, parts):
-    names = [0]
-    x = x[None]
-    for k in order[:-1]:
-        x = jnp.concatenate([x, exchange(x, k, parts)], axis=0)
-        names = names + [n ^ k for n in names]
-    return x, exchange(x, order[-1], parts), names, [n ^ order[-1] for n in names]
-
-
 def down_kernel(names, me_s, base_s, *refs):
     acts = refs[: len(names)]
-    high_ref, low_ref, w_hbm, out_ref, scr, rows_scr, buf, sem = refs[len(names) :]
-    experts = buf.shape[0]
+    high_ref, low_ref, w_ref, out_ref, scr, rows_scr = refs[len(names) :]
+    experts = w_ref.shape[0]
     each = acts[0].shape[1]
     capacity = 2 * acts[0].shape[0] * each
     slots = scr.shape[0] - capacity
     me = me_s[0]
 
-    def fetch(e):
-        return pltpu.make_async_copy(w_hbm.at[e], buf.at[e], sem.at[e])
-
-    for e in range(experts):
-        fetch(e).start()
     scr[capacity:, :] = jnp.zeros((slots, scr.shape[1]), f32)
     for a, (ref, ns) in enumerate(zip(acts, names)):
         units = ref.shape[2]
@@ -416,12 +389,10 @@
 
     def visit(step, carry):
         these = [step * unroll + i for i in range(unroll)]
-        for e in these:
-            fetch(e).wait()
         products = [
             lax.dot_general(
                 scr[pl.ds(pl.multiple_of(base_s[e], ALIGN), slots), :].astype(bf16),
-                buf[e],
+                w_ref[e],
                 (((1,), (1,)), ((), ())),
                 preferred_element_type=f32,
             ).astype(bf16)
@@ -450,13 +421,11 @@
             num_scalar_prefetch=2,
             grid=(1,),
             in_specs=[whole(a.shape) for a in acts]
-            + [whole(high.shape), whole(low.shape), pl.BlockSpec(memory_space=pltpu.HBM)],
+            + [whole(high.shape), whole(low.shape), pl.BlockSpec(memory_space=pltpu.VMEM)],
             out_specs=whole((total, features)),
             scratch_shapes=[
                 pltpu.VMEM((capacity + slots, hidden_units), f32),
                 pltpu.VMEM((experts * slots, features), bf16),
-                pltpu.VMEM(w_down_t.shape, bf16),
-                pltpu.SemaphoreType.DMA((experts,)),
             ],
         ),
         compiler_params=params(26),
@@ -492,35 +461,82 @@
     )(rank, weight)
 
 
-def sum_over_gy(x, parts):
-    k = 1
-    while k < parts:
-        x = x + exchange(x, k, parts)
-        k *= 2
-    return x
-
-
 def experts_part(capacity, x, square, w_gate_up, w_down_t, base, place, high, low, me, parts):
     units = w_down_t.shape[2] // CHUNKS
     rows = capacity // parts
     here = me[0] * rows + lax.iota(jnp.int32, rows)
     mine = jnp.any(place[None] == here[:, None, None], axis=2)
     bits = [1 << i for i in range(parts.bit_length() - 1)]
-    acts, names = [], []
-    scale = None
-    for chunk in range(CHUNKS):
-        order = bits if chunk % 2 == 0 else bits[1:] + bits[:1]
-        keep, send = gate_up(x, w_gate_up, base, me, capacity, parts, chunk, order[0])
-        both = scatter_sums(keep, send, order, parts)
-        if scale is None:
-            inv = lax.rsqrt(sum_over_gy(square, parts).reshape(-1) / D + EPSILON)
-            scale = jnp.sum(jnp.where(mine, inv[None, :], 0.0), axis=1)[:, None]
+    last_token = [me]
+    squares = [square]
+    chunks = [dict() for _ in range(CHUNKS)]
+
+    def after(*values):
+        return lax.optimization_barrier((*values, last_token[0]))[:-1]
+
+    def send(value, k):
+        last_token[0] = value
+        return exchange(value, k, parts)
+
+    def add_squares():
+        done = len(squares) - 1
+        if done < len(bits):
+            (value,) = after(squares[-1])
+            squares.append(value + send(value, bits[done]))
+
+    places = [0]
+    for k in bits[:0:-1]:
+        places = places + [n ^ k for n in places]
+
+    def start(chunk, state):
+        (ordered,) = after(base)
+        keep, away = gate_up(
+            x, w_gate_up, ordered, me, capacity, parts, chunk, places, bits[0]
+        )
+        state.update(total=keep, got=send(away, bits[0]))
+        add_squares()
+
+    def fold(k):
+        def run(chunk, state):
+            total, got = after(state["total"], state["got"])
+            half = got.shape[0] // 2
+            rest = (total[half:].astype(f32) + got[half:].astype(f32)).astype(bf16)
+            state.update(
+                total=total[:half].astype(f32) + got[:half].astype(f32), got=send(rest, k)
+            )
+
+        return run
+
+    def activate(chunk, state):
+        while len(squares) <= len(bits):
+            add_squares()
+        total, got = after(state["total"], state["got"])
+        inv = lax.rsqrt(squares[-1].reshape(-1) / D + EPSILON)
+        scale = jnp.sum(jnp.where(mine, inv[None, :], 0.0), axis=1)[:, None]
+        both = total[0].astype(f32) + got[0].astype(f32)
         gate = both[:, :units] * scale
         up = both[:, units:] * scale
-        act = (jax.nn.silu(gate) * up).astype(bf16)
-        left, right, left_names, right_names = gather_rows(act, order[::-1], parts)
-        acts += [left, right]
-        names += [left_names, right_names]
+        act = (jax.nn.silu(gate) * up).astype(bf16)[None]
+        state.update(left=act, right=send(act, bits[-1]), names=[0], last=bits[-1])
+
+    def spread(k):
+        def run(chunk, state):
+            left, right = after(state["left"], state["right"])
+            both = jnp.concatenate([left, right], axis=0)
+            names = state["names"] + [n ^ state["last"] for n in state["names"]]
+            state.update(left=both, right=send(both, k), names=names, last=k)
+
+        return run
+
+    stages = [start] + [fold(k) for k in bits[1:]] + [activate] + [spread(k) for k in bits[-2::-1]]
+    for slot in range(CHUNKS + len(stages) - 1):
+        for i, stage in enumerate(stages):
+            if 0 <= slot - i < CHUNKS:
+                stage(slot - i, chunks[slot - i])
+    acts, names = [], []
+    for state in chunks:
+        acts += [state["left"], state["right"]]
+        names += [state["names"], [n ^ state["last"] for n in state["names"]]]
     return down(acts, names, w_down_t, base, me, high, low)
 
 

time: 163 us -> 148 us (0.908); the launches traced: 162 us -> 149 us
  waiting for transfers between devices: 51.3 us -> 34.7 us
  starting transfers between devices: 40.3 us -> 48.3 us
  other arithmetic: 7.85 us -> 5.38 us
    ppermute x27, waiting for transfers between devices: 38.1 us -> 21 us  [exchange(): return lax.ppermute(x, 'gy', [(i, i ^ k) for i in range(parts)])]
    ppermute x27, starting transfers between devices: 28.3 us -> 36.3 us  [exchange(): return lax.ppermute(x, 'gy', [(i, i ^ k) for i in range(parts)])]
    another operation x4 -> x0, other arithmetic: 2.18 us -> none
  transfers between devices with their start and end apart: 29 -> 29, of which waited for: 16 -> 13; matrix products, arithmetic and copies ran while one was open for 5% -> 4% of each run, Pallas kernels for 10% -> 11%
where the time goes in v2:
time: 148 us; the launch traced here: 149 us
  starting transfers between devices  48.3 us (33%)
  Pallas kernels  39.2 us (26%)
  waiting for transfers between devices  34.7 us (23%)
  blocking collectives  16.6 us (11%)
  other arithmetic  5.38 us (4%)
  local copies, waits for them, and re-layouts  2.23 us (2%)
  between operations  1.49 us (1%)
    ppermute x27, starting transfers between devices, exchange(): return lax.ppermute(x, 'gy', [(i, i ^ k) for i in range(parts)])  36.3 us
    ppermute x27, waiting for transfers between devices, exchange(): return lax.ppermute(x, 'gy', [(i, i ^ k) for i in range(parts)])  21 us
    pallas_call x4, Pallas kernels, gate_up(): pl.pallas_call(functools.partial(gate_up_kernel, names, bit, chunk), out_...  19.4 us
    all_to_all x1, blocking collectives, shards(): routed = lax.all_to_all(routed.reshape(num_gx, rows, -1), 'gx', 0, 0)  11 us
    pallas_call x1, Pallas kernels, attend_local(): pl.pallas_call(attend_kernel, out_shape=out, grid_spec=pltpu.PrefetchScal...  8.83 us
    all_to_all x1, starting transfers between devices, shards(): part = lax.all_to_all(part, 'gy', 0, 0)  8.37 us
    all_to_all x1, waiting for transfers between devices, shards(): part = lax.all_to_all(part, 'gy', 0, 0)  7.68 us
    pallas_call x1, Pallas kernels, down(): pl.pallas_call(functools.partial(down_kernel, names), out_shape=jax.Shape...  7.57 us
  transfers between devices with their start and end apart: 29, of which 13 were waited for; matrix products, arithmetic and copies ran while one was open for 4% of the time, Pallas kernels for 11%

profile of v2, /device:TPU:0, one launch (start us, length us, event | category | flops | bytes accessed | tf_op | source)
XLA Modules:
  0.0 149.1 jit_solution(10858443930989394999)
XLA Ops:
  0.0 8.8 %attend.1 = bf16[8,8,2688]{2,1,0:T(8,128)(2,1)} custom-call(s32[4096]{0:T(1024)} %bitcast.86, bf16[64,2560]{1,0:T(8,128)(2,1)} %q_ref.1, s32[1,4096]{1,0:T(1,128)} %own_ref.1, bf16[1,4096,512]{2,1,0:T(8,128)(2,1)} %k_hbm.1, bf16[1,4096,512]{2,1,0:T(8,128)(2,1)} %v_hbm.1), custom_call_target="tpu_custom_call" | custom-call | tf_op jit(solution)/shard_map/attend/pallas_call | solution.py:160
  8.9 8.4 %all-to-all-start = ((bf16[8,8,2688]{2,1,0:T(8,128)(2,1)}), bf16[8,8,2688]{2,1,0:T(8,128)(2,1)S(1)}, u32[]{:S(2)}, u32[]{:S(2)}) async-start(bf16[8,8,2688]{2,1,0:T(8,128)(2,1)} %attend.1), calls=%async_computation | async-start | bytes 688128 | tf_op jit(solution)/shard_map/all_to_all | solution.py:584
  19.1 7.7 %all-to-all-done.part_ref = bf16[8,8,2688]{2,1,0:T(8,128)(2,1)S(1)} async-done(((bf16[8,8,2688]{2,1,0:T(8,128)(2,1)}), bf16[8,8,2688]{2,1,0:T(8,128)(2,1)S(1)}, u32[]{:S(2)}, u32[]{:S(2)}) %all-to-all-start) | async-done | bytes 344096 | tf_op jit(solution)/shard_map/all_to_all | solution.py:584
  28.1 3.6 %all-to-all-start.1 = ((bf16[8,8,2560]{2,1,0:T(8,128)(2,1)}), bf16[8,8,2560]{2,1,0:T(8,128)(2,1)S(1)}, u32[]{:S(2)}, u32[]{:S(2)}) async-start(bf16[8,8,2560]{2,1,0:T(8,128)(2,1)} %broadcast_in_dim.200), calls=%async_computation.1 | async-start | bytes 655360 | tf_op jit(solution)/shard_map/all_to_all | solution.py:590
  35.3 6.0 %all-to-all-done.1 = bf16[8,8,2560]{2,1,0:T(8,128)(2,1)S(1)} async-done(((bf16[8,8,2560]{2,1,0:T(8,128)(2,1)}), bf16[8,8,2560]{2,1,0:T(8,128)(2,1)S(1)}, u32[]{:S(2)}, u32[]{:S(2)}) %all-to-all-start.1) | async-done | bytes 327712 | tf_op jit(solution)/shard_map/all_to_all | solution.py:590
  41.9 5.6 %all_gather.3.h_ref = bf16[256,320]{1,0:T(8,128)(2,1)S(1)} all-gather(bf16[64,320]{1,0:T(8,128)(2,1)S(1)} %project.1), channel_id=1, replica_groups=mesh['gx'=4,'gy'=8] {'gx'}, dimensions={0}, use_global_device_ids=true | all-gather | bytes 204800 | tf_op jit(solution)/shard_map/all_gather | solution.py:594
  48.4 88.9 %conditional.1 = (f32[256,320]{1,0:T(8,128)}) conditional(s32[]{:T(128)} %clamp.3, (s32[16]{0:T(128)S(1)}, s32[1]{0:T(128)}, bf16[16,64,320]{2,1,0:T(8,128)(2,1)S(1)}, bf16[16,320,3072]{2,1,0:T(8,128)(2,1)}, f32[2,128]{1,0:T(2,128)S(1)}, /*index=5*/s32[256,16]{1,0:T(8,128)S(1)}, s32[]{:T(128)}, bf16[256,1024]{1,0:T(8,128)(2,1)S(1)}, ...), branch_computations={%region_9.12_spmd, %region_12.15_spmd, %region_15.18_spmd} | conditional | flops 2021451008 | bytes 136079232 | solution.py:615
  48.7 4.8 %gate_up.16 = (bf16[4,64,768]{2,1,0:T(8,128)(2,1)S(1)}, bf16[4,64,768]{2,1,0:T(8,128)(2,1)S(1)}) custom-call(s32[1]{0:T(128)} %get-tuple-element.134.me_s, s32[16]{0:T(128)S(1)} %get-tuple-element.157.base_s, bf16[16,64,320]{2,1,0:T(8,128)(2,1)S(1)} %get-tuple-element.137.x_ref, bf16[16,320,3072]{2,1,0:T(8,128)(2,1)} %get-tuple-element.138.w_hbm), custom_call_target="tpu_custom_call" | custom-call | flops 503316480 | bytes 8650752 | tf_op jit(solution)/shard_map/cond/branch_1_fun/gate_up/pallas_call | solution.py:344
  55.6 4.8 %gate_up.17 = (bf16[4,64,768]{2,1,0:T(8,128)(2,1)S(1)}, bf16[4,64,768]{2,1,0:T(8,128)(2,1)S(1)}) custom-call(s32[1]{0:T(128)} %get-tuple-element.134.me_s, s32[16]{0:T(128)S(1)} %get-tuple-element.157.base_s, bf16[16,64,320]{2,1,0:T(8,128)(2,1)S(1)} %get-tuple-element.137.x_ref, bf16[16,320,3072]{2,1,0:T(8,128)(2,1)} %get-tuple-element.138.w_hbm), custom_call_target="tpu_custom_call" | custom-call | flops 503316480 | bytes 8650752 | tf_op jit(solution)/shard_map/cond/branch_1_fun/gate_up/pallas_call | solution.py:344
  62.0 3.6 %collective-permute-done.28 = f32[2,128]{1,0:T(2,128)S(1)} collective-permute-done((f32[2,128]{1,0:T(2,128)S(1)}, f32[2,128]{1,0:T(2,128)S(1)}, u32[]{:S(2)}, u32[]{:S(2)}) %collective-permute-start.28) | collective-permute-done | bytes 1056 | tf_op jit(solution)/shard_map/cond/branch_1_fun/ppermute | solution.py:369
  66.9 2.2 %collective-permute-done.31 = f32[2,128]{1,0:T(2,128)S(1)} collective-permute-done((f32[2,128]{1,0:T(2,128)S(1)}, f32[2,128]{1,0:T(2,128)S(1)}, u32[]{:S(2)}, u32[]{:S(2)}) %collective-permute-start.31) | collective-permute-done | bytes 1056 | tf_op jit(solution)/shard_map/cond/branch_1_fun/ppermute | solution.py:369
  71.4 4.8 %gate_up.18 = (bf16[4,64,768]{2,1,0:T(8,128)(2,1)S(1)}, bf16[4,64,768]{2,1,0:T(8,128)(2,1)S(1)}) custom-call(s32[1]{0:T(128)} %get-tuple-element.134.me_s, s32[16]{0:T(128)S(1)} %get-tuple-element.157.base_s, bf16[16,64,320]{2,1,0:T(8,128)(2,1)S(1)} %get-tuple-element.137.x_ref, bf16[16,320,3072]{2,1,0:T(8,128)(2,1)} %get-tuple-element.138.w_hbm), custom_call_target="tpu_custom_call" | custom-call | flops 503316480 | bytes 8650752 | tf_op jit(solution)/shard_map/cond/branch_1_fun/gate_up/pallas_call | solution.py:344
  81.4 2.1 %collective-permute-start.32 = (bf16[1,64,768]{2,1,0:T(8,128)(2,1)S(1)}, bf16[1,64,768]{2,1,0:T(8,128)(2,1)S(1)}, u32[]{:S(2)}, u32[]{:S(2)}) collective-permute-start(bf16[1,64,768]{2,1,0:T(8,128)(2,1)S(1)} %get-tuple-element.364), channel_id=1, source_target_pairs={{0,4},{1,5},{2,6},{3,7},{4,0},{5,1},{6,2},{7,3},{8,12},{9,13},{10,... | collective-permute-start | bytes 294920 | tf_op jit(solution)/shard_map/cond/branch_1_fun/ppermute | solution.py:369
  83.4 5.0 %gate_up.19 = (bf16[4,64,768]{2,1,0:T(8,128)(2,1)S(1)}, bf16[4,64,768]{2,1,0:T(8,128)(2,1)S(1)}) custom-call(s32[1]{0:T(128)} %get-tuple-element.134.me_s, s32[16]{0:T(128)S(1)} %get-tuple-element.157.base_s, bf16[16,64,320]{2,1,0:T(8,128)(2,1)S(1)} %get-tuple-element.137.x_ref, bf16[16,320,3072]{2,1,0:T(8,128)(2,1)} %get-tuple-element.138.w_hbm), custom_call_target="tpu_custom_call" | custom-call | flops 503316480 | bytes 8650752 | tf_op jit(solution)/shard_map/cond/branch_1_fun/gate_up/pallas_call | solution.py:344
  90.3 2.0 %collective-permute-start.37 = (bf16[1,64,768]{2,1,0:T(8,128)(2,1)S(1)}, bf16[1,64,768]{2,1,0:T(8,128)(2,1)S(1)}, u32[]{:S(2)}, u32[]{:S(2)}) collective-permute-start(bf16[1,64,768]{2,1,0:T(8,128)(2,1)S(1)} %get-tuple-element.363), channel_id=1, source_target_pairs={{0,4},{1,5},{2,6},{3,7},{4,0},{5,1},{6,2},{7,3},{8,12},{9,13},{10,... | collective-permute-start | bytes 294920 | tf_op jit(solution)/shard_map/cond/branch_1_fun/ppermute | solution.py:369
  93.5 2.8 %collective-permute-done.39 = bf16[4,64,768]{2,1,0:T(8,128)(2,1)S(1)} collective-permute-done((bf16[4,64,768]{2,1,0:T(8,128)(2,1)S(1)}, bf16[4,64,768]{2,1,0:T(8,128)(2,1)S(1)}, u32[]{:S(2)}, u32[]{:S(2)}) %collective-permute-start.39) | collective-permute-done | bytes 393248 | tf_op jit(solution)/shard_map/cond/branch_1_fun/ppermute | solution.py:369
  96.6 2.3 %collective-permute-done.38 = bf16[2,64,768]{2,1,0:T(8,128)(2,1)S(1)} collective-permute-done((bf16[2,64,768]{2,1,0:T(8,128)(2,1)S(1)}, bf16[2,64,768]{2,1,0:T(8,128)(2,1)S(1)}, u32[]{:S(2)}, u32[]{:S(2)}) %collective-permute-start.38) | collective-permute-done | bytes 196640 | tf_op jit(solution)/shard_map/cond/branch_1_fun/ppermute | solution.py:369
  99.7 2.4 %collective-permute-start.41 = (bf16[1,64,384]{2,1,0:T(8,128)(2,1)S(1)}, bf16[1,64,384]{2,1,0:T(8,128)(2,1)S(1)}, u32[]{:S(2)}, u32[]{:S(2)}) collective-permute-start(bf16[1,64,384]{2,1,0:T(8,128)(2,1)S(1)} %fusion.21), channel_id=1, source_target_pairs={{0,4},{1,5},{2,6},{3,7},{4,0},{5,1},{6,2},{7,3},{8,12},{9,13},{10,... | collective-permute-start | bytes 147464 | tf_op jit(solution)/shard_map/cond/branch_1_fun/ppermute | solution.py:369
  103.6 2.4 %collective-permute-start.47 = (bf16[1,64,768]{2,1,0:T(8,128)(2,1)S(1)}, bf16[1,64,768]{2,1,0:T(8,128)(2,1)S(1)}, u32[]{:S(2)}, u32[]{:S(2)}) collective-permute-start(bf16[1,64,768]{2,1,0:T(8,128)(2,1)S(1)} %get-tuple-element.359), channel_id=1, source_target_pairs={{0,4},{1,5},{2,6},{3,7},{4,0},{5,1},{6,2},{7,3},{8,12},{9,13},{10,... | collective-permute-start | bytes 294920 | tf_op jit(solution)/shard_map/cond/branch_1_fun/ppermute | solution.py:369
  110.7 2.5 %collective-permute-start.44 = (bf16[4,64,384]{2,1,0:T(8,128)(2,1)S(1)}, bf16[4,64,384]{2,1,0:T(8,128)(2,1)S(1)}, u32[]{:S(2)}, u32[]{:S(2)}) collective-permute-start(bf16[4,64,384]{2,1,0:T(8,128)(2,1)S(1)} %constant_dynamic-update-slice_fusion.20.refs_0_), channel_id=1, source_target_pairs={{0,1},{1,0},{2,3},{3,2},{4,5},{5,4},{6,7},{7,6},{8,9},{9,8},{10,11... | collective-permute-start | bytes 589832 | tf_op jit(solution)/shard_map/cond/branch_1_fun/ppermute | solution.py:369
  123.1 2.1 %collective-permute-start.53 = (bf16[4,64,384]{2,1,0:T(8,128)(2,1)S(1)}, bf16[4,64,384]{2,1,0:T(8,128)(2,1)S(1)}, u32[]{:S(2)}, u32[]{:S(2)}) collective-permute-start(bf16[4,64,384]{2,1,0:T(8,128)(2,1)S(1)} %constant_dynamic-update-slice_fusion.30.refs_6_), channel_id=1, source_target_pairs={{0,1},{1,0},{2,3},{3,2},{4,5},{5,4},{6,7},{7,6},{8,9},{9,8},{10,11... | collective-permute-start | bytes 589832 | tf_op jit(solution)/shard_map/cond/branch_1_fun/ppermute | solution.py:369
  127.2 2.1 %collective-permute-done.53.refs_7_ = bf16[4,64,384]{2,1,0:T(8,128)(2,1)S(1)} collective-permute-done((bf16[4,64,384]{2,1,0:T(8,128)(2,1)S(1)}, bf16[4,64,384]{2,1,0:T(8,128)(2,1)S(1)}, u32[]{:S(2)}, u32[]{:S(2)}) %collective-permute-start.53) | collective-permute-done | bytes 196640 | tf_op jit(solution)/shard_map/cond/branch_1_fun/ppermute | solution.py:369
  129.3 7.6 %down.4 = f32[256,320]{1,0:T(8,128)} custom-call(s32[1]{0:T(128)} %get-tuple-element.134.me_s, s32[16]{0:T(128)S(1)} %get-tuple-element.157.base_s, bf16[4,64,384]{2,1,0:T(8,128)(2,1)S(1)} %constant_dynamic-update-slice_fusion.20.refs_0_, bf16[4,64,384]{2,1,0:T(8,128)(2,1)S(1)} %collective-permute-done.44.refs_1_, ...), custom_call_target="tpu_custom_call" | custom-call | tf_op jit(solution)/shard_map/cond/branch_1_fun/down/pallas_call | solution.py:417
  137.4 11.0 %all_to_all.15 = f32[4,64,320]{2,1,0:T(8,128)S(1)} all-to-all(f32[4,64,320]{2,1,0:T(8,128)} %bitcast.37), channel_id=1, replica_groups=mesh['gx'=4,'gy'=8] {'gx'}, dimensions={0} | all-to-all | bytes 655360 | tf_op jit(solution)/shard_map/all_to_all | solution.py:620
  (138 shorter events, 42.0 us)
Async XLA Ops:
  8.9 17.9 %all-to-all-start = ((bf16[8,8,2688]{2,1,0:T(8,128)(2,1)}), bf16[8,8,2688]{2,1,0:T(8,128)(2,1)S(1)}, u32[]{:S(2)}, u32[]{:S(2)}) async-start(bf16[8,8,2688]{2,1,0:T(8,128)(2,1)} %attend.1), calls=%async_computation | async-start | bytes 688128 | tf_op jit(solution)/shard_map/all_to_all | solution.py:584
  28.1 13.2 %all-to-all-start.1 = ((bf16[8,8,2560]{2,1,0:T(8,128)(2,1)}), bf16[8,8,2560]{2,1,0:T(8,128)(2,1)S(1)}, u32[]{:S(2)}, u32[]{:S(2)}) async-start(bf16[8,8,2560]{2,1,0:T(8,128)(2,1)} %broadcast_in_dim.200), calls=%async_computation.1 | async-start | bytes 655360 | tf_op jit(solution)/shard_map/all_to_all | solution.py:590
  53.5 15.7 %collective-permute-start.27 = (bf16[4,64,768]{2,1,0:T(8,128)(2,1)S(1)}, bf16[4,64,768]{2,1,0:T(8,128)(2,1)}, u32[]{:S(2)}, u32[]{:S(2)}) collective-permute-start(bf16[4,64,768]{2,1,0:T(8,128)(2,1)S(1)} %get-tuple-element.140), channel_id=1, source_target_pairs={{0,1},{1,0},{2,3},{3,2},{4,5},{5,4},{6,7},{7,6},{8,9},{9,8},{10,11... | collective-permute-start | bytes 1179656 | tf_op jit(solution)/shard_map/cond/branch_1_fun/ppermute | solution.py:369
  55.1 10.5 %collective-permute-start.28 = (f32[2,128]{1,0:T(2,128)S(1)}, f32[2,128]{1,0:T(2,128)S(1)}, u32[]{:S(2)}, u32[]{:S(2)}) collective-permute-start(f32[2,128]{1,0:T(2,128)S(1)} %get-tuple-element.142), channel_id=1, source_target_pairs={{0,1},{1,0},{2,3},{3,2},{4,5},{5,4},{6,7},{7,6},{8,9},{9,8},{10,11... | collective-permute-start | bytes 3080 | tf_op jit(solution)/shard_map/cond/branch_1_fun/ppermute | solution.py:369
  60.4 18.3 %collective-permute-start.30 = (bf16[4,64,768]{2,1,0:T(8,128)(2,1)S(1)}, bf16[4,64,768]{2,1,0:T(8,128)(2,1)}, u32[]{:S(2)}, u32[]{:S(2)}) collective-permute-start(bf16[4,64,768]{2,1,0:T(8,128)(2,1)S(1)} %get-tuple-element.144), channel_id=1, source_target_pairs={{0,1},{1,0},{2,3},{3,2},{4,5},{5,4},{6,7},{7,6},{8,9},{9,8},{10,11... | collective-permute-start | bytes 1179656 | tf_op jit(solution)/shard_map/cond/branch_1_fun/ppermute | solution.py:369
  70.3 11.0 %collective-permute-start.29 = (bf16[2,64,768]{2,1,0:T(8,128)(2,1)S(1)}, bf16[2,64,768]{2,1,0:T(8,128)(2,1)S(1)}, u32[]{:S(2)}, u32[]{:S(2)}) collective-permute-start(bf16[2,64,768]{2,1,0:T(8,128)(2,1)S(1)} %get-tuple-element.356), channel_id=1, source_target_pairs={{0,2},{1,3},{2,0},{3,1},{4,6},{5,7},{6,4},{7,5},{8,10},{9,11},{10,... | collective-permute-start | bytes 589832 | tf_op jit(solution)/shard_map/cond/branch_1_fun/ppermute | solution.py:369
  76.2 12.6 %collective-permute-start.34 = (bf16[4,64,768]{2,1,0:T(8,128)(2,1)S(1)}, bf16[4,64,768]{2,1,0:T(8,128)(2,1)S(1)}, u32[]{:S(2)}, u32[]{:S(2)}) collective-permute-start(bf16[4,64,768]{2,1,0:T(8,128)(2,1)S(1)} %get-tuple-element.150), channel_id=1, source_target_pairs={{0,1},{1,0},{2,3},{3,2},{4,5},{5,4},{6,7},{7,6},{8,9},{9,8},{10,11... | collective-permute-start | bytes 1179656 | tf_op jit(solution)/shard_map/cond/branch_1_fun/ppermute | solution.py:369
  79.8 10.5 %collective-permute-start.33 = (bf16[2,64,768]{2,1,0:T(8,128)(2,1)S(1)}, bf16[2,64,768]{2,1,0:T(8,128)(2,1)S(1)}, u32[]{:S(2)}, u32[]{:S(2)}) collective-permute-start(bf16[2,64,768]{2,1,0:T(8,128)(2,1)S(1)} %get-tuple-element.355), channel_id=1, source_target_pairs={{0,2},{1,3},{2,0},{3,1},{4,6},{5,7},{6,4},{7,5},{8,10},{9,11},{10,... | collective-permute-start | bytes 589832 | tf_op jit(solution)/shard_map/cond/branch_1_fun/ppermute | solution.py:369
  81.4 11.0 %collective-permute-start.32 = (bf16[1,64,768]{2,1,0:T(8,128)(2,1)S(1)}, bf16[1,64,768]{2,1,0:T(8,128)(2,1)S(1)}, u32[]{:S(2)}, u32[]{:S(2)}) collective-permute-start(bf16[1,64,768]{2,1,0:T(8,128)(2,1)S(1)} %get-tuple-element.364), channel_id=1, source_target_pairs={{0,4},{1,5},{2,6},{3,7},{4,0},{5,1},{6,2},{7,3},{8,12},{9,13},{10,... | collective-permute-start | bytes 294920 | tf_op jit(solution)/shard_map/cond/branch_1_fun/ppermute | solution.py:369
  88.5 7.8 %collective-permute-start.39 = (bf16[4,64,768]{2,1,0:T(8,128)(2,1)S(1)}, bf16[4,64,768]{2,1,0:T(8,128)(2,1)S(1)}, u32[]{:S(2)}, u32[]{:S(2)}) collective-permute-start(bf16[4,64,768]{2,1,0:T(8,128)(2,1)S(1)} %get-tuple-element.158), channel_id=1, source_target_pairs={{0,1},{1,0},{2,3},{3,2},{4,5},{5,4},{6,7},{7,6},{8,9},{9,8},{10,11... | collective-permute-start | bytes 1179656 | tf_op jit(solution)/shard_map/cond/branch_1_fun/ppermute | solution.py:369
  88.9 9.9 %collective-permute-start.38 = (bf16[2,64,768]{2,1,0:T(8,128)(2,1)S(1)}, bf16[2,64,768]{2,1,0:T(8,128)(2,1)S(1)}, u32[]{:S(2)}, u32[]{:S(2)}) collective-permute-start(bf16[2,64,768]{2,1,0:T(8,128)(2,1)S(1)} %get-tuple-element.353), channel_id=1, source_target_pairs={{0,2},{1,3},{2,0},{3,1},{4,6},{5,7},{6,4},{7,5},{8,10},{9,11},{10,... | collective-permute-start | bytes 589832 | tf_op jit(solution)/shard_map/cond/branch_1_fun/ppermute | solution.py:369
  90.3 9.2 %collective-permute-start.37 = (bf16[1,64,768]{2,1,0:T(8,128)(2,1)S(1)}, bf16[1,64,768]{2,1,0:T(8,128)(2,1)S(1)}, u32[]{:S(2)}, u32[]{:S(2)}) collective-permute-start(bf16[1,64,768]{2,1,0:T(8,128)(2,1)S(1)} %get-tuple-element.363), channel_id=1, source_target_pairs={{0,4},{1,5},{2,6},{3,7},{4,0},{5,1},{6,2},{7,3},{8,12},{9,13},{10,... | collective-permute-start | bytes 294920 | tf_op jit(solution)/shard_map/cond/branch_1_fun/ppermute | solution.py:369
  92.5 9.6 %collective-permute-start.36 = (bf16[1,64,384]{2,1,0:T(8,128)(2,1)S(1)}, bf16[1,64,384]{2,1,0:T(8,128)(2,1)S(1)}, u32[]{:S(2)}, u32[]{:S(2)}) collective-permute-start(bf16[1,64,384]{2,1,0:T(8,128)(2,1)S(1)} %fusion.20), channel_id=1, source_target_pairs={{0,4},{1,5},{2,6},{3,7},{4,0},{5,1},{6,2},{7,3},{8,12},{9,13},{10,... | collective-permute-start | bytes 147464 | tf_op jit(solution)/shard_map/cond/branch_1_fun/ppermute | solution.py:369
  96.4 7.1 %collective-permute-start.43 = (bf16[2,64,768]{2,1,0:T(8,128)(2,1)S(1)}, bf16[2,64,768]{2,1,0:T(8,128)(2,1)S(1)}, u32[]{:S(2)}, u32[]{:S(2)}) collective-permute-start(bf16[2,64,768]{2,1,0:T(8,128)(2,1)S(1)} %get-tuple-element.351), channel_id=1, source_target_pairs={{0,2},{1,3},{2,0},{3,1},{4,6},{5,7},{6,4},{7,5},{8,10},{9,11},{10,... | collective-permute-start | bytes 589832 | tf_op jit(solution)/shard_map/cond/branch_1_fun/ppermute | solution.py:369
  98.9 7.0 %collective-permute-start.42 = (bf16[1,64,768]{2,1,0:T(8,128)(2,1)S(1)}, bf16[1,64,768]{2,1,0:T(8,128)(2,1)S(1)}, u32[]{:S(2)}, u32[]{:S(2)}) collective-permute-start(bf16[1,64,768]{2,1,0:T(8,128)(2,1)S(1)} %get-tuple-element.361), channel_id=1, source_target_pairs={{0,4},{1,5},{2,6},{3,7},{4,0},{5,1},{6,2},{7,3},{8,12},{9,13},{10,... | collective-permute-start | bytes 294920 | tf_op jit(solution)/shard_map/cond/branch_1_fun/ppermute | solution.py:369
  99.7 9.2 %collective-permute-start.41 = (bf16[1,64,384]{2,1,0:T(8,128)(2,1)S(1)}, bf16[1,64,384]{2,1,0:T(8,128)(2,1)S(1)}, u32[]{:S(2)}, u32[]{:S(2)}) collective-permute-start(bf16[1,64,384]{2,1,0:T(8,128)(2,1)S(1)} %fusion.21), channel_id=1, source_target_pairs={{0,4},{1,5},{2,6},{3,7},{4,0},{5,1},{6,2},{7,3},{8,12},{9,13},{10,... | collective-permute-start | bytes 147464 | tf_op jit(solution)/shard_map/cond/branch_1_fun/ppermute | solution.py:369
  102.1 8.5 %collective-permute-start.40 = (bf16[2,64,384]{2,1,0:T(8,128)(2,1)S(1)}, bf16[2,64,384]{2,1,0:T(8,128)(2,1)S(1)}, u32[]{:S(2)}, u32[]{:S(2)}) collective-permute-start(bf16[2,64,384]{2,1,0:T(8,128)(2,1)S(1)} %constant_dynamic-update-slice_fusion.16), channel_id=1, source_target_pairs={{0,2},{1,3},{2,0},{3,1},{4,6},{5,7},{6,4},{7,5},{8,10},{9,11},{10,... | collective-permute-start | bytes 294920 | tf_op jit(solution)/shard_map/cond/branch_1_fun/ppermute | solution.py:369
  103.6 9.6 %collective-permute-start.47 = (bf16[1,64,768]{2,1,0:T(8,128)(2,1)S(1)}, bf16[1,64,768]{2,1,0:T(8,128)(2,1)S(1)}, u32[]{:S(2)}, u32[]{:S(2)}) collective-permute-start(bf16[1,64,768]{2,1,0:T(8,128)(2,1)S(1)} %get-tuple-element.359), channel_id=1, source_target_pairs={{0,4},{1,5},{2,6},{3,7},{4,0},{5,1},{6,2},{7,3},{8,12},{9,13},{10,... | collective-permute-start | bytes 294920 | tf_op jit(solution)/shard_map/cond/branch_1_fun/ppermute | solution.py:369
  106.1 9.2 %collective-permute-start.46 = (bf16[1,64,384]{2,1,0:T(8,128)(2,1)S(1)}, bf16[1,64,384]{2,1,0:T(8,128)(2,1)S(1)}, u32[]{:S(2)}, u32[]{:S(2)}) collective-permute-start(bf16[1,64,384]{2,1,0:T(8,128)(2,1)S(1)} %fusion.22), channel_id=1, source_target_pairs={{0,4},{1,5},{2,6},{3,7},{4,0},{5,1},{6,2},{7,3},{8,12},{9,13},{10,... | collective-permute-start | bytes 147464 | tf_op jit(solution)/shard_map/cond/branch_1_fun/ppermute | solution.py:369
  108.9 7.3 %collective-permute-start.45 = (bf16[2,64,384]{2,1,0:T(8,128)(2,1)S(1)}, bf16[2,64,384]{2,1,0:T(8,128)(2,1)S(1)}, u32[]{:S(2)}, u32[]{:S(2)}) collective-permute-start(bf16[2,64,384]{2,1,0:T(8,128)(2,1)S(1)} %constant_dynamic-update-slice_fusion.18), channel_id=1, source_target_pairs={{0,2},{1,3},{2,0},{3,1},{4,6},{5,7},{6,4},{7,5},{8,10},{9,11},{10,... | collective-permute-start | bytes 294920 | tf_op jit(solution)/shard_map/cond/branch_1_fun/ppermute | solution.py:369
  110.7 14.5 %collective-permute-start.44 = (bf16[4,64,384]{2,1,0:T(8,128)(2,1)S(1)}, bf16[4,64,384]{2,1,0:T(8,128)(2,1)S(1)}, u32[]{:S(2)}, u32[]{:S(2)}) collective-permute-start(bf16[4,64,384]{2,1,0:T(8,128)(2,1)S(1)} %constant_dynamic-update-slice_fusion.20.refs_0_), channel_id=1, source_target_pairs={{0,1},{1,0},{2,3},{3,2},{4,5},{5,4},{6,7},{7,6},{8,9},{9,8},{10,11... | collective-permute-start | bytes 589832 | tf_op jit(solution)/shard_map/cond/branch_1_fun/ppermute | solution.py:369
  116.3 8.9 %collective-permute-start.48 = (bf16[4,64,384]{2,1,0:T(8,128)(2,1)S(1)}, bf16[4,64,384]{2,1,0:T(8,128)(2,1)S(1)}, u32[]{:S(2)}, u32[]{:S(2)}) collective-permute-start(bf16[4,64,384]{2,1,0:T(8,128)(2,1)S(1)} %constant_dynamic-update-slice_fusion.24.refs_2_), channel_id=1, source_target_pairs={{0,1},{1,0},{2,3},{3,2},{4,5},{5,4},{6,7},{7,6},{8,9},{9,8},{10,11... | collective-permute-start | bytes 589832 | tf_op jit(solution)/shard_map/cond/branch_1_fun/ppermute | solution.py:369
  120.2 7.0 %collective-permute-start.51 = (bf16[4,64,384]{2,1,0:T(8,128)(2,1)S(1)}, bf16[4,64,384]{2,1,0:T(8,128)(2,1)S(1)}, u32[]{:S(2)}, u32[]{:S(2)}) collective-permute-start(bf16[4,64,384]{2,1,0:T(8,128)(2,1)S(1)} %constant_dynamic-update-slice_fusion.28.refs_4_), channel_id=1, source_target_pairs={{0,1},{1,0},{2,3},{3,2},{4,5},{5,4},{6,7},{7,6},{8,9},{9,8},{10,11... | collective-permute-start | bytes 589832 | tf_op jit(solution)/shard_map/cond/branch_1_fun/ppermute | solution.py:369
  123.1 6.2 %collective-permute-start.53 = (bf16[4,64,384]{2,1,0:T(8,128)(2,1)S(1)}, bf16[4,64,384]{2,1,0:T(8,128)(2,1)S(1)}, u32[]{:S(2)}, u32[]{:S(2)}) collective-permute-start(bf16[4,64,384]{2,1,0:T(8,128)(2,1)S(1)} %constant_dynamic-update-slice_fusion.30.refs_6_), channel_id=1, source_target_pairs={{0,1},{1,0},{2,3},{3,2},{4,5},{5,4},{6,7},{7,6},{8,9},{9,8},{10,11... | collective-permute-start | bytes 589832 | tf_op jit(solution)/shard_map/cond/branch_1_fun/ppermute | solution.py:369
  (17 other events, 404.3 us)

commit v3 on v2

--- a/solution.py
+++ b/solution.py
@@ -22,8 +22,8 @@
 BLOCK = 1024
 ROWS = 16
 ALIGN = 8
-CHUNKS = 4
-UNROLL = 2
+SHARES = (3, 3, 3, 3)
+UNROLL = 4
 
 f32 = jnp.float32
 bf16 = jnp.bfloat16
@@ -291,15 +291,14 @@
     )(hidden_all, gain.reshape(1, -1), rank_t)
 
 
-def gate_up_kernel(names, bit, chunk, me_s, base_s, x_ref, w_hbm, keep_ref, send_ref, scr, buf, sem):
+def gate_up_kernel(names, bit, first, hidden_units, me_s, base_s, x_ref, w_hbm, keep_ref, send_ref, scr, buf, sem):
     experts, slots, _ = x_ref.shape
     units = buf.shape[3]
-    hidden_units = units * CHUNKS
 
     def copies(e):
         return [
             pltpu.make_async_copy(
-                w_hbm.at[e, :, pl.ds(half * hidden_units + chunk * units, units)],
+                w_hbm.at[e, :, pl.ds(half * hidden_units + first, units)],
                 buf.at[e, half],
                 sem.at[e, half],
             )
@@ -337,12 +336,12 @@
         send_ref[i] = scr[pl.ds(pl.multiple_of(at, ALIGN), each), :].astype(bf16)
 
 
-def gate_up(x, w_gate_up, base, me, capacity, parts, chunk, names, bit):
+def gate_up(x, w_gate_up, base, me, capacity, parts, first, units, names, bit):
     experts, slots, features = x.shape
-    units = w_gate_up.shape[2] // (2 * CHUNKS)
+    hidden_units = w_gate_up.shape[2] // 2
     out = jax.ShapeDtypeStruct((parts // 2, capacity // parts, 2 * units), bf16)
     return pl.pallas_call(
-        functools.partial(gate_up_kernel, names, bit, chunk),
+        functools.partial(gate_up_kernel, names, bit, first, hidden_units),
         out_shape=(out, out),
         grid_spec=pltpu.PrefetchScalarGridSpec(
             num_scalar_prefetch=2,
@@ -369,22 +368,20 @@
     return lax.ppermute(x, "gy", [(i, i ^ k) for i in range(parts)])
 
 
-def down_kernel(names, me_s, base_s, *refs):
-    acts = refs[: len(names)]
-    high_ref, low_ref, w_ref, out_ref, scr, rows_scr = refs[len(names) :]
-    experts = w_ref.shape[0]
+def place_rows(acts, firsts, names, me, scr):
     each = acts[0].shape[1]
     capacity = 2 * acts[0].shape[0] * each
-    slots = scr.shape[0] - capacity
-    me = me_s[0]
-
-    scr[capacity:, :] = jnp.zeros((slots, scr.shape[1]), f32)
-    for a, (ref, ns) in enumerate(zip(acts, names)):
-        units = ref.shape[2]
-        lanes = slice((a // 2) * units, (a // 2 + 1) * units)
+    scr[capacity:, :] = jnp.zeros((scr.shape[0] - capacity, scr.shape[1]), f32)
+    for ref, first, ns in zip(acts, firsts, names):
+        lanes = slice(first - firsts[0], first - firsts[0] + ref.shape[2])
         for i, n in enumerate(ns):
             at = jnp.bitwise_xor(me, n) * each
             scr[pl.ds(pl.multiple_of(at, ALIGN), each), lanes] = ref[i].astype(f32)
+
+
+def expert_products(base_s, w_ref, scr, first, slots, store):
+    experts = w_ref.shape[0]
+    lanes = slice(first, first + scr.shape[1])
     unroll = min(UNROLL, experts)
 
     def visit(step, carry):
@@ -392,45 +389,107 @@
         products = [
             lax.dot_general(
                 scr[pl.ds(pl.multiple_of(base_s[e], ALIGN), slots), :].astype(bf16),
-                w_ref[e],
+                w_ref[e, :, lanes],
                 (((1,), (1,)), ((), ())),
                 preferred_element_type=f32,
-            ).astype(bf16)
+            )
             for e in these
         ]
-        for e, product in zip(these, products):
-            rows_scr[pl.ds(pl.multiple_of(e * slots, 16), slots), :] = product
+        at = [pl.ds(pl.multiple_of(e * slots, 16), slots) for e in these]
+        store(at, products)
         return carry
 
     lax.fori_loop(0, experts // unroll, visit, 0)
+
+
+def down_early_kernel(firsts, names, me_s, base_s, *refs):
+    acts = refs[: len(names)]
+    w_ref, out_ref, scr = refs[len(names) :]
+    slots = out_ref.shape[0] // w_ref.shape[0]
+    place_rows(acts, firsts, names, me_s[0], scr)
+
+    def store(at, products):
+        for rows, product in zip(at, products):
+            out_ref[rows, :] = product
+
+    expert_products(base_s, w_ref, scr, firsts[0], slots, store)
+
+
+def down_early(pieces, w_down_t, base, me, total_slots):
+    experts, features, _ = w_down_t.shape
+    firsts, acts, names = [list(column) for column in zip(*pieces)]
+    capacity = 2 * acts[0].shape[0] * acts[0].shape[1]
+    width = firsts[-1] + acts[-1].shape[2] - firsts[0]
+    return pl.pallas_call(
+        functools.partial(down_early_kernel, firsts, names),
+        out_shape=jax.ShapeDtypeStruct((total_slots, features), f32),
+        grid_spec=pltpu.PrefetchScalarGridSpec(
+            num_scalar_prefetch=2,
+            grid=(1,),
+            in_specs=[whole(a.shape) for a in acts] + [pl.BlockSpec(memory_space=pltpu.VMEM)],
+            out_specs=whole((total_slots, features)),
+            scratch_shapes=[pltpu.VMEM((capacity + total_slots // experts, width), f32)],
+        ),
+        compiler_params=params(14),
+        cost_estimate=pl.CostEstimate(
+            flops=2 * total_slots * width * features,
+            bytes_accessed=experts * features * width * 2,
+            transcendentals=0,
+        ),
+        name="down_early",
+    )(me, base, *acts, w_down_t)
+
+
+def down_kernel(firsts, names, me_s, base_s, *refs):
+    acts = refs[: len(names)]
+    early_ref, high_ref, low_ref, w_ref = refs[len(names) : len(names) + 4]
+    outs = refs[len(names) + 4 : -3]
+    scr, rows_scr, total_scr = refs[-3:]
+    slots = early_ref.shape[0] // w_ref.shape[0]
+    place_rows(acts, firsts, names, me_s[0], scr)
+
+    def store(at, products):
+        sums = [early_ref[rows, :] + product for rows, product in zip(at, products)]
+        for rows, product in zip(at, sums):
+            rows_scr[rows, :] = product.astype(bf16)
+
+    expert_products(base_s, w_ref, scr, firsts[0], slots, store)
     rows = rows_scr[...]
-    out_ref[...] = jnp.dot(high_ref[...], rows, preferred_element_type=f32) + jnp.dot(
+    total_scr[...] = jnp.dot(high_ref[...], rows, preferred_element_type=f32) + jnp.dot(
         low_ref[...], rows, preferred_element_type=f32
     )
-
-
-def down(acts, names, w_down_t, base, me, high, low):
-    experts, features, hidden_units = w_down_t.shape
-    capacity = acts[0].shape[0] * acts[0].shape[1] * 2
+    each = outs[0].shape[0]
+    for k, out_ref in enumerate(outs):
+        at = jnp.bitwise_xor(me_s[1], k) * each
+        out_ref[...] = total_scr[pl.ds(pl.multiple_of(at, ALIGN), each), :]
+
+
+def down(pieces, w_down_t, base, me, early, high, low):
+    experts, features, _ = w_down_t.shape
+    firsts, acts, names = [list(column) for column in zip(*pieces)]
+    capacity = 2 * acts[0].shape[0] * acts[0].shape[1]
     slots = high.shape[1] // experts
-    total = high.shape[0]
+    num_gx = E // experts
+    each = high.shape[0] // num_gx
     return pl.pallas_call(
-        functools.partial(down_kernel, names),
-        out_shape=jax.ShapeDtypeStruct((total, features), f32),
+        functools.partial(down_kernel, firsts, names),
+        out_shape=[jax.ShapeDtypeStruct((each, features), f32)] * num_gx,
         grid_spec=pltpu.PrefetchScalarGridSpec(
             num_scalar_prefetch=2,
             grid=(1,),
             in_specs=[whole(a.shape) for a in acts]
-            + [whole(high.shape), whole(low.shape), pl.BlockSpec(memory_space=pltpu.VMEM)],
-            out_specs=whole((total, features)),
+            + [whole(early.shape), whole(high.shape), whole(low.shape)]
+            + [pl.BlockSpec(memory_space=pltpu.VMEM)],
+            out_specs=[whole((each, features))] * num_gx,
             scratch_shapes=[
-                pltpu.VMEM((capacity + slots, hidden_units), f32),
+                pltpu.VMEM((capacity + slots, acts[0].shape[2]), f32),
                 pltpu.VMEM((experts * slots, features), bf16),
+                pltpu.VMEM((high.shape[0], features), f32),
             ],
         ),
-        compiler_params=params(26),
+        compiler_params=params(14),
         name="down",
-    )(me, base, *acts, high, low, w_down_t)
+    )(me, base, *acts, early, high, low, w_down_t)
 
 
 def plan_kernel(rank_ref, weight_ref, high_ref, low_ref):
@@ -462,14 +521,15 @@
 
 
 def experts_part(capacity, x, square, w_gate_up, w_down_t, base, place, high, low, me, parts):
-    units = w_down_t.shape[2] // CHUNKS
+    hidden_units = w_down_t.shape[2]
+    widths = [hidden_units * share // sum(SHARES) for share in SHARES]
     rows = capacity // parts
     here = me[0] * rows + lax.iota(jnp.int32, rows)
     mine = jnp.any(place[None] == here[:, None, None], axis=2)
     bits = [1 << i for i in range(parts.bit_length() - 1)]
-    last_token = [me]
+    last_token = [square]
     squares = [square]
-    chunks = [dict() for _ in range(CHUNKS)]
+    chunks = [dict(units=w, first=sum(widths[:i])) for i, w in enumerate(widths)]
 
     def after(*values):
         return lax.optimization_barrier((*values, last_token[0]))[:-1]
@@ -482,22 +542,21 @@
         done = len(squares) - 1
         if done < len(bits):
             (value,) = after(squares[-1])
-            squares.append(value + send(value, bits[done]))
+            squares.append(value + send(value, bits[::-1][done]))
 
     places = [0]
     for k in bits[:0:-1]:
         places = places + [n ^ k for n in places]
 
-    def start(chunk, state):
+    def start(state):
         (ordered,) = after(base)
         keep, away = gate_up(
-            x, w_gate_up, ordered, me, capacity, parts, chunk, places, bits[0]
+            x, w_gate_up, ordered, me, capacity, parts, state["first"], state["units"], places, bits[0]
         )
         state.update(total=keep, got=send(away, bits[0]))
-        add_squares()
 
     def fold(k):
-        def run(chunk, state):
+        def run(state):
             total, got = after(state["total"], state["got"])
             half = got.shape[0] // 2
             rest = (total[half:].astype(f32) + got[half:].astype(f32)).astype(bf16)
@@ -507,20 +566,21 @@
 
         return run
 
-    def activate(chunk, state):
+    def activate(state):
         while len(squares) <= len(bits):
             add_squares()
         total, got = after(state["total"], state["got"])
         inv = lax.rsqrt(squares[-1].reshape(-1) / D + EPSILON)
         scale = jnp.sum(jnp.where(mine, inv[None, :], 0.0), axis=1)[:, None]
         both = total[0].astype(f32) + got[0].astype(f32)
+        units = state["units"]
         gate = both[:, :units] * scale
         up = both[:, units:] * scale
         act = (jax.nn.silu(gate) * up).astype(bf16)[None]
         state.update(left=act, right=send(act, bits[-1]), names=[0], last=bits[-1])
 
     def spread(k):
-        def run(chunk, state):
+        def run(state):
             left, right = after(state["left"], state["right"])
             both = jnp.concatenate([left, right], axis=0)
             names = state["names"] + [n ^ state["last"] for n in state["names"]]
@@ -529,31 +589,48 @@
         return run
 
     stages = [start] + [fold(k) for k in bits[1:]] + [activate] + [spread(k) for k in bits[-2::-1]]
-    for slot in range(CHUNKS + len(stages) - 1):
+    for slot in range(len(chunks) + len(stages) - 1):
         for i, stage in enumerate(stages):
-            if 0 <= slot - i < CHUNKS:
-                stage(slot - i, chunks[slot - i])
-    acts, names = [], []
+            if 0 <= slot - i < len(chunks):
+                stage(chunks[slot - i])
+        add_squares()
+    pieces = []
     for state in chunks:
-        acts += [state["left"], state["right"]]
-        names += [state["names"], [n ^ state["last"] for n in state["names"]]]
-    return down(acts, names, w_down_t, base, me, high, low)
-
-
-def out_kernel(a_ref, w_ref, r_ref, o_ref):
+        other = [n ^ state["last"] for n in state["names"]]
+        pieces.append((state["first"], state["left"], state["names"]))
+        pieces.append((state["first"], state["right"], other))
+    (ordered,) = after(base)
+    early = down_early(pieces[:-2], w_down_t, ordered, me, high.shape[1])
+    return down(pieces[-2:], w_down_t, base, me, early, high, low)
+
+
+def out_kernel(me_s, *refs):
+    pieces, (w_ref, r_ref, o_ref, scr) = refs[:-4], refs[-4:]
+    rows = pieces[0].shape[0]
+    for k, ref in enumerate(pieces):
+        at = jnp.bitwise_xor(me_s[0] // 2, k) * rows
+        scr[pl.ds(pl.multiple_of(at, ALIGN), rows), :] = ref[...].astype(f32)
     projected = lax.dot_general(
-        a_ref[...], w_ref[...], (((1,), (1,)), ((), ())), preferred_element_type=f32
+        scr[...].astype(bf16), w_ref[...], (((1,), (1,)), ((), ())), preferred_element_type=f32
     )
     o_ref[...] = (r_ref[...].astype(f32) + projected).astype(bf16)
 
 
-def project(attention, out_weight, residual):
+def project(pieces, out_weight, residual, me):
     return pl.pallas_call(
         out_kernel,
         out_shape=jax.ShapeDtypeStruct(residual.shape, bf16),
+        grid_spec=pltpu.PrefetchScalarGridSpec(
+            num_scalar_prefetch=1,
+            grid=(1,),
+            in_specs=[whole(p.shape) for p in pieces]
+            + [whole(out_weight.shape), whole(residual.shape)],
+            out_specs=whole(residual.shape),
+            scratch_shapes=[pltpu.VMEM((residual.shape[0], pieces[0].shape[1]), f32)],
+        ),
         compiler_params=params(8),
         name="project",
-    )(attention, out_weight, residual)
+    )(me, *pieces, out_weight, residual)
 
 
 def shards(
@@ -570,12 +647,12 @@
     w_gate_up,
     w_down,
 ):
-    rows, width = queries.shape
+    rows = queries.shape[0]
     parts = lax.axis_size("gy")
     num_gx = lax.axis_size("gx")
     me_y = lax.axis_index("gy")
     me_x = lax.axis_index("gx")
-    me = jnp.full((1,), me_y, jnp.int32)
+    me = jnp.stack([me_y, me_x]).astype(jnp.int32)
     each = rows // parts
     slots = -(-(num_gx * CAPS + ALIGN - 1) // 16) * 16
     local = w_gate_up.shape[0]
@@ -587,10 +664,10 @@
         lax.dynamic_slice_in_dim(queries, me_y * each, each, 0),
         lax.dynamic_slice_in_dim(token_key_value, me_y * each, each, 0),
     )
-    attention = lax.all_to_all(
-        jnp.broadcast_to(attention[None], (parts,) + attention.shape), "gy", 0, 0
-    ).reshape(rows, width)
-    hidden = project(attention, out_weight.T, residual)
+    pairs = [[i, i + 1] for i in range(0, parts, 2)]
+    attention = lax.all_gather(attention, "gy", axis=0, tiled=True, axis_index_groups=pairs)
+    pieces = [attention] + [exchange(attention, 2 * k, parts) for k in range(1, parts // 2)]
+    hidden = project(pieces, out_weight.T, residual, me)
     hidden_all = lax.all_gather(hidden, "gx", axis=0, tiled=True)
 
     mixing = jax.nn.softmax(gate_logits, axis=-1)
@@ -617,8 +694,10 @@
         [lambda *o, c=c: experts_part(c, *o, parts=parts) for c in sizes],
         *operands,
     )
-    routed = lax.all_to_all(routed.reshape(num_gx, rows, -1), "gx", 0, 0)
-    return hidden.astype(f32) + jnp.sum(routed, axis=0)
+    total = hidden.astype(f32) + routed[0]
+    for k in range(num_gx - 1, 0, -1):
+        total = total + lax.ppermute(routed[k], "gx", [(i, i ^ k) for i in range(num_gx)])
+    return total
 
 
 def solution(mesh):

time: 148 us -> 140 us (0.946); the launches traced: 149 us -> 139 us
  starting transfers between devices: 48.3 us -> 40.8 us
  blocking collectives: 16.6 us -> 10.3 us
  waiting for transfers between devices: 34.7 us -> 37.9 us
    all_to_all x1 -> x0, blocking collectives: 11 us -> none  [shards(): routed = lax.all_to_all(routed.reshape(num_gx, rows, -1), 'gx', 0, 0)]
    ppermute x27 -> x30, waiting for transfers between devices: 21 us -> 27.4 us  [exchange(): return lax.ppermute(x, 'gy', [(i, i ^ k) for i in range(parts)])]
    all_to_all x1 -> x0, waiting for transfers between devices: 6.05 us -> none  [shards(): lax.all_to_all(jnp.broadcast_to(attention[None], (parts,) + attention.sha...]
    ppermute x0 -> x3, waiting for transfers between devices: none -> 5.15 us  [shards(): lax.ppermute(routed[k], 'gx', [(i, i ^ k) for i in range(num_gx)])]
    ppermute x27 -> x30, starting transfers between devices: 36.3 us -> 31.4 us  [exchange(): return lax.ppermute(x, 'gy', [(i, i ^ k) for i in range(parts)])]
    all_gather x0 -> x1, blocking collectives: none -> 4.68 us  [shards(): lax.all_gather(attention, 'gy', axis=0, tiled=True, axis_index_groups=pairs)]
    all_to_all x1 -> x0, starting transfers between devices: 3.64 us -> none  [shards(): lax.all_to_all(jnp.broadcast_to(attention[None], (parts,) + attention.sha...]
    all_to_all x1, waiting for transfers between devices: 7.68 us -> 5.29 us  [shards(): part = lax.all_to_all(part, 'gy', 0, 0)]
  transfers between devices with their start and end apart: 29 -> 34, of which waited for: 13 -> 17; matrix products, arithmetic and copies ran while one was open for 4% -> 5% of each run, Pallas kernels for 11% -> 15%
where the time goes in v3:
time: 140 us; the launch traced here: 139 us
  starting transfers between devices  40.8 us (29%)
  Pallas kernels  40.5 us (29%)
  waiting for transfers between devices  37.9 us (27%)
  blocking collectives  10.3 us (7%)
  other arithmetic  5.45 us (4%)
  between operations  1.49 us (1%)
  local copies, waits for them, and re-layouts  1.46 us (1%)
    ppermute x30, starting transfers between devices, exchange(): return lax.ppermute(x, 'gy', [(i, i ^ k) for i in range(parts)])  31.4 us
    ppermute x30, waiting for transfers between devices, exchange(): return lax.ppermute(x, 'gy', [(i, i ^ k) for i in range(parts)])  27.4 us
    pallas_call x4, Pallas kernels, gate_up(): pl.pallas_call(functools.partial(gate_up_kernel, names, bit, first, hidde...  19.5 us
    pallas_call x1, Pallas kernels, attend_local(): pl.pallas_call(attend_kernel, out_shape=out, grid_spec=pltpu.PrefetchScal...  8.85 us
    all_to_all x1, starting transfers between devices, shards(): part = lax.all_to_all(part, 'gy', 0, 0)  7.54 us
    all_gather x1, blocking collectives, shards(): hidden_all = lax.all_gather(hidden, 'gx', axis=0, tiled=True)  5.61 us
    all_to_all x1, waiting for transfers between devices, shards(): part = lax.all_to_all(part, 'gy', 0, 0)  5.29 us
    ppermute x3, waiting for transfers between devices, shards(): lax.ppermute(routed[k], 'gx', [(i, i ^ k) for i in range(num_gx)])  5.15 us
  transfers between devices with their start and end apart: 34, of which 17 were waited for; matrix products, arithmetic and copies ran while one was open for 5% of the time, Pallas kernels for 15%

profile of v3, /device:TPU:0, one launch (start us, length us, event | category | flops | bytes accessed | tf_op | source)
XLA Modules:
  0.0 138.9 jit_solution(11173264977655810704)
XLA Ops:
  0.0 8.8 %attend.1 = bf16[8,8,2688]{2,1,0:T(8,128)(2,1)} custom-call(s32[4096]{0:T(1024)} %bitcast.84, bf16[64,2560]{1,0:T(8,128)(2,1)} %q_ref.1, s32[1,4096]{1,0:T(1,128)} %own_ref.1, bf16[1,4096,512]{2,1,0:T(8,128)(2,1)} %k_hbm.1, bf16[1,4096,512]{2,1,0:T(8,128)(2,1)} %v_hbm.1), custom_call_target="tpu_custom_call" | custom-call | tf_op jit(solution)/shard_map/attend/pallas_call | solution.py:160
  8.9 7.5 %all-to-all-start = ((bf16[8,8,2688]{2,1,0:T(8,128)(2,1)}), bf16[8,8,2688]{2,1,0:T(8,128)(2,1)S(1)}, u32[]{:S(2)}, u32[]{:S(2)}) async-start(bf16[8,8,2688]{2,1,0:T(8,128)(2,1)} %attend.1), calls=%async_computation | async-start | bytes 688128 | tf_op jit(solution)/shard_map/all_to_all | solution.py:661
  21.8 5.3 %all-to-all-done.part_ref = bf16[8,8,2688]{2,1,0:T(8,128)(2,1)S(1)} async-done(((bf16[8,8,2688]{2,1,0:T(8,128)(2,1)}), bf16[8,8,2688]{2,1,0:T(8,128)(2,1)S(1)}, u32[]{:S(2)}, u32[]{:S(2)}) %all-to-all-start) | async-done | bytes 344096 | tf_op jit(solution)/shard_map/all_to_all | solution.py:661
  27.6 4.7 %all_gather.6.refs_0_ = bf16[16,2560]{1,0:T(8,128)(2,1)S(1)} all-gather(bf16[8,2560]{1,0:T(8,128)(2,1)S(1)} %merge.1), channel_id=1, replica_groups={{0,1},{2,3},{4,5},{6,7},{8,9},{10,11},{12,13},{14,15},{16,17},{18,19},{..., dimensions={0}, use_global_device_ids=true | all-gather | bytes 122880 | tf_op jit(solution)/shard_map/all_gather | solution.py:668
  34.0 2.7 %collective-permute-start.83 = (bf16[16,2560]{1,0:T(8,128)(2,1)S(1)}, bf16[16,2560]{1,0:T(8,128)(2,1)S(1)}, u32[]{:S(2)}, u32[]{:S(2)}) collective-permute-start(bf16[16,2560]{1,0:T(8,128)(2,1)S(1)} %all_gather.6.refs_0_), channel_id=1, source_target_pairs={{0,6},{1,7},{2,4},{3,5},{4,2},{5,3},{6,0},{7,1},{8,14},{9,15},{10,... | collective-permute-start | bytes 245768 | tf_op jit(solution)/shard_map/ppermute | solution.py:368
  37.6 2.7 %collective-permute-done.82.refs_2_ = bf16[16,2560]{1,0:T(8,128)(2,1)S(1)} collective-permute-done((bf16[16,2560]{1,0:T(8,128)(2,1)S(1)}, bf16[16,2560]{1,0:T(8,128)(2,1)S(1)}, u32[]{:S(2)}, u32[]{:S(2)}) %collective-permute-start.82) | collective-permute-done | bytes 81952 | tf_op jit(solution)/shard_map/ppermute | solution.py:368
  41.6 5.6 %all_gather.7.h_ref = bf16[256,320]{1,0:T(8,128)(2,1)S(1)} all-gather(bf16[64,320]{1,0:T(8,128)(2,1)S(1)} %project.1), channel_id=1, replica_groups=mesh['gx'=4,'gy'=8] {'gx'}, dimensions={0}, use_global_device_ids=true | all-gather | bytes 204800 | tf_op jit(solution)/shard_map/all_gather | solution.py:671
  48.1 83.1 %conditional.1 = ((f32[64,320]{1,0:T(8,128)S(1)}, f32[64,320]{1,0:T(8,128)S(1)}, f32[64,320]{1,0:T(8,128)}, f32[64,320]{1,0:T(8,128)})) conditional(s32[]{:T(128)} %clamp.3, (s32[16]{0:T(128)S(1)}, f32[2,128]{1,0:T(2,128)S(1)}, s32[2]{0:T(128)S(1)}, bf16[16,64,320]{2,1,0:T(8,128)(2,1)S(1)}, bf16[16,320,3072]{2,1,0:T(8,128)(2,1)}, ...), branch_computations={%region_9.12_spmd, %region_12.15_spmd, %region_15.18_spmd} | conditional | flops 2776425728 | bytes 147875712 | solution.py:692
  48.5 4.8 %gate_up.16 = (bf16[4,64,768]{2,1,0:T(8,128)(2,1)S(1)}, bf16[4,64,768]{2,1,0:T(8,128)(2,1)S(1)}) custom-call(s32[2]{0:T(128)S(1)} %get-tuple-element.131.me_s, s32[16]{0:T(128)S(1)} %get-tuple-element.193.base_s, bf16[16,64,320]{2,1,0:T(8,128)(2,1)S(1)} %get-tuple-element.135.x_ref, bf16[16,320,3072]{2,1,0:T(8,128)(2,1)} %get-tuple-element.136.w_hbm), custom_call_target="tpu_custom_call" | custom-call | flops 503316480 | bytes 8650752 | tf_op jit(solution)/shard_map/cond/branch_1_fun/gate_up/pallas_call | solution.py:343
  53.4 1.8 %collective-permute-start.28 = (bf16[4,64,768]{2,1,0:T(8,128)(2,1)S(1)}, bf16[4,64,768]{2,1,0:T(8,128)(2,1)}, u32[]{:S(2)}, u32[]{:S(2)}) collective-permute-start(bf16[4,64,768]{2,1,0:T(8,128)(2,1)S(1)} %get-tuple-element.137), channel_id=1, source_target_pairs={{0,1},{1,0},{2,3},{3,2},{4,5},{5,4},{6,7},{7,6},{8,9},{9,8},{10,11... | collective-permute-start | bytes 1179656 | tf_op jit(solution)/shard_map/cond/branch_1_fun/ppermute | solution.py:368
  55.2 4.8 %gate_up.17 = (bf16[4,64,768]{2,1,0:T(8,128)(2,1)S(1)}, bf16[4,64,768]{2,1,0:T(8,128)(2,1)S(1)}) custom-call(s32[2]{0:T(128)S(1)} %get-tuple-element.131.me_s, s32[16]{0:T(128)S(1)} %get-tuple-element.193.base_s, bf16[16,64,320]{2,1,0:T(8,128)(2,1)S(1)} %get-tuple-element.135.x_ref, bf16[16,320,3072]{2,1,0:T(8,128)(2,1)} %get-tuple-element.136.w_hbm), custom_call_target="tpu_custom_call" | custom-call | flops 503316480 | bytes 8650752 | tf_op jit(solution)/shard_map/cond/branch_1_fun/gate_up/pallas_call | solution.py:343
  61.3 4.2 %collective-permute-done.28 = bf16[4,64,768]{2,1,0:T(8,128)(2,1)} collective-permute-done((bf16[4,64,768]{2,1,0:T(8,128)(2,1)S(1)}, bf16[4,64,768]{2,1,0:T(8,128)(2,1)}, u32[]{:S(2)}, u32[]{:S(2)}) %collective-permute-start.28) | collective-permute-done | bytes 393248 | tf_op jit(solution)/shard_map/cond/branch_1_fun/ppermute | solution.py:368
  68.7 4.8 %gate_up.18 = (bf16[4,64,768]{2,1,0:T(8,128)(2,1)S(1)}, bf16[4,64,768]{2,1,0:T(8,128)(2,1)S(1)}) custom-call(s32[2]{0:T(128)S(1)} %get-tuple-element.131.me_s, s32[16]{0:T(128)S(1)} %get-tuple-element.193.base_s, bf16[16,64,320]{2,1,0:T(8,128)(2,1)S(1)} %get-tuple-element.135.x_ref, bf16[16,320,3072]{2,1,0:T(8,128)(2,1)} %get-tuple-element.136.w_hbm), custom_call_target="tpu_custom_call" | custom-call | flops 503316480 | bytes 8650752 | tf_op jit(solution)/shard_map/cond/branch_1_fun/gate_up/pallas_call | solution.py:343
  80.0 5.1 %gate_up.19 = (bf16[4,64,768]{2,1,0:T(8,128)(2,1)S(1)}, bf16[4,64,768]{2,1,0:T(8,128)(2,1)S(1)}) custom-call(s32[2]{0:T(128)S(1)} %get-tuple-element.131.me_s, s32[16]{0:T(128)S(1)} %get-tuple-element.193.base_s, bf16[16,64,320]{2,1,0:T(8,128)(2,1)S(1)} %get-tuple-element.135.x_ref, bf16[16,320,3072]{2,1,0:T(8,128)(2,1)} %get-tuple-element.136.w_hbm), custom_call_target="tpu_custom_call" | custom-call | flops 503316480 | bytes 8650752 | tf_op jit(solution)/shard_map/cond/branch_1_fun/gate_up/pallas_call | solution.py:343
  87.0 2.1 %collective-permute-start.39 = (bf16[1,64,768]{2,1,0:T(8,128)(2,1)S(1)}, bf16[1,64,768]{2,1,0:T(8,128)(2,1)S(1)}, u32[]{:S(2)}, u32[]{:S(2)}) collective-permute-start(bf16[1,64,768]{2,1,0:T(8,128)(2,1)S(1)} %get-tuple-element.370), channel_id=1, source_target_pairs={{0,4},{1,5},{2,6},{3,7},{4,0},{5,1},{6,2},{7,3},{8,12},{9,13},{10,... | collective-permute-start | bytes 294920 | tf_op jit(solution)/shard_map/cond/branch_1_fun/ppermute | solution.py:368
  90.2 3.8 %collective-permute-done.32 = bf16[4,64,768]{2,1,0:T(8,128)(2,1)S(1)} collective-permute-done((bf16[4,64,768]{2,1,0:T(8,128)(2,1)S(1)}, bf16[4,64,768]{2,1,0:T(8,128)(2,1)S(1)}, u32[]{:S(2)}, u32[]{:S(2)}) %collective-permute-start.32) | collective-permute-done | bytes 393248 | tf_op jit(solution)/shard_map/cond/branch_1_fun/ppermute | solution.py:368
  99.6 3.4 %collective-permute-done.37 = bf16[2,64,768]{2,1,0:T(8,128)(2,1)S(1)} collective-permute-done((bf16[2,64,768]{2,1,0:T(8,128)(2,1)S(1)}, bf16[2,64,768]{2,1,0:T(8,128)(2,1)S(1)}, u32[]{:S(2)}, u32[]{:S(2)}) %collective-permute-start.37) | collective-permute-done | bytes 196640 | tf_op jit(solution)/shard_map/cond/branch_1_fun/ppermute | solution.py:368
  103.2 3.0 %collective-permute-start.47 = (bf16[1,64,384]{2,1,0:T(8,128)(2,1)S(1)}, bf16[1,64,384]{2,1,0:T(8,128)(2,1)S(1)}, u32[]{:S(2)}, u32[]{:S(2)}) collective-permute-start(bf16[1,64,384]{2,1,0:T(8,128)(2,1)S(1)} %fusion.22), channel_id=1, source_target_pairs={{0,4},{1,5},{2,6},{3,7},{4,0},{5,1},{6,2},{7,3},{8,12},{9,13},{10,... | collective-permute-start | bytes 147464 | tf_op jit(solution)/shard_map/cond/branch_1_fun/ppermute | solution.py:368
  107.1 2.8 %collective-permute-done.41 = bf16[1,64,768]{2,1,0:T(8,128)(2,1)S(1)} collective-permute-done((bf16[1,64,768]{2,1,0:T(8,128)(2,1)S(1)}, bf16[1,64,768]{2,1,0:T(8,128)(2,1)S(1)}, u32[]{:S(2)}, u32[]{:S(2)}) %collective-permute-start.41) | collective-permute-done | bytes 98336 | tf_op jit(solution)/shard_map/cond/branch_1_fun/ppermute | solution.py:368
  113.2 2.0 %collective-permute-done.45 = bf16[1,64,384]{2,1,0:T(8,128)(2,1)S(1)} collective-permute-done((bf16[1,64,384]{2,1,0:T(8,128)(2,1)S(1)}, bf16[1,64,384]{2,1,0:T(8,128)(2,1)S(1)}, u32[]{:S(2)}, u32[]{:S(2)}) %collective-permute-start.45) | collective-permute-done | bytes 49184 | tf_op jit(solution)/shard_map/cond/branch_1_fun/ppermute | solution.py:368
  117.2 2.7 %collective-permute-done.48 = bf16[2,64,384]{2,1,0:T(8,128)(2,1)S(1)} collective-permute-done((bf16[2,64,384]{2,1,0:T(8,128)(2,1)S(1)}, bf16[2,64,384]{2,1,0:T(8,128)(2,1)S(1)}, u32[]{:S(2)}, u32[]{:S(2)}) %collective-permute-start.48) | collective-permute-done | bytes 98336 | tf_op jit(solution)/shard_map/cond/branch_1_fun/ppermute | solution.py:368
  122.9 4.4 %down_early.4.refs_2_ = f32[1024,320]{1,0:T(8,128)S(1)} custom-call(s32[2]{0:T(128)S(1)} %get-tuple-element.131.me_s, s32[16]{0:T(128)S(1)} %get-tuple-element.193.base_s, bf16[4,64,384]{2,1,0:T(8,128)(2,1)S(1)} %constant_dynamic-update-slice_fusion.20.refs_0_, bf16[4,64,384]{2,1,0:T(8,128)(2,1)S(1)} %collective-permute-done.51.refs_1_, ...), custom_call_target="tpu_custom_call" | custom-call | flops 754974720 | bytes 11796480 | tf_op jit(solution)/shard_map/cond/branch_1_fun/down_early/pallas_call | solution.py:423
  127.4 3.8 %down.4 = (f32[64,320]{1,0:T(8,128)S(1)}, f32[64,320]{1,0:T(8,128)S(1)}, f32[64,320]{1,0:T(8,128)}, f32[64,320]{1,0:T(8,128)}) custom-call(s32[2]{0:T(128)S(1)} %get-tuple-element.131.me_s, s32[16]{0:T(128)S(1)} %get-tuple-element.193.base_s, bf16[4,64,384]{2,1,0:T(8,128)(2,1)S(1)} %constant_dynamic-update-slice_fusion.30.refs_0_, ...), custom_call_target="tpu_custom_call" | custom-call | tf_op jit(solution)/shard_map/cond/branch_1_fun/down/pallas_call | solution.py:474
  133.0 3.4 %collective-permute-done.84 = f32[64,320]{1,0:T(8,128)S(1)} collective-permute-done((f32[64,320]{1,0:T(8,128)}, f32[64,320]{1,0:T(8,128)S(1)}, u32[]{:S(2)}, u32[]{:S(2)}) %collective-permute-start.84) | collective-permute-done | bytes 81952 | tf_op jit(solution)/shard_map/ppermute | solution.py:699
  (152 shorter events, 42.1 us)
Async XLA Ops:
  8.9 18.2 %all-to-all-start = ((bf16[8,8,2688]{2,1,0:T(8,128)(2,1)}), bf16[8,8,2688]{2,1,0:T(8,128)(2,1)S(1)}, u32[]{:S(2)}, u32[]{:S(2)}) async-start(bf16[8,8,2688]{2,1,0:T(8,128)(2,1)} %attend.1), calls=%async_computation | async-start | bytes 688128 | tf_op jit(solution)/shard_map/all_to_all | solution.py:661
  33.3 7.1 %collective-permute-start.82 = (bf16[16,2560]{1,0:T(8,128)(2,1)S(1)}, bf16[16,2560]{1,0:T(8,128)(2,1)S(1)}, u32[]{:S(2)}, u32[]{:S(2)}) collective-permute-start(bf16[16,2560]{1,0:T(8,128)(2,1)S(1)} %all_gather.6.refs_0_), channel_id=1, source_target_pairs={{0,4},{1,5},{2,6},{3,7},{4,0},{5,1},{6,2},{7,3},{8,12},{9,13},{10,... | collective-permute-start | bytes 245768 | tf_op jit(solution)/shard_map/ppermute | solution.py:368
  53.4 12.1 %collective-permute-start.28 = (bf16[4,64,768]{2,1,0:T(8,128)(2,1)S(1)}, bf16[4,64,768]{2,1,0:T(8,128)(2,1)}, u32[]{:S(2)}, u32[]{:S(2)}) collective-permute-start(bf16[4,64,768]{2,1,0:T(8,128)(2,1)S(1)} %get-tuple-element.137), channel_id=1, source_target_pairs={{0,1},{1,0},{2,3},{3,2},{4,5},{5,4},{6,7},{7,6},{8,9},{9,8},{10,11... | collective-permute-start | bytes 1179656 | tf_op jit(solution)/shard_map/cond/branch_1_fun/ppermute | solution.py:368
  60.1 15.2 %collective-permute-start.31 = (bf16[4,64,768]{2,1,0:T(8,128)(2,1)S(1)}, bf16[4,64,768]{2,1,0:T(8,128)(2,1)}, u32[]{:S(2)}, u32[]{:S(2)}) collective-permute-start(bf16[4,64,768]{2,1,0:T(8,128)(2,1)S(1)} %get-tuple-element.141), channel_id=1, source_target_pairs={{0,1},{1,0},{2,3},{3,2},{4,5},{5,4},{6,7},{7,6},{8,9},{9,8},{10,11... | collective-permute-start | bytes 1179656 | tf_op jit(solution)/shard_map/cond/branch_1_fun/ppermute | solution.py:368
  66.6 10.6 %collective-permute-start.30 = (bf16[2,64,768]{2,1,0:T(8,128)(2,1)S(1)}, bf16[2,64,768]{2,1,0:T(8,128)(2,1)S(1)}, u32[]{:S(2)}, u32[]{:S(2)}) collective-permute-start(bf16[2,64,768]{2,1,0:T(8,128)(2,1)S(1)} %get-tuple-element.364), channel_id=1, source_target_pairs={{0,2},{1,3},{2,0},{3,1},{4,6},{5,7},{6,4},{7,5},{8,10},{9,11},{10,... | collective-permute-start | bytes 589832 | tf_op jit(solution)/shard_map/cond/branch_1_fun/ppermute | solution.py:368
  68.1 9.1 %collective-permute-start.29 = (f32[2,128]{1,0:T(2,128)S(1)}, f32[2,128]{1,0:T(2,128)S(1)}, u32[]{:S(2)}, u32[]{:S(2)}) collective-permute-start(f32[2,128]{1,0:T(2,128)S(1)} %add.313), channel_id=1, source_target_pairs={{0,2},{1,3},{2,0},{3,1},{4,6},{5,7},{6,4},{7,5},{8,10},{9,11},{10,... | collective-permute-start | bytes 3080 | tf_op jit(solution)/shard_map/cond/branch_1_fun/ppermute | solution.py:368
  73.5 13.2 %collective-permute-start.35 = (bf16[4,64,768]{2,1,0:T(8,128)(2,1)S(1)}, bf16[4,64,768]{2,1,0:T(8,128)(2,1)S(1)}, u32[]{:S(2)}, u32[]{:S(2)}) collective-permute-start(bf16[4,64,768]{2,1,0:T(8,128)(2,1)S(1)} %get-tuple-element.147), channel_id=1, source_target_pairs={{0,1},{1,0},{2,3},{3,2},{4,5},{5,4},{6,7},{7,6},{8,9},{9,8},{10,11... | collective-permute-start | bytes 1179656 | tf_op jit(solution)/shard_map/cond/branch_1_fun/ppermute | solution.py:368
  76.4 10.6 %collective-permute-start.34 = (bf16[2,64,768]{2,1,0:T(8,128)(2,1)S(1)}, bf16[2,64,768]{2,1,0:T(8,128)(2,1)S(1)}, u32[]{:S(2)}, u32[]{:S(2)}) collective-permute-start(bf16[2,64,768]{2,1,0:T(8,128)(2,1)S(1)} %get-tuple-element.362), channel_id=1, source_target_pairs={{0,2},{1,3},{2,0},{3,1},{4,6},{5,7},{6,4},{7,5},{8,10},{9,11},{10,... | collective-permute-start | bytes 589832 | tf_op jit(solution)/shard_map/cond/branch_1_fun/ppermute | solution.py:368
  77.2 9.4 %collective-permute-start.36 = (f32[2,128]{1,0:T(2,128)S(1)}, f32[2,128]{1,0:T(2,128)S(1)}, u32[]{:S(2)}, u32[]{:S(2)}) collective-permute-start(f32[2,128]{1,0:T(2,128)S(1)} %add.315), channel_id=1, source_target_pairs={{0,1},{1,0},{2,3},{3,2},{4,5},{5,4},{6,7},{7,6},{8,9},{9,8},{10,11... | collective-permute-start | bytes 3080 | tf_op jit(solution)/shard_map/cond/branch_1_fun/ppermute | solution.py:368
  78.4 10.8 %collective-permute-start.33 = (bf16[1,64,768]{2,1,0:T(8,128)(2,1)S(1)}, bf16[1,64,768]{2,1,0:T(8,128)(2,1)S(1)}, u32[]{:S(2)}, u32[]{:S(2)}) collective-permute-start(bf16[1,64,768]{2,1,0:T(8,128)(2,1)S(1)} %get-tuple-element.372), channel_id=1, source_target_pairs={{0,4},{1,5},{2,6},{3,7},{4,0},{5,1},{6,2},{7,3},{8,12},{9,13},{10,... | collective-permute-start | bytes 294920 | tf_op jit(solution)/shard_map/cond/branch_1_fun/ppermute | solution.py:368
  85.1 9.0 %collective-permute-start.32 = (bf16[4,64,768]{2,1,0:T(8,128)(2,1)S(1)}, bf16[4,64,768]{2,1,0:T(8,128)(2,1)S(1)}, u32[]{:S(2)}, u32[]{:S(2)}) collective-permute-start(bf16[4,64,768]{2,1,0:T(8,128)(2,1)S(1)} %get-tuple-element.155), channel_id=1, source_target_pairs={{0,1},{1,0},{2,3},{3,2},{4,5},{5,4},{6,7},{7,6},{8,9},{9,8},{10,11... | collective-permute-start | bytes 1179656 | tf_op jit(solution)/shard_map/cond/branch_1_fun/ppermute | solution.py:368
  86.9 7.9 %collective-permute-start.40 = (bf16[2,64,768]{2,1,0:T(8,128)(2,1)S(1)}, bf16[2,64,768]{2,1,0:T(8,128)(2,1)S(1)}, u32[]{:S(2)}, u32[]{:S(2)}) collective-permute-start(bf16[2,64,768]{2,1,0:T(8,128)(2,1)S(1)} %get-tuple-element.358), channel_id=1, source_target_pairs={{0,2},{1,3},{2,0},{3,1},{4,6},{5,7},{6,4},{7,5},{8,10},{9,11},{10,... | collective-permute-start | bytes 589832 | tf_op jit(solution)/shard_map/cond/branch_1_fun/ppermute | solution.py:368
  87.0 9.4 %collective-permute-start.39 = (bf16[1,64,768]{2,1,0:T(8,128)(2,1)S(1)}, bf16[1,64,768]{2,1,0:T(8,128)(2,1)S(1)}, u32[]{:S(2)}, u32[]{:S(2)}) collective-permute-start(bf16[1,64,768]{2,1,0:T(8,128)(2,1)S(1)} %get-tuple-element.370), channel_id=1, source_target_pairs={{0,4},{1,5},{2,6},{3,7},{4,0},{5,1},{6,2},{7,3},{8,12},{9,13},{10,... | collective-permute-start | bytes 294920 | tf_op jit(solution)/shard_map/cond/branch_1_fun/ppermute | solution.py:368
  89.3 8.7 %collective-permute-start.38 = (bf16[1,64,384]{2,1,0:T(8,128)(2,1)S(1)}, bf16[1,64,384]{2,1,0:T(8,128)(2,1)S(1)}, u32[]{:S(2)}, u32[]{:S(2)}) collective-permute-start(bf16[1,64,384]{2,1,0:T(8,128)(2,1)S(1)} %fusion.20), channel_id=1, source_target_pairs={{0,4},{1,5},{2,6},{3,7},{4,0},{5,1},{6,2},{7,3},{8,12},{9,13},{10,... | collective-permute-start | bytes 147464 | tf_op jit(solution)/shard_map/cond/branch_1_fun/ppermute | solution.py:368
  94.2 8.8 %collective-permute-start.37 = (bf16[2,64,768]{2,1,0:T(8,128)(2,1)S(1)}, bf16[2,64,768]{2,1,0:T(8,128)(2,1)S(1)}, u32[]{:S(2)}, u32[]{:S(2)}) collective-permute-start(bf16[2,64,768]{2,1,0:T(8,128)(2,1)S(1)} %get-tuple-element.359), channel_id=1, source_target_pairs={{0,2},{1,3},{2,0},{3,1},{4,6},{5,7},{6,4},{7,5},{8,10},{9,11},{10,... | collective-permute-start | bytes 589832 | tf_op jit(solution)/shard_map/cond/branch_1_fun/ppermute | solution.py:368
  94.8 8.3 %collective-permute-start.44 = (bf16[1,64,768]{2,1,0:T(8,128)(2,1)S(1)}, bf16[1,64,768]{2,1,0:T(8,128)(2,1)S(1)}, u32[]{:S(2)}, u32[]{:S(2)}) collective-permute-start(bf16[1,64,768]{2,1,0:T(8,128)(2,1)S(1)} %get-tuple-element.366), channel_id=1, source_target_pairs={{0,4},{1,5},{2,6},{3,7},{4,0},{5,1},{6,2},{7,3},{8,12},{9,13},{10,... | collective-permute-start | bytes 294920 | tf_op jit(solution)/shard_map/cond/branch_1_fun/ppermute | solution.py:368
  96.6 9.6 %collective-permute-start.43 = (bf16[1,64,384]{2,1,0:T(8,128)(2,1)S(1)}, bf16[1,64,384]{2,1,0:T(8,128)(2,1)S(1)}, u32[]{:S(2)}, u32[]{:S(2)}) collective-permute-start(bf16[1,64,384]{2,1,0:T(8,128)(2,1)S(1)} %fusion.21), channel_id=1, source_target_pairs={{0,4},{1,5},{2,6},{3,7},{4,0},{5,1},{6,2},{7,3},{8,12},{9,13},{10,... | collective-permute-start | bytes 147464 | tf_op jit(solution)/shard_map/cond/branch_1_fun/ppermute | solution.py:368
  98.0 8.6 %collective-permute-start.42 = (bf16[2,64,384]{2,1,0:T(8,128)(2,1)S(1)}, bf16[2,64,384]{2,1,0:T(8,128)(2,1)S(1)}, u32[]{:S(2)}, u32[]{:S(2)}) collective-permute-start(bf16[2,64,384]{2,1,0:T(8,128)(2,1)S(1)} %constant_dynamic-update-slice_fusion.16), channel_id=1, source_target_pairs={{0,2},{1,3},{2,0},{3,1},{4,6},{5,7},{6,4},{7,5},{8,10},{9,11},{10,... | collective-permute-start | bytes 294920 | tf_op jit(solution)/shard_map/cond/branch_1_fun/ppermute | solution.py:368
  103.0 6.9 %collective-permute-start.41 = (bf16[1,64,768]{2,1,0:T(8,128)(2,1)S(1)}, bf16[1,64,768]{2,1,0:T(8,128)(2,1)S(1)}, u32[]{:S(2)}, u32[]{:S(2)}) collective-permute-start(bf16[1,64,768]{2,1,0:T(8,128)(2,1)S(1)} %get-tuple-element.367), channel_id=1, source_target_pairs={{0,4},{1,5},{2,6},{3,7},{4,0},{5,1},{6,2},{7,3},{8,12},{9,13},{10,... | collective-permute-start | bytes 294920 | tf_op jit(solution)/shard_map/cond/branch_1_fun/ppermute | solution.py:368
  103.2 7.7 %collective-permute-start.47 = (bf16[1,64,384]{2,1,0:T(8,128)(2,1)S(1)}, bf16[1,64,384]{2,1,0:T(8,128)(2,1)S(1)}, u32[]{:S(2)}, u32[]{:S(2)}) collective-permute-start(bf16[1,64,384]{2,1,0:T(8,128)(2,1)S(1)} %fusion.22), channel_id=1, source_target_pairs={{0,4},{1,5},{2,6},{3,7},{4,0},{5,1},{6,2},{7,3},{8,12},{9,13},{10,... | collective-permute-start | bytes 147464 | tf_op jit(solution)/shard_map/cond/branch_1_fun/ppermute | solution.py:368
  106.6 14.5 %collective-permute-start.51 = (bf16[4,64,384]{2,1,0:T(8,128)(2,1)S(1)}, bf16[4,64,384]{2,1,0:T(8,128)(2,1)S(1)}, u32[]{:S(2)}, u32[]{:S(2)}) collective-permute-start(bf16[4,64,384]{2,1,0:T(8,128)(2,1)S(1)} %constant_dynamic-update-slice_fusion.20.refs_0_), channel_id=1, source_target_pairs={{0,1},{1,0},{2,3},{3,2},{4,5},{5,4},{6,7},{7,6},{8,9},{9,8},{10,11... | collective-permute-start | bytes 589832 | tf_op jit(solution)/shard_map/cond/branch_1_fun/ppermute | solution.py:368
  112.3 8.8 %collective-permute-start.52 = (bf16[4,64,384]{2,1,0:T(8,128)(2,1)S(1)}, bf16[4,64,384]{2,1,0:T(8,128)(2,1)S(1)}, u32[]{:S(2)}, u32[]{:S(2)}) collective-permute-start(bf16[4,64,384]{2,1,0:T(8,128)(2,1)S(1)} %constant_dynamic-update-slice_fusion.24.refs_2_), channel_id=1, source_target_pairs={{0,1},{1,0},{2,3},{3,2},{4,5},{5,4},{6,7},{7,6},{8,9},{9,8},{10,11... | collective-permute-start | bytes 589832 | tf_op jit(solution)/shard_map/cond/branch_1_fun/ppermute | solution.py:368
  120.0 7.4 %collective-permute-start.50 = (bf16[4,64,384]{2,1,0:T(8,128)(2,1)S(1)}, bf16[4,64,384]{2,1,0:T(8,128)(2,1)S(1)}, u32[]{:S(2)}, u32[]{:S(2)}) collective-permute-start(bf16[4,64,384]{2,1,0:T(8,128)(2,1)S(1)} %constant_dynamic-update-slice_fusion.30.refs_0_), channel_id=1, source_target_pairs={{0,1},{1,0},{2,3},{3,2},{4,5},{5,4},{6,7},{7,6},{8,9},{9,8},{10,11... | collective-permute-start | bytes 589832 | tf_op jit(solution)/shard_map/cond/branch_1_fun/ppermute | solution.py:368
  131.2 7.0 %collective-permute-start.85 = (f32[64,320]{1,0:T(8,128)}, f32[64,320]{1,0:T(8,128)S(1)}, u32[]{:S(2)}, u32[]{:S(2)}) collective-permute-start(f32[64,320]{1,0:T(8,128)} %get-tuple-element.277), channel_id=1, source_target_pairs={{0,16},{8,24},{16,0},{24,8},{1,17},{9,25},{17,1},{25,9},{2,18},{10... | collective-permute-start | bytes 245768 | tf_op jit(solution)/shard_map/ppermute | solution.py:699
  (24 other events, 465.4 us)

commit v4 on v3

--- a/solution.py
+++ b/solution.py
@@ -23,6 +23,9 @@
 ROWS = 16
 ALIGN = 8
 SHARES = (3, 3, 3, 3)
+JOINED = ()
+TURNED = ()
+YFIRST = (1, 3)
 UNROLL = 4
 
 f32 = jnp.float32
@@ -544,27 +547,37 @@
             (value,) = after(squares[-1])
             squares.append(value + send(value, bits[::-1][done]))
 
-    places = [0]
-    for k in bits[:0:-1]:
-        places = places + [n ^ k for n in places]
+    for i, state in enumerate(chunks):
+        order = bits[1:] + bits[:1] if i in TURNED else bits
+        places = [0]
+        for k in order[:0:-1]:
+            places = places + [n ^ k for n in places]
+        state.update(order=order, places=places, joined=i in JOINED)
+        back = order[::-1]
+        state.update(back=back[-1:] + back[:-1] if i in YFIRST else back)
 
     def start(state):
         (ordered,) = after(base)
+        order = state["order"]
         keep, away = gate_up(
-            x, w_gate_up, ordered, me, capacity, parts, state["first"], state["units"], places, bits[0]
+            x, w_gate_up, ordered, me, capacity, parts, state["first"], state["units"],
+            state["places"], order[0]
         )
-        state.update(total=keep, got=send(away, bits[0]))
-
-    def fold(k):
+        state.update(total=keep, got=send(away, order[0]))
+
+    def fold(i):
         def run(state):
             total, got = after(state["total"], state["got"])
             half = got.shape[0] // 2
             rest = (total[half:].astype(f32) + got[half:].astype(f32)).astype(bf16)
             state.update(
-                total=total[:half].astype(f32) + got[:half].astype(f32), got=send(rest, k)
+                total=total[:half].astype(f32) + got[:half].astype(f32),
+                got=send(rest, state["order"][i]),
             )
 
         return run
+
+    waiting = []
 
     def activate(state):
         while len(squares) <= len(bits):
@@ -577,10 +590,20 @@
         gate = both[:, :units] * scale
         up = both[:, units:] * scale
         act = (jax.nn.silu(gate) * up).astype(bf16)[None]
-        state.update(left=act, right=send(act, bits[-1]), names=[0], last=bits[-1])
-
-    def spread(k):
+        waiting.append((state["first"], act))
+        if state["joined"]:
+            return
+        state.update(first=waiting[0][0])
+        act = jnp.concatenate([a for _, a in waiting], axis=2)
+        waiting.clear()
+        last = state["back"][0]
+        state.update(left=act, right=send(act, last), names=[0], last=last)
+
+    def spread(i):
         def run(state):
+            if state["joined"]:
+                return
+            k = state["back"][i]
             left, right = after(state["left"], state["right"])
             both = jnp.concatenate([left, right], axis=0)
             names = state["names"] + [n ^ state["last"] for n in state["names"]]
@@ -588,7 +611,8 @@
 
         return run
 
-    stages = [start] + [fold(k) for k in bits[1:]] + [activate] + [spread(k) for k in bits[-2::-1]]
+    steps = range(len(bits))
+    stages = [start] + [fold(i) for i in steps[1:]] + [activate] + [spread(i) for i in steps[1:]]
     for slot in range(len(chunks) + len(stages) - 1):
         for i, stage in enumerate(stages):
             if 0 <= slot - i < len(chunks):
@@ -596,6 +620,8 @@
         add_squares()
     pieces = []
     for state in chunks:
+        if state["joined"]:
+            continue
         other = [n ^ state["last"] for n in state["names"]]
         pieces.append((state["first"], state["left"], state["names"]))
         pieces.append((state["first"], state["right"], other))

time: 140 us -> 134 us (0.957)
  waiting for transfers between devices: 37.9 us -> 29.8 us
  starting transfers between devices: 40.8 us -> 44.2 us
    ppermute x30, waiting for transfers between devices: 27.4 us -> 19.5 us  [exchange(): return lax.ppermute(x, 'gy', [(i, i ^ k) for i in range(parts)])]
    ppermute x30, starting transfers between devices: 31.4 us -> 34.8 us  [exchange(): return lax.ppermute(x, 'gy', [(i, i ^ k) for i in range(parts)])]
  transfers between devices with their start and end apart: 34 -> 34, of which waited for: 17 -> 13; matrix products, arithmetic and copies ran while one was open for 5% -> 4% of each run, Pallas kernels for 15% -> 16%
where the time goes in v4:
time: 134 us; the launch traced here: 133 us
  starting transfers between devices  44.2 us (33%)
  Pallas kernels  41 us (31%)
  waiting for transfers between devices  29.8 us (22%)
  blocking collectives  10.3 us (8%)
  other arithmetic  4.37 us (3%)
  between operations  1.49 us (1%)
  local copies, waits for them, and re-layouts  1.45 us (1%)
    ppermute x30, starting transfers between devices, exchange(): return lax.ppermute(x, 'gy', [(i, i ^ k) for i in range(parts)])  34.8 us
    pallas_call x4, Pallas kernels, gate_up(): pl.pallas_call(functools.partial(gate_up_kernel, names, bit, first, hidde...  20 us
    ppermute x30, waiting for transfers between devices, exchange(): return lax.ppermute(x, 'gy', [(i, i ^ k) for i in range(parts)])  19.5 us
    pallas_call x1, Pallas kernels, attend_local(): pl.pallas_call(attend_kernel, out_shape=out, grid_spec=pltpu.PrefetchScal...  8.85 us
    all_to_all x1, starting transfers between devices, shards(): part = lax.all_to_all(part, 'gy', 0, 0)  7.54 us
    all_to_all x1, waiting for transfers between devices, shards(): part = lax.all_to_all(part, 'gy', 0, 0)  6.32 us
    all_gather x1, blocking collectives, shards(): hidden_all = lax.all_gather(hidden, 'gx', axis=0, tiled=True)  5.61 us
    all_gather x1, blocking collectives, shards(): lax.all_gather(attention, 'gy', axis=0, tiled=True, axis_index_groups=pairs)  4.68 us
  transfers between devices with their start and end apart: 34, of which 13 were waited for; matrix products, arithmetic and copies ran while one was open for 4% of the time, Pallas kernels for 16%

profile of v4, /device:TPU:0, one launch (start us, length us, event | category | flops | bytes accessed | tf_op | source)
XLA Modules:
  0.0 133.3 jit_solution(6989711117068487731)
XLA Ops:
  0.0 8.8 %attend.1 = bf16[8,8,2688]{2,1,0:T(8,128)(2,1)} custom-call(s32[4096]{0:T(1024)} %bitcast.84, bf16[64,2560]{1,0:T(8,128)(2,1)} %q_ref.1, s32[1,4096]{1,0:T(1,128)} %own_ref.1, bf16[1,4096,512]{2,1,0:T(8,128)(2,1)} %k_hbm.1, bf16[1,4096,512]{2,1,0:T(8,128)(2,1)} %v_hbm.1), custom_call_target="tpu_custom_call" | custom-call | tf_op jit(solution)/shard_map/attend/pallas_call | solution.py:163
  8.9 7.5 %all-to-all-start = ((bf16[8,8,2688]{2,1,0:T(8,128)(2,1)}), bf16[8,8,2688]{2,1,0:T(8,128)(2,1)S(1)}, u32[]{:S(2)}, u32[]{:S(2)}) async-start(bf16[8,8,2688]{2,1,0:T(8,128)(2,1)} %attend.1), calls=%async_computation | async-start | bytes 688128 | tf_op jit(solution)/shard_map/all_to_all | solution.py:687
  21.8 6.3 %all-to-all-done.part_ref = bf16[8,8,2688]{2,1,0:T(8,128)(2,1)S(1)} async-done(((bf16[8,8,2688]{2,1,0:T(8,128)(2,1)}), bf16[8,8,2688]{2,1,0:T(8,128)(2,1)S(1)}, u32[]{:S(2)}, u32[]{:S(2)}) %all-to-all-start) | async-done | bytes 344096 | tf_op jit(solution)/shard_map/all_to_all | solution.py:687
  28.7 4.7 %all_gather.6.refs_0_ = bf16[16,2560]{1,0:T(8,128)(2,1)S(1)} all-gather(bf16[8,2560]{1,0:T(8,128)(2,1)S(1)} %merge.1), channel_id=1, replica_groups={{0,1},{2,3},{4,5},{6,7},{8,9},{10,11},{12,13},{14,15},{16,17},{18,19},{..., dimensions={0}, use_global_device_ids=true | all-gather | bytes 122880 | tf_op jit(solution)/shard_map/all_gather | solution.py:694
  35.1 2.6 %collective-permute-start.83 = (bf16[16,2560]{1,0:T(8,128)(2,1)S(1)}, bf16[16,2560]{1,0:T(8,128)(2,1)S(1)}, u32[]{:S(2)}, u32[]{:S(2)}) collective-permute-start(bf16[16,2560]{1,0:T(8,128)(2,1)S(1)} %all_gather.6.refs_0_), channel_id=1, source_target_pairs={{0,6},{1,7},{2,4},{3,5},{4,2},{5,3},{6,0},{7,1},{8,14},{9,15},{10,... | collective-permute-start | bytes 245768 | tf_op jit(solution)/shard_map/ppermute | solution.py:371
  37.8 4.1 %collective-permute-done.82.refs_2_ = bf16[16,2560]{1,0:T(8,128)(2,1)S(1)} collective-permute-done((bf16[16,2560]{1,0:T(8,128)(2,1)S(1)}, bf16[16,2560]{1,0:T(8,128)(2,1)S(1)}, u32[]{:S(2)}, u32[]{:S(2)}) %collective-permute-start.82) | collective-permute-done | bytes 81952 | tf_op jit(solution)/shard_map/ppermute | solution.py:371
  43.1 5.6 %all_gather.7.h_ref = bf16[256,320]{1,0:T(8,128)(2,1)S(1)} all-gather(bf16[64,320]{1,0:T(8,128)(2,1)S(1)} %project.1), channel_id=1, replica_groups=mesh['gx'=4,'gy'=8] {'gx'}, dimensions={0}, use_global_device_ids=true | all-gather | bytes 204800 | tf_op jit(solution)/shard_map/all_gather | solution.py:697
  49.6 77.1 %conditional.1 = ((f32[64,320]{1,0:T(8,128)S(1)}, f32[64,320]{1,0:T(8,128)S(1)}, f32[64,320]{1,0:T(8,128)}, f32[64,320]{1,0:T(8,128)})) conditional(s32[]{:T(128)} %clamp.3, (s32[16]{0:T(128)S(1)}, f32[2,128]{1,0:T(2,128)S(1)}, s32[2]{0:T(128)S(1)}, bf16[16,64,320]{2,1,0:T(8,128)(2,1)S(1)}, bf16[16,320,3072]{2,1,0:T(8,128)(2,1)}, ...), branch_computations={%region_9.12_spmd, %region_12.15_spmd, %region_15.18_spmd} | conditional | flops 2776425728 | bytes 147875712 | solution.py:718
  49.8 4.8 %gate_up.12 = (bf16[4,56,768]{2,1,0:T(8,128)(2,1)S(1)}, bf16[4,56,768]{2,1,0:T(8,128)(2,1)S(1)}) custom-call(s32[2]{0:T(128)S(1)} %get-tuple-element.65.me_s, s32[16]{0:T(128)S(1)} %get-tuple-element.127.base_s, bf16[16,64,320]{2,1,0:T(8,128)(2,1)S(1)} %get-tuple-element.69.x_ref, bf16[16,320,3072]{2,1,0:T(8,128)(2,1)} %get-tuple-element.70.w_hbm), custom_call_target="tpu_custom_call" | custom-call | flops 503316480 | bytes 8552448 | tf_op jit(solution)/shard_map/cond/branch_0_fun/gate_up/pallas_call | solution.py:346
  57.6 4.8 %gate_up.13 = (bf16[4,56,768]{2,1,0:T(8,128)(2,1)S(1)}, bf16[4,56,768]{2,1,0:T(8,128)(2,1)S(1)}) custom-call(s32[2]{0:T(128)S(1)} %get-tuple-element.65.me_s, s32[16]{0:T(128)S(1)} %get-tuple-element.127.base_s, bf16[16,64,320]{2,1,0:T(8,128)(2,1)S(1)} %get-tuple-element.69.x_ref, bf16[16,320,3072]{2,1,0:T(8,128)(2,1)} %get-tuple-element.70.w_hbm), custom_call_target="tpu_custom_call" | custom-call | flops 503316480 | bytes 8552448 | tf_op jit(solution)/shard_map/cond/branch_0_fun/gate_up/pallas_call | solution.py:346
  66.3 1.6 %collective-permute-start.3 = (bf16[2,56,768]{2,1,0:T(8,128)(2,1)S(1)}, bf16[2,56,768]{2,1,0:T(8,128)(2,1)S(1)}, u32[]{:S(2)}, u32[]{:S(2)}) collective-permute-start(bf16[2,56,768]{2,1,0:T(8,128)(2,1)S(1)} %get-tuple-element.348), channel_id=1, source_target_pairs={{0,2},{1,3},{2,0},{3,1},{4,6},{5,7},{6,4},{7,5},{8,10},{9,11},{10,... | collective-permute-start | bytes 516104 | tf_op jit(solution)/shard_map/cond/branch_0_fun/ppermute | solution.py:371
  68.3 4.8 %gate_up.14 = (bf16[4,56,768]{2,1,0:T(8,128)(2,1)S(1)}, bf16[4,56,768]{2,1,0:T(8,128)(2,1)S(1)}) custom-call(s32[2]{0:T(128)S(1)} %get-tuple-element.65.me_s, s32[16]{0:T(128)S(1)} %get-tuple-element.127.base_s, bf16[16,64,320]{2,1,0:T(8,128)(2,1)S(1)} %get-tuple-element.69.x_ref, bf16[16,320,3072]{2,1,0:T(8,128)(2,1)} %get-tuple-element.70.w_hbm), custom_call_target="tpu_custom_call" | custom-call | flops 503316480 | bytes 8552448 | tf_op jit(solution)/shard_map/cond/branch_0_fun/gate_up/pallas_call | solution.py:346
  73.2 1.8 %collective-permute-start.8 = (bf16[4,56,768]{2,1,0:T(8,128)(2,1)S(1)}, bf16[4,56,768]{2,1,0:T(8,128)(2,1)S(1)}, u32[]{:S(2)}, u32[]{:S(2)}) collective-permute-start(bf16[4,56,768]{2,1,0:T(8,128)(2,1)S(1)} %get-tuple-element.81), channel_id=1, source_target_pairs={{0,1},{1,0},{2,3},{3,2},{4,5},{5,4},{6,7},{7,6},{8,9},{9,8},{10,11... | collective-permute-start | bytes 1032200 | tf_op jit(solution)/shard_map/cond/branch_0_fun/ppermute | solution.py:371
  78.4 5.5 %gate_up.15 = (bf16[4,56,768]{2,1,0:T(8,128)(2,1)S(1)}, bf16[4,56,768]{2,1,0:T(8,128)(2,1)S(1)}) custom-call(s32[2]{0:T(128)S(1)} %get-tuple-element.65.me_s, s32[16]{0:T(128)S(1)} %get-tuple-element.127.base_s, bf16[16,64,320]{2,1,0:T(8,128)(2,1)S(1)} %get-tuple-element.69.x_ref, bf16[16,320,3072]{2,1,0:T(8,128)(2,1)} %get-tuple-element.70.w_hbm), custom_call_target="tpu_custom_call" | custom-call | flops 503316480 | bytes 8552448 | tf_op jit(solution)/shard_map/cond/branch_0_fun/gate_up/pallas_call | solution.py:346
  87.8 1.6 %collective-permute-start.11 = (bf16[1,56,384]{2,1,0:T(8,128)(2,1)S(1)}, bf16[1,56,384]{2,1,0:T(8,128)(2,1)S(1)}, u32[]{:S(2)}, u32[]{:S(2)}) collective-permute-start(bf16[1,56,384]{2,1,0:T(8,128)(2,1)S(1)} %fusion.8), channel_id=1, source_target_pairs={{0,4},{1,5},{2,6},{3,7},{4,0},{5,1},{6,2},{7,3},{8,12},{9,13},{10,... | collective-permute-start | bytes 129032 | tf_op jit(solution)/shard_map/cond/branch_0_fun/ppermute | solution.py:371
  89.4 2.3 %collective-permute-done.5 = bf16[4,56,768]{2,1,0:T(8,128)(2,1)S(1)} collective-permute-done((bf16[4,56,768]{2,1,0:T(8,128)(2,1)S(1)}, bf16[4,56,768]{2,1,0:T(8,128)(2,1)S(1)}, u32[]{:S(2)}, u32[]{:S(2)}) %collective-permute-start.5) | collective-permute-done | bytes 344096 | tf_op jit(solution)/shard_map/cond/branch_0_fun/ppermute | solution.py:371
  97.0 2.2 %collective-permute-done.10 = bf16[2,56,768]{2,1,0:T(8,128)(2,1)S(1)} collective-permute-done((bf16[2,56,768]{2,1,0:T(8,128)(2,1)S(1)}, bf16[2,56,768]{2,1,0:T(8,128)(2,1)S(1)}, u32[]{:S(2)}, u32[]{:S(2)}) %collective-permute-start.10) | collective-permute-done | bytes 172064 | tf_op jit(solution)/shard_map/cond/branch_0_fun/ppermute | solution.py:371
  99.7 2.8 %collective-permute-start.20 = (bf16[1,56,384]{2,1,0:T(8,128)(2,1)S(1)}, bf16[1,56,384]{2,1,0:T(8,128)(2,1)S(1)}, u32[]{:S(2)}, u32[]{:S(2)}) collective-permute-start(bf16[1,56,384]{2,1,0:T(8,128)(2,1)S(1)} %fusion.10), channel_id=1, source_target_pairs={{0,4},{1,5},{2,6},{3,7},{4,0},{5,1},{6,2},{7,3},{8,12},{9,13},{10,... | collective-permute-start | bytes 129032 | tf_op jit(solution)/shard_map/cond/branch_0_fun/ppermute | solution.py:371
  102.8 1.6 %collective-permute-start.24 = (bf16[4,56,384]{2,1,0:T(8,128)(2,1)S(1)}, bf16[4,56,384]{2,1,0:T(8,128)(2,1)S(1)}, u32[]{:S(2)}, u32[]{:S(2)}) collective-permute-start(bf16[4,56,384]{2,1,0:T(8,128)(2,1)S(1)} %constant_dynamic-update-slice_fusion.4.refs_0_), channel_id=1, source_target_pairs={{0,1},{1,0},{2,3},{3,2},{4,5},{5,4},{6,7},{7,6},{8,9},{9,8},{10,11... | collective-permute-start | bytes 516104 | tf_op jit(solution)/shard_map/cond/branch_0_fun/ppermute | solution.py:371
  104.5 1.7 %collective-permute-done.14 = bf16[1,56,768]{2,1,0:T(8,128)(2,1)S(1)} collective-permute-done((bf16[1,56,768]{2,1,0:T(8,128)(2,1)S(1)}, bf16[1,56,768]{2,1,0:T(8,128)(2,1)S(1)}, u32[]{:S(2)}, u32[]{:S(2)}) %collective-permute-start.14) | collective-permute-done | bytes 86048 | tf_op jit(solution)/shard_map/cond/branch_0_fun/ppermute | solution.py:371
  113.5 3.4 %collective-permute-done.21 = bf16[2,56,384]{2,1,0:T(8,128)(2,1)S(1)} collective-permute-done((bf16[2,56,384]{2,1,0:T(8,128)(2,1)S(1)}, bf16[2,56,384]{2,1,0:T(8,128)(2,1)S(1)}, u32[]{:S(2)}, u32[]{:S(2)}) %collective-permute-start.21) | collective-permute-done | bytes 86048 | tf_op jit(solution)/shard_map/cond/branch_0_fun/ppermute | solution.py:371
  118.5 4.4 %down_early.3.refs_2_ = f32[1024,320]{1,0:T(8,128)S(1)} custom-call(s32[2]{0:T(128)S(1)} %get-tuple-element.65.me_s, s32[16]{0:T(128)S(1)} %get-tuple-element.127.base_s, bf16[4,56,384]{2,1,0:T(8,128)(2,1)S(1)} %constant_dynamic-update-slice_fusion.4.refs_0_, bf16[4,56,384]{2,1,0:T(8,128)(2,1)S(1)} %collective-permute-done.24.refs_1_, ...), custom_call_target="tpu_custom_call" | custom-call | flops 754974720 | bytes 11796480 | tf_op jit(solution)/shard_map/cond/branch_0_fun/down_early/pallas_call | solution.py:426
  122.9 3.8 %down.3 = (f32[64,320]{1,0:T(8,128)S(1)}, f32[64,320]{1,0:T(8,128)S(1)}, f32[64,320]{1,0:T(8,128)}, f32[64,320]{1,0:T(8,128)}) custom-call(s32[2]{0:T(128)S(1)} %get-tuple-element.65.me_s, s32[16]{0:T(128)S(1)} %get-tuple-element.127.base_s, bf16[4,56,384]{2,1,0:T(8,128)(2,1)S(1)} %constant_dynamic-update-slice_fusion.14.refs_0_, ...), custom_call_target="tpu_custom_call" | custom-call | tf_op jit(solution)/shard_map/cond/branch_0_fun/down/pallas_call | solution.py:477
  128.6 2.9 %collective-permute-done.84 = f32[64,320]{1,0:T(8,128)S(1)} collective-permute-done((f32[64,320]{1,0:T(8,128)}, f32[64,320]{1,0:T(8,128)S(1)}, u32[]{:S(2)}, u32[]{:S(2)}) %collective-permute-start.84) | collective-permute-done | bytes 81952 | tf_op jit(solution)/shard_map/ppermute | solution.py:725
  (152 shorter events, 41.3 us)
Async XLA Ops:
  8.9 19.2 %all-to-all-start = ((bf16[8,8,2688]{2,1,0:T(8,128)(2,1)}), bf16[8,8,2688]{2,1,0:T(8,128)(2,1)S(1)}, u32[]{:S(2)}, u32[]{:S(2)}) async-start(bf16[8,8,2688]{2,1,0:T(8,128)(2,1)} %attend.1), calls=%async_computation | async-start | bytes 688128 | tf_op jit(solution)/shard_map/all_to_all | solution.py:687
  34.2 7.7 %collective-permute-start.82 = (bf16[16,2560]{1,0:T(8,128)(2,1)S(1)}, bf16[16,2560]{1,0:T(8,128)(2,1)S(1)}, u32[]{:S(2)}, u32[]{:S(2)}) collective-permute-start(bf16[16,2560]{1,0:T(8,128)(2,1)S(1)} %all_gather.6.refs_0_), channel_id=1, source_target_pairs={{0,4},{1,5},{2,6},{3,7},{4,0},{5,1},{6,2},{7,3},{8,12},{9,13},{10,... | collective-permute-start | bytes 245768 | tf_op jit(solution)/shard_map/ppermute | solution.py:371
  35.1 6.8 %collective-permute-start.83 = (bf16[16,2560]{1,0:T(8,128)(2,1)S(1)}, bf16[16,2560]{1,0:T(8,128)(2,1)S(1)}, u32[]{:S(2)}, u32[]{:S(2)}) collective-permute-start(bf16[16,2560]{1,0:T(8,128)(2,1)S(1)} %all_gather.6.refs_0_), channel_id=1, source_target_pairs={{0,6},{1,7},{2,4},{3,5},{4,2},{5,3},{6,0},{7,1},{8,14},{9,15},{10,... | collective-permute-start | bytes 245768 | tf_op jit(solution)/shard_map/ppermute | solution.py:371
  54.6 10.5 %collective-permute-start.1 = (bf16[4,56,768]{2,1,0:T(8,128)(2,1)S(1)}, bf16[4,56,768]{2,1,0:T(8,128)(2,1)}, u32[]{:S(2)}, u32[]{:S(2)}) collective-permute-start(bf16[4,56,768]{2,1,0:T(8,128)(2,1)S(1)} %get-tuple-element.71), channel_id=1, source_target_pairs={{0,1},{1,0},{2,3},{3,2},{4,5},{5,4},{6,7},{7,6},{8,9},{9,8},{10,11... | collective-permute-start | bytes 1032200 | tf_op jit(solution)/shard_map/cond/branch_0_fun/ppermute | solution.py:371
  56.0 7.7 %collective-permute-start = (f32[2,128]{1,0:T(2,128)S(1)}, f32[2,128]{1,0:T(2,128)S(1)}, u32[]{:S(2)}, u32[]{:S(2)}) collective-permute-start(f32[2,128]{1,0:T(2,128)S(1)} %get-tuple-element.72), channel_id=1, source_target_pairs={{0,4},{1,5},{2,6},{3,7},{4,0},{5,1},{6,2},{7,3},{8,12},{9,13},{10,... | collective-permute-start | bytes 3080 | tf_op jit(solution)/shard_map/cond/branch_0_fun/ppermute | solution.py:371
  62.4 12.6 %collective-permute-start.4 = (bf16[4,56,768]{2,1,0:T(8,128)(2,1)S(1)}, bf16[4,56,768]{2,1,0:T(8,128)(2,1)S(1)}, u32[]{:S(2)}, u32[]{:S(2)}) collective-permute-start(bf16[4,56,768]{2,1,0:T(8,128)(2,1)S(1)} %get-tuple-element.75), channel_id=1, source_target_pairs={{0,1},{1,0},{2,3},{3,2},{4,5},{5,4},{6,7},{7,6},{8,9},{9,8},{10,11... | collective-permute-start | bytes 1032200 | tf_op jit(solution)/shard_map/cond/branch_0_fun/ppermute | solution.py:371
  66.3 10.2 %collective-permute-start.3 = (bf16[2,56,768]{2,1,0:T(8,128)(2,1)S(1)}, bf16[2,56,768]{2,1,0:T(8,128)(2,1)S(1)}, u32[]{:S(2)}, u32[]{:S(2)}) collective-permute-start(bf16[2,56,768]{2,1,0:T(8,128)(2,1)S(1)} %get-tuple-element.348), channel_id=1, source_target_pairs={{0,2},{1,3},{2,0},{3,1},{4,6},{5,7},{6,4},{7,5},{8,10},{9,11},{10,... | collective-permute-start | bytes 516104 | tf_op jit(solution)/shard_map/cond/branch_0_fun/ppermute | solution.py:371
  67.9 8.6 %collective-permute-start.2 = (f32[2,128]{1,0:T(2,128)S(1)}, f32[2,128]{1,0:T(2,128)S(1)}, u32[]{:S(2)}, u32[]{:S(2)}) collective-permute-start(f32[2,128]{1,0:T(2,128)S(1)} %add.279), channel_id=1, source_target_pairs={{0,2},{1,3},{2,0},{3,1},{4,6},{5,7},{6,4},{7,5},{8,10},{9,11},{10,... | collective-permute-start | bytes 3080 | tf_op jit(solution)/shard_map/cond/branch_0_fun/ppermute | solution.py:371
  73.2 12.1 %collective-permute-start.8 = (bf16[4,56,768]{2,1,0:T(8,128)(2,1)S(1)}, bf16[4,56,768]{2,1,0:T(8,128)(2,1)S(1)}, u32[]{:S(2)}, u32[]{:S(2)}) collective-permute-start(bf16[4,56,768]{2,1,0:T(8,128)(2,1)S(1)} %get-tuple-element.81), channel_id=1, source_target_pairs={{0,1},{1,0},{2,3},{3,2},{4,5},{5,4},{6,7},{7,6},{8,9},{9,8},{10,11... | collective-permute-start | bytes 1032200 | tf_op jit(solution)/shard_map/cond/branch_0_fun/ppermute | solution.py:371
  75.1 11.1 %collective-permute-start.7 = (bf16[2,56,768]{2,1,0:T(8,128)(2,1)S(1)}, bf16[2,56,768]{2,1,0:T(8,128)(2,1)S(1)}, u32[]{:S(2)}, u32[]{:S(2)}) collective-permute-start(bf16[2,56,768]{2,1,0:T(8,128)(2,1)S(1)} %get-tuple-element.346), channel_id=1, source_target_pairs={{0,2},{1,3},{2,0},{3,1},{4,6},{5,7},{6,4},{7,5},{8,10},{9,11},{10,... | collective-permute-start | bytes 516104 | tf_op jit(solution)/shard_map/cond/branch_0_fun/ppermute | solution.py:371
  76.6 8.6 %collective-permute-start.9 = (f32[2,128]{1,0:T(2,128)S(1)}, f32[2,128]{1,0:T(2,128)S(1)}, u32[]{:S(2)}, u32[]{:S(2)}) collective-permute-start(f32[2,128]{1,0:T(2,128)S(1)} %add.281), channel_id=1, source_target_pairs={{0,1},{1,0},{2,3},{3,2},{4,5},{5,4},{6,7},{7,6},{8,9},{9,8},{10,11... | collective-permute-start | bytes 3080 | tf_op jit(solution)/shard_map/cond/branch_0_fun/ppermute | solution.py:371
  77.2 10.5 %collective-permute-start.6 = (bf16[1,56,768]{2,1,0:T(8,128)(2,1)S(1)}, bf16[1,56,768]{2,1,0:T(8,128)(2,1)S(1)}, u32[]{:S(2)}, u32[]{:S(2)}) collective-permute-start(bf16[1,56,768]{2,1,0:T(8,128)(2,1)S(1)} %get-tuple-element.356), channel_id=1, source_target_pairs={{0,4},{1,5},{2,6},{3,7},{4,0},{5,1},{6,2},{7,3},{8,12},{9,13},{10,... | collective-permute-start | bytes 258056 | tf_op jit(solution)/shard_map/cond/branch_0_fun/ppermute | solution.py:371
  84.0 7.7 %collective-permute-start.5 = (bf16[4,56,768]{2,1,0:T(8,128)(2,1)S(1)}, bf16[4,56,768]{2,1,0:T(8,128)(2,1)S(1)}, u32[]{:S(2)}, u32[]{:S(2)}) collective-permute-start(bf16[4,56,768]{2,1,0:T(8,128)(2,1)S(1)} %get-tuple-element.89), channel_id=1, source_target_pairs={{0,1},{1,0},{2,3},{3,2},{4,5},{5,4},{6,7},{7,6},{8,9},{9,8},{10,11... | collective-permute-start | bytes 1032200 | tf_op jit(solution)/shard_map/cond/branch_0_fun/ppermute | solution.py:371
  85.4 7.5 %collective-permute-start.13 = (bf16[2,56,768]{2,1,0:T(8,128)(2,1)S(1)}, bf16[2,56,768]{2,1,0:T(8,128)(2,1)S(1)}, u32[]{:S(2)}, u32[]{:S(2)}) collective-permute-start(bf16[2,56,768]{2,1,0:T(8,128)(2,1)S(1)} %get-tuple-element.342), channel_id=1, source_target_pairs={{0,2},{1,3},{2,0},{3,1},{4,6},{5,7},{6,4},{7,5},{8,10},{9,11},{10,... | collective-permute-start | bytes 516104 | tf_op jit(solution)/shard_map/cond/branch_0_fun/ppermute | solution.py:371
  86.2 7.9 %collective-permute-start.12 = (bf16[1,56,768]{2,1,0:T(8,128)(2,1)S(1)}, bf16[1,56,768]{2,1,0:T(8,128)(2,1)S(1)}, u32[]{:S(2)}, u32[]{:S(2)}) collective-permute-start(bf16[1,56,768]{2,1,0:T(8,128)(2,1)S(1)} %get-tuple-element.354), channel_id=1, source_target_pairs={{0,4},{1,5},{2,6},{3,7},{4,0},{5,1},{6,2},{7,3},{8,12},{9,13},{10,... | collective-permute-start | bytes 258056 | tf_op jit(solution)/shard_map/cond/branch_0_fun/ppermute | solution.py:371
  87.8 7.9 %collective-permute-start.11 = (bf16[1,56,384]{2,1,0:T(8,128)(2,1)S(1)}, bf16[1,56,384]{2,1,0:T(8,128)(2,1)S(1)}, u32[]{:S(2)}, u32[]{:S(2)}) collective-permute-start(bf16[1,56,384]{2,1,0:T(8,128)(2,1)S(1)} %fusion.8), channel_id=1, source_target_pairs={{0,4},{1,5},{2,6},{3,7},{4,0},{5,1},{6,2},{7,3},{8,12},{9,13},{10,... | collective-permute-start | bytes 129032 | tf_op jit(solution)/shard_map/cond/branch_0_fun/ppermute | solution.py:371
  91.8 7.5 %collective-permute-start.10 = (bf16[2,56,768]{2,1,0:T(8,128)(2,1)S(1)}, bf16[2,56,768]{2,1,0:T(8,128)(2,1)S(1)}, u32[]{:S(2)}, u32[]{:S(2)}) collective-permute-start(bf16[2,56,768]{2,1,0:T(8,128)(2,1)S(1)} %get-tuple-element.343), channel_id=1, source_target_pairs={{0,2},{1,3},{2,0},{3,1},{4,6},{5,7},{6,4},{7,5},{8,10},{9,11},{10,... | collective-permute-start | bytes 516104 | tf_op jit(solution)/shard_map/cond/branch_0_fun/ppermute | solution.py:371
  92.9 6.7 %collective-permute-start.17 = (bf16[1,56,768]{2,1,0:T(8,128)(2,1)S(1)}, bf16[1,56,768]{2,1,0:T(8,128)(2,1)S(1)}, u32[]{:S(2)}, u32[]{:S(2)}) collective-permute-start(bf16[1,56,768]{2,1,0:T(8,128)(2,1)S(1)} %get-tuple-element.350), channel_id=1, source_target_pairs={{0,4},{1,5},{2,6},{3,7},{4,0},{5,1},{6,2},{7,3},{8,12},{9,13},{10,... | collective-permute-start | bytes 258056 | tf_op jit(solution)/shard_map/cond/branch_0_fun/ppermute | solution.py:371
  94.3 8.2 %collective-permute-start.16 = (bf16[1,56,384]{2,1,0:T(8,128)(2,1)S(1)}, bf16[1,56,384]{2,1,0:T(8,128)(2,1)S(1)}, u32[]{:S(2)}, u32[]{:S(2)}) collective-permute-start(bf16[1,56,384]{2,1,0:T(8,128)(2,1)S(1)} %fusion.9), channel_id=1, source_target_pairs={{0,1},{1,0},{2,3},{3,2},{4,5},{5,4},{6,7},{7,6},{8,9},{9,8},{10,11... | collective-permute-start | bytes 129032 | tf_op jit(solution)/shard_map/cond/branch_0_fun/ppermute | solution.py:371
  95.7 7.1 %collective-permute-start.15 = (bf16[2,56,384]{2,1,0:T(8,128)(2,1)S(1)}, bf16[2,56,384]{2,1,0:T(8,128)(2,1)S(1)}, u32[]{:S(2)}, u32[]{:S(2)}) collective-permute-start(bf16[2,56,384]{2,1,0:T(8,128)(2,1)S(1)} %constant_dynamic-update-slice_fusion), channel_id=1, source_target_pairs={{0,2},{1,3},{2,0},{3,1},{4,6},{5,7},{6,4},{7,5},{8,10},{9,11},{10,... | collective-permute-start | bytes 258056 | tf_op jit(solution)/shard_map/cond/branch_0_fun/ppermute | solution.py:371
  99.3 6.9 %collective-permute-start.14 = (bf16[1,56,768]{2,1,0:T(8,128)(2,1)S(1)}, bf16[1,56,768]{2,1,0:T(8,128)(2,1)S(1)}, u32[]{:S(2)}, u32[]{:S(2)}) collective-permute-start(bf16[1,56,768]{2,1,0:T(8,128)(2,1)S(1)} %get-tuple-element.351), channel_id=1, source_target_pairs={{0,4},{1,5},{2,6},{3,7},{4,0},{5,1},{6,2},{7,3},{8,12},{9,13},{10,... | collective-permute-start | bytes 258056 | tf_op jit(solution)/shard_map/cond/branch_0_fun/ppermute | solution.py:371
  99.7 8.0 %collective-permute-start.20 = (bf16[1,56,384]{2,1,0:T(8,128)(2,1)S(1)}, bf16[1,56,384]{2,1,0:T(8,128)(2,1)S(1)}, u32[]{:S(2)}, u32[]{:S(2)}) collective-permute-start(bf16[1,56,384]{2,1,0:T(8,128)(2,1)S(1)} %fusion.10), channel_id=1, source_target_pairs={{0,4},{1,5},{2,6},{3,7},{4,0},{5,1},{6,2},{7,3},{8,12},{9,13},{10,... | collective-permute-start | bytes 129032 | tf_op jit(solution)/shard_map/cond/branch_0_fun/ppermute | solution.py:371
  102.8 14.3 %collective-permute-start.24 = (bf16[4,56,384]{2,1,0:T(8,128)(2,1)S(1)}, bf16[4,56,384]{2,1,0:T(8,128)(2,1)S(1)}, u32[]{:S(2)}, u32[]{:S(2)}) collective-permute-start(bf16[4,56,384]{2,1,0:T(8,128)(2,1)S(1)} %constant_dynamic-update-slice_fusion.4.refs_0_), channel_id=1, source_target_pairs={{0,1},{1,0},{2,3},{3,2},{4,5},{5,4},{6,7},{7,6},{8,9},{9,8},{10,11... | collective-permute-start | bytes 516104 | tf_op jit(solution)/shard_map/cond/branch_0_fun/ppermute | solution.py:371
  108.7 8.4 %collective-permute-start.25 = (bf16[4,56,384]{2,1,0:T(8,128)(2,1)S(1)}, bf16[4,56,384]{2,1,0:T(8,128)(2,1)S(1)}, u32[]{:S(2)}, u32[]{:S(2)}) collective-permute-start(bf16[4,56,384]{2,1,0:T(8,128)(2,1)S(1)} %constant_dynamic-update-slice_fusion.8.refs_2_), channel_id=1, source_target_pairs={{0,2},{1,3},{2,0},{3,1},{4,6},{5,7},{6,4},{7,5},{8,10},{9,11},{10,... | collective-permute-start | bytes 516104 | tf_op jit(solution)/shard_map/cond/branch_0_fun/ppermute | solution.py:371
  (24 other events, 462.0 us)
